TPU v7x, 128 devices: a whole 4x4x4 slice. The times are simulated.
128 devices in a mesh: dom: 64 (over x, z, y), batch: 2 (over core).
Axes of the slice: x: 4, y: 4, z: 4, core: 2. Of those that a mesh axis runs over, the one named last changes fastest.
Arguments:
- features: bfloat16 [4, 65536, 512], P('batch', 'dom'), may hold values from -6 to 6
- tile_vals: bfloat16 [2048, 128, 128], P('dom'), may hold values from -0.25 to 0.25
- tile_row: int32 [2048], P('dom'), may hold values from 0 to 7
- tile_col: int32 [2048], P('dom'), may hold values from 0 to 11
- send_next: int32 [128], P('dom'), may hold values from 0 to 7
- send_prev: int32 [128], P('dom'), may hold values from 0 to 7
- cluster: int32 [65536], P('dom'), may hold values from 0 to 1023, as said below
- cotangent: bfloat16 [4, 65536, 512], P('batch', 'dom'), may hold values from -6 to 6
- self_weight: bfloat16 [512, 512], replicated, may hold values from -0.25 to 0.25
- neighbour_weight: bfloat16 [512, 512], replicated, may hold values from -0.25 to 0.25
- w_coarse: bfloat16 [512, 512], replicated, may hold values from -0.25 to 0.25
Outputs:
- output: bfloat16 [4, 65536, 512], P('batch', 'dom')
- self_weight_gradient: float32 [512, 512], replicated
- neighbour_weight_gradient: float32 [512, 512], replicated
- grad_coarse: float32 [512, 512], replicated
Inputs may be any that keep to these rules, and one draw needn't show every extreme that they name: Within each pair of partitions 2m, 2m + 1, every cluster number names exactly two of the pair's 2 * 1024 nodes.
All inputs are finite; a program needn't handle non-finite values.
Results may differ from a plain program's by a relative error of at most 0.012.
Values may be sent and summed in bfloat16 or wider, within the bound.
A program may use at most 128 MiB of HBM per device.

v0:
```python
import math

import jax
import jax.numpy as jnp
from jax import lax
from jax.sharding import PartitionSpec as P


def shifted(x, axis, by):
    length = lax.axis_size(axis)
    pairs = [(i, i + by) for i in range(length) if 0 <= i + by < length]
    return lax.ppermute(x, axis, pairs)


def partner(value, axis, distance):
    mask = 2**distance
    pairs = [(source, source ^ mask) for source in range(lax.axis_size(axis))]
    return lax.ppermute(value, axis, pairs)


def dsilu(value):
    sig = jax.nn.sigmoid(value)
    return sig * (1.0 + value * (1.0 - sig))


def member_table(labels, count):
    return (labels[None, :] == jnp.arange(count, dtype=jnp.int32)[:, None]).astype(jnp.bfloat16)


def pooling(rows, table):
    return jnp.einsum("cn,snd->scd", table, rows, preferred_element_type=jnp.float32)


def lookup(coarse_rows, table):
    return jnp.einsum("cn,scd->snd", table, coarse_rows, preferred_element_type=jnp.float32)


def pick_blocks(labels, count, tiled):
    table = (labels[:, None] == jnp.arange(count, dtype=jnp.int32)[None, :]).astype(jnp.bfloat16)
    return jnp.einsum("tb,sbjd->stjd", table, tiled, preferred_element_type=jnp.float32).astype(
        jnp.bfloat16
    )


def local(
    features,
    tile_vals,
    tile_row,
    tile_col,
    send_next,
    send_prev,
    cluster,
    cotangent,
    self_weight,
    neighbour_weight,
    w_coarse,
):
    scen, nodes, width = features.shape
    side = tile_vals.shape[1]
    blocks = nodes // side
    tiled = features.reshape(scen, blocks, side, width)
    to_next = pick_blocks(send_next, blocks, tiled)
    to_prev = pick_blocks(send_prev, blocks, tiled)
    got_prev = shifted(to_next, "dom", 1)
    got_next = shifted(to_prev, "dom", -1)
    extended = jnp.concatenate([tiled, got_prev, got_next], axis=1)
    picked = pick_blocks(tile_col, extended.shape[1], extended)
    terms = jnp.einsum("tij,stjd->stid", tile_vals, picked, preferred_element_type=jnp.float32)
    rowhot = (tile_row[None, :] == jnp.arange(blocks, dtype=jnp.int32)[:, None]).astype(jnp.float32)
    summed = jnp.einsum("rt,stid->srid", rowhot, terms, precision=lax.Precision.HIGHEST)
    neighbour_total = summed.reshape(scen, nodes, width).astype(jnp.bfloat16)
    preactivation = jnp.einsum(
        "jkb,bt->jkt", features, self_weight, preferred_element_type=jnp.float32
    )
    preactivation = preactivation + jnp.einsum(
        "jkb,bt->jkt", neighbour_total, neighbour_weight, preferred_element_type=jnp.float32
    )
    hidden = jax.nn.silu(preactivation).astype(jnp.bfloat16)
    table = member_table(cluster, nodes)
    parity = lax.axis_index("dom") % 2
    half = nodes // 2
    own_start = parity * half

    def owned(array):
        return lax.dynamic_slice_in_dim(array, own_start, half, 1)

    partial_value = pooling(hidden, table)
    grad_partial = pooling(cotangent, table)
    partner_sums = partner(partial_value.astype(jnp.bfloat16), "dom", 0).astype(partial_value.dtype)
    coarse = (0.5 * (partial_value + partner_sums)).astype(jnp.bfloat16)
    act = jnp.einsum("skd,de->ske", coarse, w_coarse, preferred_element_type=jnp.float32)
    lifted = jax.nn.silu(act).astype(jnp.bfloat16)
    grad_lift = grad_partial + partner(grad_partial.astype(jnp.bfloat16), "dom", 0).astype(
        grad_partial.dtype
    )
    grad_act = (grad_lift * dsilu(act)).astype(jnp.bfloat16)
    term_coarse = jnp.einsum(
        "skd,ske->de", owned(coarse), owned(grad_act), preferred_element_type=jnp.float32
    )
    grad_down = jnp.einsum(
        "ske,de->skd", grad_act, w_coarse, preferred_element_type=jnp.float32
    ).astype(jnp.bfloat16)
    spread = lookup(lifted, table)
    output = (hidden.astype(jnp.float32) + spread).astype(jnp.bfloat16)
    back = lookup(grad_down, table)
    grad_hidden = cotangent.astype(jnp.float32) + 0.5 * back
    preactivation_gradient = (grad_hidden * dsilu(preactivation)).astype(jnp.bfloat16)
    self_contribution = jnp.einsum(
        "btv,btq->vq", features, preactivation_gradient, preferred_element_type=jnp.float32
    )
    neighbour_contribution = jnp.einsum(
        "btv,btq->vq", neighbour_total, preactivation_gradient, preferred_element_type=jnp.float32
    )
    totals = lax.psum((self_contribution, neighbour_contribution, term_coarse), ("dom", "batch"))
    gradient_scale = 1.0 / math.sqrt(scen * lax.axis_size("batch") * nodes * lax.axis_size("dom"))
    return (
        output,
        totals[0] * gradient_scale,
        totals[1] * gradient_scale,
        totals[2] * gradient_scale,
    )


def solution(mesh):
    in_specs = (
        P("batch", "dom", None),
        P("dom", None, None),
        P("dom"),
        P("dom"),
        P("dom"),
        P("dom"),
        P("dom"),
        P("batch", "dom", None),
        P(),
        P(),
        P(),
    )
    out_specs = (P("batch", "dom", None), P(), P(), P())
    return jax.shard_map(local, mesh=mesh, in_specs=in_specs, out_specs=out_specs, check_vma=False)
```

profile of v0, /device:TPU:1, one launch (start us, length us, event | category | flops | bytes accessed | tf_op | source)
XLA Modules:
  0.0 384.2 jit_solution(13734323582045857980)
XLA Ops:
  7.2 0.0 copy-start
  7.2 0.0 copy-start.2
  7.2 0.0 all-reduce.3.cloned.1.call-start
  7.2 0.0 copy-start.9
  7.2 3.2 fusion.35
  10.5 4.1 %collective-permute-start = (bf16[2,2,128,512]{3,1,2,0:T(2,128)(2,1)S(1)}, bf16[2,2,128,512]{3,1,2,0:T(2,128)(2,1)S(1)}, u32[]{:S(2)}, u32[]{:S(2)}) collective-permute-start(bf16[2,2,128,512]{3,1,2,0:T(2,128)(2,1)S(1)} %fusion.35), channel_id=1, source_target_pairs={{0,2},{2,4},{4,6},{6,8},{8,10},{10,12},{12,14},{14,16},{16,18},{18... | collective-permute-start | bytes 1572872 | tf_op jit(solution)/shard_map/ppermute | solution.py:12
  14.5 3.1 fusion.36
  17.6 1.3 collective-permute-start.1
  18.9 0.0 copy-done.2
  18.9 1.2 copy.58
  20.1 0.0 copy-done.9
  20.1 0.0 copy-start.15
  20.1 3.3 fusion.45
  23.4 1.7 collective-permute-done
  25.1 6.9 %collective-permute-done.1 = bf16[2,2,128,512]{3,1,2,0:T(2,128)(2,1)S(1)} collective-permute-done((bf16[2,2,128,512]{3,1,2,0:T(2,128)(2,1)S(1)}, bf16[2,2,128,512]{3,1,2,0:T(2,128)(2,1)S(1)}, u32[]{:S(2)}, u32[]{:S(2)}) %collective-permute-start.1) | collective-permute-done | bytes 524320 | tf_op jit(solution)/shard_map/ppermute | solution.py:12
  32.0 0.0 copy-done.15
  32.0 5.0 %convert_bitcast_fusion = bf16[2,32,128,512]{3,1,2,0:T(8,128)(2,1)} fusion(bf16[2,2,128,512]{3,1,2,0:T(2,128)(2,1)S(1)} %collective-permute-done.1, bf16[2,2,128,512]{3,1,2,0:T(2,128)(2,1)S(1)} %collective-permute-done, bf16[2,8,128,512]{3,1,2,0:T(8,128)(2,1)S(1)} %copy.58, s32[32]{0:T(128)S(1)} %copy-done.15), kind=kOutput, calls=%fused_computation.2 | convolution fusion | flops 114295168 | bytes 11534464 | tf_op jit(solution)/shard_map/tb,sbjd->stjd/dot_general | solution.py:40
  37.0 0.0 copy-done
  37.0 18.5 %convolution_bitcast_fusion = f32[2,32,128,512]{2,3,0,1:T(8,128)} fusion(bf16[2,32,128,512]{3,1,2,0:T(8,128)(2,1)} %convert_bitcast_fusion, bf16[32,128,128]{2,1,0:T(8,128)(2,1)S(1)} %copy-done), kind=kOutput, calls=%fused_computation | convolution fusion | flops 1073741824 | bytes 26214400 | tf_op jit(solution)/shard_map/tij,stjd->stid/dot_general | solution.py:68
  55.5 0.0 copy-start.11
  55.5 20.1 %copy.60 = f32[2,32,128,512]{3,1,2,0:T(8,128)} copy(f32[2,32,128,512]{2,3,0,1:T(8,128)} %convolution_bitcast_fusion) | data formatting | bytes 33554432 | tf_op jit(solution)/shard_map/tij,stjd->stid/transpose | solution.py:68
  75.6 0.0 copy-done.11
  75.6 9.3 %convert_bitcast_fusion.1 = bf16[2,8,128,512]{3,1,2,0:T(8,128)(2,1)S(1)} fusion(f32[2,32,128,512]{3,1,2,0:T(8,128)} %copy.60, s32[32]{0:T(128)S(1)} %copy-done.11), kind=kOutput, calls=%fused_computation.37 | convolution fusion | flops 403702016 | bytes 18874496 | tf_op jit(solution)/shard_map/rt,stid->srid/dot_general | solution.py:70
  84.8 0.0 copy-start.3
  84.8 0.7 copy.61
  85.5 0.0 copy-start.4
  85.5 1.3 copy-done.4
  86.8 0.0 copy-done.10
  86.8 0.9 copy-done.3
  87.8 1.2 convolution_add_fusion
  89.0 0.0 copy-done.14
  89.0 0.0 copy-start.5
  89.0 0.0 copy-start.12
  89.1 5.5 %bitcast_convert_fusion.1 = (bf16[2,1024,512]{1,2,0:T(8,128)(2,1)}, f32[2,512,1024]{2,1,0:T(8,128)}) fusion(s32[1024]{0:T(1024)S(1)} %copy-done.14, f32[2,1024,512]{2,1,0:T(8,128)S(1)} %convolution_add_fusion), kind=kOutput, calls=%fused_computation.18 | convolution fusion | flops 2154823680 | bytes 10489856 | tf_op jit(solution)/shard_map/cn,snd->scd/dot_general | solution.py:31
  94.5 0.0 copy-done.5
  94.5 1.3 collective-permute-start.2
  95.8 0.0 copy-done.12
  95.8 5.0 %bitcast_convert_fusion = (bf16[2,1024,512]{2,1,0:T(8,128)(2,1)}, f32[1024,2,512]{2,0,1:T(8,128)}) fusion(bf16[2,1024,512]{2,1,0:T(8,128)(2,1)S(1)} %copy-done.12, s32[1024]{0:T(1024)S(1)} %copy-done.14), kind=kOutput, calls=%fused_computation.12 | convolution fusion | flops 2149580800 | bytes 8392704 | tf_op jit(solution)/shard_map/cn,snd->scd/dot_general | solution.py:31
  100.8 0.4 collective-permute-start.3
  101.3 38.8 %collective-permute-done.2 = bf16[2,1024,512]{1,2,0:T(8,128)(2,1)} collective-permute-done((bf16[2,1024,512]{1,2,0:T(8,128)(2,1)}, bf16[2,1024,512]{1,2,0:T(8,128)(2,1)}, u32[]{:S(2)}, u32[]{:S(2)}) %collective-permute-start.2) | collective-permute-done | bytes 2097184 | tf_op jit(solution)/shard_map/ppermute | solution.py:18
  140.1 3.8 fusion.12
  143.9 0.0 copy-start.7
  143.9 41.1 %collective-permute-done.3 = bf16[2,1024,512]{2,1,0:T(8,128)(2,1)} collective-permute-done((bf16[2,1024,512]{2,1,0:T(8,128)(2,1)}, bf16[2,1024,512]{2,1,0:T(8,128)(2,1)}, u32[]{:S(2)}, u32[]{:S(2)}) %collective-permute-start.3) | collective-permute-done | bytes 2097184 | tf_op jit(solution)/shard_map/ppermute | solution.py:18
  185.0 0.0 copy-done.13
  185.0 0.0 copy-done.17
  185.0 6.8 %fusion.9 = (bf16[2,1024,512]{2,1,0:T(8,128)(2,1)}, f32[2,1024,512]{2,1,0:T(8,128)}) fusion(f32[1024,2,512]{2,0,1:T(8,128)S(1)} %copy-done.17, bf16[2,1024,512]{2,1,0:T(8,128)(2,1)} %collective-permute-done.3, bf16[2,1024,512]{1,2,0:T(8,128)(2,1)S(1)} %fusion.12, bf16[512,512]{1,0:T(8,128)(2,1)S(1)} %copy-done.13), kind=kOutput, calls=%fused_computation.14 | convolution fusion | flops 1085276160 | bytes 15204352 | tf_op jit(solution)/shard_map/skd,de->ske/dot_general | solution.py:91
  191.8 0.0 copy-done.7
  191.8 8.1 %fusion.7 = bf16[2,1024,512]{2,1,0:T(8,128)(2,1)} fusion(f32[2,1024,512]{2,1,0:T(8,128)} %copy-done.5, bf16[2,1024,512]{2,1,0:T(8,128)(2,1)} %param.18, s32[1024]{0:T(1024)S(1)} %copy-done.14, bf16[2,1024,512]{2,1,0:T(8,128)(2,1)} %get-tuple-element.27, bf16[512,512]{1,0:T(8,128)(2,1)S(1)} %copy-done.13), kind=kOutput, calls=%fused_computation.10 | convolution fusion | flops 3235905536 | bytes 11014144 | tf_op jit(solution)/shard_map/cn,scd->snd/dot_general | solution.py:35
  199.9 4.6 %convolution_bitcast_fusion.2 = f32[512,512]{0,1:T(8,128)} fusion(bf16[2,1024,512]{2,1,0:T(8,128)(2,1)} %bitcast.111, bf16[2,1024,512]{2,1,0:T(8,128)(2,1)} %fusion.7), kind=kOutput, calls=%fused_computation.40 | convolution fusion | flops 1073741824 | bytes 5242880 | tf_op jit(solution)/shard_map/btv,btq->vq/dot_general | solution.py:111
  204.5 0.0 copy-done.6
  204.5 2.2 convolution_bitcast_fusion.3
  206.8 0.0 copy-done.8
  206.8 0.0 copy-done.16
  206.8 1.7 convolution_bitcast_fusion.1
  208.5 0.0 all-reduce.3.cloned.1.call-update
  208.5 8.0 %fusion.10 = bf16[2,1024,512]{2,1,0:T(8,128)(2,1)} fusion(s32[1024]{0:T(1024)S(1)} %copy-done.14, f32[2,1024,512]{2,1,0:T(8,128)} %get-tuple-element.28, f32[2,1024,512]{2,1,0:T(8,128)} %copy-done.5), kind=kOutput, calls=%fused_computation.16 | convolution fusion | flops 2162163712 | bytes 10489856 | tf_op jit(solution)/shard_map/cn,scd->snd/dot_general | solution.py:35
  216.5 153.4 %all-reduce.3.cloned.1.call-done = (f32[512,512]{0,1:T(8,128)}, f32[512,512]{0,1:T(8,128)}, f32[512,512]{0,1:T(8,128)}) async-done(((f32[512,512]{0,1:T(8,128)}, f32[512,512]{0,1:T(8,128)}, f32[512,512]{0,1:T(8,128)}), (f32[512,512]{0,1:T(8,128)}, f32[512,512]{0,1:T(8,128)}, f32[512,512]{0,1:T(8,128)})) %all-reduce.3.cloned.1.call-update) | async-done | bytes 3145744 | tf_op jit(solution)/shard_map/psum | solution.py:114
  369.9 1.8 broadcast_multiply_fusion
  371.7 0.0 copy-start.1
  371.7 1.3 copy.73
  373.0 1.3 copy.74
  374.3 1.3 broadcast_multiply_fusion.2
  375.6 1.3 copy.72
  376.9 0.0 copy-done.1
  (7 shorter events, 0.0 us)
Async XLA Ops:
  7.2 29.8 %copy-start = (bf16[32,128,128]{2,1,0:T(8,128)(2,1)S(1)}, bf16[32,128,128]{2,1,0:T(8,128)(2,1)}, u32[]{:S(2)}) copy-start(bf16[32,128,128]{2,1,0:T(8,128)(2,1)} %param.12) | copy-start | bytes 3145732
  7.2 11.7 %copy-start.2 = (bf16[2,1024,512]{2,1,0:T(8,128)(2,1)S(1)}, bf16[2,1024,512]{2,1,0:T(8,128)(2,1)}, u32[]{:S(2)}) copy-start(bf16[2,1024,512]{2,1,0:T(8,128)(2,1)} %param.11) | copy-start | bytes 6291460
  7.2 362.7 %all-reduce.3.cloned.1.call-start = ((), (), s32[]{:S(2)}) async-start(), calls=%async_computation | async-start | bytes 6291456 | tf_op jit(solution)/shard_map/psum | solution.py:114
  7.2 12.8 %copy-start.9 = (bf16[512,512]{1,0:T(8,128)(2,1)S(1)}, bf16[512,512]{1,0:T(8,128)(2,1)}, u32[]{:S(2)}) copy-start(bf16[512,512]{1,0:T(8,128)(2,1)} %param.19) | copy-start | bytes 1572868
  10.5 14.6 %collective-permute-start = (bf16[2,2,128,512]{3,1,2,0:T(2,128)(2,1)S(1)}, bf16[2,2,128,512]{3,1,2,0:T(2,128)(2,1)S(1)}, u32[]{:S(2)}, u32[]{:S(2)}) collective-permute-start(bf16[2,2,128,512]{3,1,2,0:T(2,128)(2,1)S(1)} %fusion.35), channel_id=1, source_target_pairs={{0,2},{2,4},{4,6},{6,8},{8,10},{10,12},{12,14},{14,16},{16,18},{18... | collective-permute-start | bytes 1572872 | tf_op jit(solution)/shard_map/ppermute | solution.py:12
  17.6 14.4 %collective-permute-start.1 = (bf16[2,2,128,512]{3,1,2,0:T(2,128)(2,1)S(1)}, bf16[2,2,128,512]{3,1,2,0:T(2,128)(2,1)S(1)}, u32[]{:S(2)}, u32[]{:S(2)}) collective-permute-start(bf16[2,2,128,512]{3,1,2,0:T(2,128)(2,1)S(1)} %fusion.36), channel_id=1, source_target_pairs={{2,0},{4,2},{6,4},{8,6},{10,8},{12,10},{14,12},{16,14},{18,16},{20... | collective-permute-start | bytes 1572872 | tf_op jit(solution)/shard_map/ppermute | solution.py:12
  20.1 11.9 %copy-start.15 = (s32[32]{0:T(128)S(1)}, s32[32]{0:T(128)}, u32[]{:S(2)}) copy-start(s32[32]{0:T(128)} %param.14) | copy-start | bytes 388
  55.5 20.1 %copy-start.11 = (s32[32]{0:T(128)S(1)}, s32[32]{0:T(128)}, u32[]{:S(2)}) copy-start(s32[32]{0:T(128)} %param.13) | copy-start | bytes 388
  75.6 11.3 %copy-start.10 = (bf16[512,512]{1,0:T(8,128)(2,1)S(1)}, bf16[512,512]{1,0:T(8,128)(2,1)}, u32[]{:S(2)}) copy-start(bf16[512,512]{1,0:T(8,128)(2,1)} %param.20) | copy-start | bytes 1572868
  84.8 2.9 copy-start.3
  85.5 1.3 copy-start.4
  87.8 1.3 copy-start.14
  89.0 5.5 %copy-start.5 = (f32[2,1024,512]{2,1,0:T(8,128)}, f32[2,1024,512]{2,1,0:T(8,128)S(1)}, u32[]{:S(2)}) copy-start(f32[2,1024,512]{2,1,0:T(8,128)S(1)} %convolution_add_fusion) | copy-start | bytes 12582916
  89.0 6.8 %copy-start.12 = (bf16[2,1024,512]{2,1,0:T(8,128)(2,1)S(1)}, bf16[2,1024,512]{2,1,0:T(8,128)(2,1)}, u32[]{:S(2)}) copy-start(bf16[2,1024,512]{2,1,0:T(8,128)(2,1)} %param.18) | copy-start | bytes 6291460
  94.5 45.6 %collective-permute-start.2 = (bf16[2,1024,512]{1,2,0:T(8,128)(2,1)}, bf16[2,1024,512]{1,2,0:T(8,128)(2,1)}, u32[]{:S(2)}, u32[]{:S(2)}) collective-permute-start(bf16[2,1024,512]{1,2,0:T(8,128)(2,1)} %get-tuple-element.23), channel_id=1, source_target_pairs={{0,2},{2,0},{4,6},{6,4},{8,10},{10,8},{12,14},{14,12},{16,18},{18,... | collective-permute-start | bytes 6291464 | tf_op jit(solution)/shard_map/ppermute | solution.py:18
  100.8 84.2 %collective-permute-start.3 = (bf16[2,1024,512]{2,1,0:T(8,128)(2,1)}, bf16[2,1024,512]{2,1,0:T(8,128)(2,1)}, u32[]{:S(2)}, u32[]{:S(2)}) collective-permute-start(bf16[2,1024,512]{2,1,0:T(8,128)(2,1)} %get-tuple-element.25), channel_id=1, source_target_pairs={{0,2},{2,0},{4,6},{6,4},{8,10},{10,8},{12,14},{14,12},{16,18},{18,... | collective-permute-start | bytes 6291464 | tf_op jit(solution)/shard_map/ppermute | solution.py:18
  140.1 44.9 %copy-start.13 = (bf16[512,512]{1,0:T(8,128)(2,1)S(1)}, bf16[512,512]{1,0:T(8,128)(2,1)}, u32[]{:S(2)}) copy-start(bf16[512,512]{1,0:T(8,128)(2,1)} %param.21) | copy-start | bytes 1572868
  140.1 44.9 %copy-start.17 = (f32[1024,2,512]{2,0,1:T(8,128)S(1)}, f32[1024,2,512]{2,0,1:T(8,128)}, u32[]{:S(2)}) copy-start(f32[1024,2,512]{2,0,1:T(8,128)} %get-tuple-element.26) | copy-start | bytes 12582916
  143.9 47.9 %copy-start.7 = (bf16[2,1024,512]{1,2,0:T(8,128)(2,1)}, bf16[2,1024,512]{1,2,0:T(8,128)(2,1)S(1)}, u32[]{:S(2)}) copy-start(bf16[2,1024,512]{1,2,0:T(8,128)(2,1)S(1)} %fusion.12) | copy-start | bytes 6291460
  199.9 4.6 %copy-start.6 = (bf16[2,1024,512]{2,1,0:T(8,128)(2,1)S(1)}, bf16[2,1024,512]{2,1,0:T(8,128)(2,1)}, u32[]{:S(2)}) copy-start(bf16[2,1024,512]{2,1,0:T(8,128)(2,1)} %fusion.7) | copy-start | bytes 6291460
  204.5 2.2 copy-start.8
  204.5 2.2 copy-start.16
  371.7 5.3 %copy-start.1 = (bf16[32,128,128]{2,1,0:T(8,128)(2,1)S(1)}, bf16[32,128,128]{2,1,0:T(8,128)(2,1)}, u32[]{:S(2)}) copy-start(bf16[32,128,128]{2,1,0:T(8,128)(2,1)} %param.12) | copy-start | bytes 3145732
Sparse Core Ops, SparseCore 0:
  208.6 161.1 all-reduce.2
where the time goes:
time: 389 us; the launch traced here: 384 us
  waiting for transfers between devices  242 us (62%)
  matrix products  85.5 us (22%)
  local copies, waits for them, and re-layouts  28.1 us (7%)
  between operations  14.7 us (4%)
  starting transfers between devices  7.09 us (2%)
  other arithmetic  6.86 us (2%)
    psum x1, waiting for transfers between devices, local(): lax.psum((self_contribution, neighbour_contribution, term_coarse), ('dom'...  153 us
    ppermute x2, waiting for transfers between devices, partner(): return lax.ppermute(value, axis, pairs)  80 us
    transpose x1, local copies, waits for them, and re-layouts, local(): jnp.einsum('tij,stjd->stid', tile_vals, picked, preferred_element_type=jn...  20.1 us
    dot_general x1, matrix products, local(): jnp.einsum('tij,stjd->stid', tile_vals, picked, preferred_element_type=jn...  18.5 us
    dot_general x2, matrix products, lookup(): jnp.einsum('cn,scd->snd', table, coarse_rows, preferred_element_type=jnp....  16.1 us
    dot_general x3, matrix products, pick_blocks(): jnp.einsum('tb,sbjd->stjd', table, tiled, preferred_element_type=jnp.floa...  11.3 us
    dot_general x2, matrix products, pooling(): jnp.einsum('cn,snd->scd', table, rows, preferred_element_type=jnp.float32)  10.5 us
    dot_general x1, matrix products, local(): jnp.einsum('rt,stid->srid', rowhot, terms, precision=lax.Precision.HIGHEST)  9.26 us
  transfers between devices with their start and end apart: 5, of which 5 were waited for; matrix products, arithmetic and copies ran while one was open for 6% of the time, Pallas kernels for 0%

commit v1 on v0

--- a/solution.py
+++ b/solution.py
@@ -3,6 +3,8 @@
 import jax
 import jax.numpy as jnp
 from jax import lax
+from jax.experimental import pallas as pl
+from jax.experimental.pallas import tpu as pltpu
 from jax.sharding import PartitionSpec as P
 
 
@@ -40,6 +42,171 @@
     return jnp.einsum("tb,sbjd->stjd", table, tiled, preferred_element_type=jnp.float32).astype(
         jnp.bfloat16
     )
+
+
+MESH = pl.DeviceIdType.MESH
+ORDERS = ((0, 1, 2), (1, 2, 0), (2, 0, 1))
+
+
+def reduce_kernel(
+    g0, g1, g2, out, send0, recv0, acc, buf1, recv1, sum2, buf2, recv2, sum3, buf3, recv3,
+    send_sem, recv_sem, side_send, side_recv,
+):
+    gs = (g0, g1, g2)
+    core = lax.axis_index("batch")
+    dom = lax.axis_index("dom")
+    where = (dom // 16, (dom // 4) % 4, dom % 4)
+    weight = (16, 4, 1)
+
+    def peer(axis, k):
+        place = (where[axis] + k) % 4
+        return (dom + (place - where[axis]) * weight[axis], core), place
+
+    other = (dom, 1 - core)
+    barrier = pltpu.get_barrier_semaphore()
+    pl.semaphore_signal(barrier, inc=1, device_id=other, device_id_type=MESH)
+    for axis in range(3):
+        for k in (1, 2, 3):
+            pl.semaphore_signal(barrier, inc=1, device_id=peer(axis, k)[0], device_id_type=MESH)
+    for p in range(3):
+        send0[p] = gs[p][1 - core].astype(jnp.bfloat16)
+    pl.semaphore_wait(barrier, 10)
+
+    first = []
+    for p in range(3):
+        copy = pltpu.make_async_remote_copy(
+            src_ref=send0.at[p], dst_ref=recv0.at[p], send_sem=side_send.at[0, p],
+            recv_sem=side_recv.at[0, p], device_id=other, device_id_type=MESH)
+        copy.start()
+        first.append(copy)
+
+    def scatter(p, phase, pick, landing):
+        copies = []
+        for k in (1, 2, 3):
+            device, place = peer(ORDERS[p][phase], k)
+            copy = pltpu.make_async_remote_copy(
+                src_ref=pick(place), dst_ref=landing.at[p, k - 1],
+                send_sem=send_sem.at[phase, p, k - 1], recv_sem=recv_sem.at[phase, p, k - 1],
+                device_id=device, device_id_type=MESH)
+            copy.start()
+            copies.append(copy)
+        return copies
+
+    def gather(p, phase, part):
+        copies = []
+        for k in (1, 2, 3):
+            device, _ = peer(ORDERS[p][phase], k)
+            copy = pltpu.make_async_remote_copy(
+                src_ref=part, dst_ref=part,
+                send_sem=send_sem.at[5 - phase, p, k - 1], recv_sem=recv_sem.at[5 - phase, p, k - 1],
+                device_id=device, device_id_type=MESH)
+            copy.start()
+            copies.append(copy)
+        return copies
+
+    def mine(p, phase):
+        return where[ORDERS[p][phase]]
+
+    def cols(place):
+        return pl.ds(pl.multiple_of(place * 128, 128), 128)
+
+    pending = list(first)
+    stage1 = []
+    for p in range(3):
+        first[p].wait_recv()
+        total = gs[p][core] + recv0[p].astype(jnp.float32)
+        acc[p] = total
+        buf1[p] = total.astype(jnp.bfloat16)
+        stage1.append(scatter(p, 0, lambda place: buf1.at[p, place], recv1))
+    stage2 = []
+    for p in range(3):
+        for copy in stage1[p]:
+            copy.wait_recv()
+        total = acc[p, mine(p, 0)]
+        for k in range(3):
+            total = total + recv1[p, k].astype(jnp.float32)
+        sum2[p] = total
+        buf2[p] = total.astype(jnp.bfloat16)
+        stage2.append(scatter(p, 1, lambda place: buf2.at[p, place], recv2))
+    stage3 = []
+    for p in range(3):
+        for copy in stage2[p]:
+            copy.wait_recv()
+        total = sum2[p, mine(p, 1)]
+        for k in range(3):
+            total = total + recv2[p, k].astype(jnp.float32)
+        sum3[p] = total
+        buf3[p] = total.astype(jnp.bfloat16)
+        stage3.append(scatter(p, 2, lambda place: buf3.at[p, :, cols(place)], recv3))
+    stage4 = []
+    for p in range(3):
+        for copy in stage3[p]:
+            copy.wait_recv()
+        total = sum3[p, :, cols(mine(p, 2))]
+        for k in range(3):
+            total = total + recv3[p, k].astype(jnp.float32)
+        part = out.at[p, core, mine(p, 0), mine(p, 1), :, cols(mine(p, 2))]
+        part[...] = total.astype(jnp.bfloat16)
+        stage4.append(gather(p, 2, part))
+    stage5 = []
+    for p in range(3):
+        for copy in stage4[p]:
+            copy.wait_recv()
+        stage5.append(gather(p, 1, out.at[p, core, mine(p, 0), mine(p, 1)]))
+    stage6 = []
+    for p in range(3):
+        for copy in stage5[p]:
+            copy.wait_recv()
+        stage6.append(gather(p, 0, out.at[p, core, mine(p, 0)]))
+    last = []
+    for p in range(3):
+        for copy in stage6[p]:
+            copy.wait_recv()
+        copy = pltpu.make_async_remote_copy(
+            src_ref=out.at[p, core], dst_ref=out.at[p, core], send_sem=side_send.at[1, p],
+            recv_sem=side_recv.at[1, p], device_id=other, device_id_type=MESH)
+        copy.start()
+        last.append(copy)
+    for copy in last:
+        copy.wait_recv()
+    for group in stage1 + stage2 + stage3 + stage4 + stage5 + stage6:
+        for copy in group:
+            copy.wait_send()
+    for copy in first + last:
+        copy.wait_send()
+
+
+def reduce_all(parts):
+    whole = pl.BlockSpec(memory_space=pltpu.VMEM)
+    shaped = [part.reshape(2, 4, 4, 16, 512) for part in parts]
+    half = (3, 4, 4, 16, 512)
+    out = pl.pallas_call(
+        reduce_kernel,
+        out_shape=jax.ShapeDtypeStruct((3, 2, 4, 4, 16, 512), jnp.bfloat16),
+        in_specs=[whole] * 3,
+        out_specs=whole,
+        scratch_shapes=[
+            pltpu.VMEM(half, jnp.bfloat16),
+            pltpu.VMEM(half, jnp.bfloat16),
+            pltpu.VMEM(half, jnp.float32),
+            pltpu.VMEM(half, jnp.bfloat16),
+            pltpu.VMEM((3, 3, 4, 16, 512), jnp.bfloat16),
+            pltpu.VMEM((3, 4, 16, 512), jnp.float32),
+            pltpu.VMEM((3, 4, 16, 512), jnp.bfloat16),
+            pltpu.VMEM((3, 3, 16, 512), jnp.bfloat16),
+            pltpu.VMEM((3, 16, 512), jnp.float32),
+            pltpu.VMEM((3, 16, 512), jnp.bfloat16),
+            pltpu.VMEM((3, 3, 16, 128), jnp.bfloat16),
+            pltpu.SemaphoreType.DMA((6, 3, 3)),
+            pltpu.SemaphoreType.DMA((6, 3, 3)),
+            pltpu.SemaphoreType.DMA((2, 3)),
+            pltpu.SemaphoreType.DMA((2, 3)),
+        ],
+        compiler_params=pltpu.CompilerParams(
+            collective_id=0, has_side_effects=True, vmem_limit_bytes=32 * 2**20
+        ),
+    )(*shaped)
+    return out.reshape(3, 512, 512)
 
 
 def local(
@@ -111,7 +278,8 @@
     neighbour_contribution = jnp.einsum(
         "btv,btq->vq", neighbour_total, preactivation_gradient, preferred_element_type=jnp.float32
     )
-    totals = lax.psum((self_contribution, neighbour_contribution, term_coarse), ("dom", "batch"))
+    totals = reduce_all((self_contribution, neighbour_contribution, term_coarse))
+    totals = totals.astype(jnp.float32)
     gradient_scale = 1.0 / math.sqrt(scen * lax.axis_size("batch") * nodes * lax.axis_size("dom"))
     return (
         output,

time: 389 us -> 253 us (0.65)
  waiting for transfers between devices: 242 us -> 84.6 us
  Pallas kernels: 0 us -> 40 us
  between operations: 14.7 us -> 1.1 us
  matrix products: 85.5 us -> 78.3 us
    psum x1 -> x0, waiting for transfers between devices: 153 us -> none  [local(): lax.psum((self_contribution, neighbour_contribution, term_coarse), ('dom'...]
    pallas_call x0 -> x1, Pallas kernels: none -> 40 us  [reduce_all(): pl.pallas_call(reduce_kernel, out_shape=jax.ShapeDtypeStruct((3, 2, 4, 4,...]
    dot_general x0 -> x2, local copies, waits for them, and re-layouts: none -> 4.25 us  [local(): jnp.einsum('btv,btq->vq', neighbour_total, preactivation_gradient, prefer...]
    ppermute x2, waiting for transfers between devices: 80 us -> 76.1 us  [partner(): return lax.ppermute(value, axis, pairs)]
  transfers between devices with their start and end apart: 5 -> 4, of which waited for: 5 -> 4; matrix products, arithmetic and copies ran while one was open for 6% -> 8% of each run, Pallas kernels for 0% -> 0%
where the time goes in v1:
time: 253 us; the launch traced here: 248 us
  waiting for transfers between devices  84.6 us (33%)
  matrix products  78.3 us (31%)
  Pallas kernels  40 us (16%)
  local copies, waits for them, and re-layouts  31.1 us (12%)
  starting transfers between devices  6.82 us (3%)
  other arithmetic  6.06 us (2%)
    ppermute x2, waiting for transfers between devices, partner(): return lax.ppermute(value, axis, pairs)  76.1 us
    pallas_call x1, Pallas kernels, reduce_all(): pl.pallas_call(reduce_kernel, out_shape=jax.ShapeDtypeStruct((3, 2, 4, 4,...  40 us
    transpose x1, local copies, waits for them, and re-layouts, local(): jnp.einsum('tij,stjd->stid', tile_vals, picked, preferred_element_type=jn...  20 us
    dot_general x1, matrix products, local(): jnp.einsum('tij,stjd->stid', tile_vals, picked, preferred_element_type=jn...  18.5 us
    dot_general x2, matrix products, lookup(): jnp.einsum('cn,scd->snd', table, coarse_rows, preferred_element_type=jnp....  12.3 us
    dot_general x3, matrix products, pick_blocks(): jnp.einsum('tb,sbjd->stjd', table, tiled, preferred_element_type=jnp.floa...  11.6 us
    dot_general x2, matrix products, pooling(): jnp.einsum('cn,snd->scd', table, rows, preferred_element_type=jnp.float32)  10.4 us
    dot_general x1, matrix products, local(): jnp.einsum('rt,stid->srid', rowhot, terms, precision=lax.Precision.HIGHEST)  9.25 us
  transfers between devices with their start and end apart: 4, of which 4 were waited for; matrix products, arithmetic and copies ran while one was open for 8% of the time, Pallas kernels for 0%

profile of v1, /device:TPU:1, one launch (start us, length us, event | category | flops | bytes accessed | tf_op | source)
XLA Modules:
  0.0 248.0 jit_solution(18043114428963388546)
XLA Ops:
  0.6 0.0 copy-start
  0.6 0.0 copy-start.2
  0.7 0.0 copy-start.9
  0.7 3.2 %fusion.43 = bf16[2,2,128,512]{3,1,2,0:T(2,128)(2,1)S(1)} fusion(s32[2]{0:T(128)} %param.15, bf16[2,8,128,512]{3,2,1,0:T(8,128)(2,1)} %bitcast.122), kind=kOutput, calls=%fused_computation.45 | convolution fusion | flops 4456464 | bytes 2621448 | tf_op jit(solution)/shard_map/tb,sbjd->stjd/dot_general | solution.py:42
  3.9 4.1 %collective-permute-start = (bf16[2,2,128,512]{3,1,2,0:T(2,128)(2,1)S(1)}, bf16[2,2,128,512]{3,1,2,0:T(2,128)(2,1)S(1)}, u32[]{:S(2)}, u32[]{:S(2)}) collective-permute-start(bf16[2,2,128,512]{3,1,2,0:T(2,128)(2,1)S(1)} %fusion.43), channel_id=1, source_target_pairs={{0,2},{2,4},{4,6},{6,8},{8,10},{10,12},{12,14},{14,16},{16,18},{18... | collective-permute-start | bytes 1572872 | tf_op jit(solution)/shard_map/ppermute | solution.py:14
  8.0 3.1 %fusion.44 = bf16[2,2,128,512]{3,1,2,0:T(2,128)(2,1)S(1)} fusion(s32[2]{0:T(128)} %param.16, bf16[2,8,128,512]{3,2,1,0:T(8,128)(2,1)} %bitcast.123), kind=kOutput, calls=%fused_computation.46 | convolution fusion | flops 4456464 | bytes 2621448 | tf_op jit(solution)/shard_map/tb,sbjd->stjd/dot_general | solution.py:42
  11.0 1.3 collective-permute-start.1
  12.3 0.0 copy-done.2
  12.3 1.2 copy.45
  13.5 0.0 copy-done.9
  13.5 0.0 copy-start.15
  13.5 3.3 %fusion.54 = f32[2,1024,512]{2,1,0:T(8,128)} fusion(bf16[2,1024,512]{2,1,0:T(8,128)(2,1)S(1)} %copy-done.2, bf16[512,512]{1,0:T(8,128)(2,1)S(1)} %copy-done.9), kind=kOutput, calls=%fused_computation.58 | convolution fusion | flops 1073741824 | bytes 6815744 | tf_op jit(solution)/shard_map/jkb,bt->jkt/dot_general | solution.py:239
  16.8 1.6 collective-permute-done
  18.5 6.9 %collective-permute-done.1 = bf16[2,2,128,512]{3,1,2,0:T(2,128)(2,1)S(1)} collective-permute-done((bf16[2,2,128,512]{3,1,2,0:T(2,128)(2,1)S(1)}, bf16[2,2,128,512]{3,1,2,0:T(2,128)(2,1)S(1)}, u32[]{:S(2)}, u32[]{:S(2)}) %collective-permute-start.1) | collective-permute-done | bytes 524320 | tf_op jit(solution)/shard_map/ppermute | solution.py:14
  25.4 0.0 copy-done.15
  25.4 5.3 %convert_bitcast_fusion = bf16[2,32,128,512]{3,1,2,0:T(8,128)(2,1)} fusion(bf16[2,2,128,512]{3,1,2,0:T(2,128)(2,1)S(1)} %collective-permute-done.1, bf16[2,2,128,512]{3,1,2,0:T(2,128)(2,1)S(1)} %collective-permute-done, bf16[2,8,128,512]{3,1,2,0:T(8,128)(2,1)S(1)} %copy.45, s32[32]{0:T(128)S(1)} %copy-done.15), kind=kOutput, calls=%fused_computation.2 | convolution fusion | flops 114295168 | bytes 11534464 | tf_op jit(solution)/shard_map/tb,sbjd->stjd/dot_general | solution.py:42
  30.7 0.0 copy-done
  30.7 18.5 %convolution_bitcast_fusion = f32[2,32,128,512]{2,3,0,1:T(8,128)} fusion(bf16[2,32,128,512]{3,1,2,0:T(8,128)(2,1)} %convert_bitcast_fusion, bf16[32,128,128]{2,1,0:T(8,128)(2,1)S(1)} %copy-done), kind=kOutput, calls=%fused_computation | convolution fusion | flops 1073741824 | bytes 26214400 | tf_op jit(solution)/shard_map/tij,stjd->stid/dot_general | solution.py:235
  49.2 0.0 copy-start.11
  49.2 20.0 %copy.47 = f32[2,32,128,512]{3,1,2,0:T(8,128)} copy(f32[2,32,128,512]{2,3,0,1:T(8,128)} %convolution_bitcast_fusion) | data formatting | bytes 33554432 | tf_op jit(solution)/shard_map/tij,stjd->stid/transpose | solution.py:235
  69.2 0.0 copy-done.11
  69.2 9.2 %convert_bitcast_fusion.1 = bf16[2,8,128,512]{3,1,2,0:T(8,128)(2,1)S(1)} fusion(f32[2,32,128,512]{3,1,2,0:T(8,128)} %copy.47, s32[32]{0:T(128)S(1)} %copy-done.11), kind=kOutput, calls=%fused_computation.40 | convolution fusion | flops 403702016 | bytes 18874496 | tf_op jit(solution)/shard_map/rt,stid->srid/dot_general | solution.py:237
  78.5 0.0 copy-start.4
  78.5 0.7 copy.48
  79.2 0.0 copy-start.3
  79.2 1.3 copy-done.3
  80.5 0.0 copy-done.10
  80.5 0.9 copy-done.4
  81.4 1.2 convolution_add_fusion
  82.7 0.0 copy-done.14
  82.7 0.0 copy-start.5
  82.7 0.0 copy-start.12
  82.7 5.4 %bitcast_convert_fusion.1 = (bf16[2,1024,512]{1,2,0:T(8,128)(2,1)}, f32[2,512,1024]{2,1,0:T(8,128)}) fusion(s32[1024]{0:T(1024)S(1)} %copy-done.14, f32[2,1024,512]{2,1,0:T(8,128)S(1)} %convolution_add_fusion), kind=kOutput, calls=%fused_computation.18 | convolution fusion | flops 2154823680 | bytes 10489856 | tf_op jit(solution)/shard_map/cn,snd->scd/dot_general | solution.py:33
  88.1 0.0 copy-done.5
  88.1 1.3 collective-permute-start.2
  89.3 0.0 copy-done.12
  89.3 5.0 %bitcast_convert_fusion = (bf16[2,1024,512]{2,1,0:T(8,128)(2,1)}, f32[1024,2,512]{2,0,1:T(8,128)}) fusion(bf16[2,1024,512]{2,1,0:T(8,128)(2,1)S(1)} %copy-done.12, s32[1024]{0:T(1024)S(1)} %copy-done.14), kind=kOutput, calls=%fused_computation.12 | convolution fusion | flops 2149580800 | bytes 8392704 | tf_op jit(solution)/shard_map/cn,snd->scd/dot_general | solution.py:33
  94.4 0.2 collective-permute-start.3
  94.6 4.1 %copy.56 = bf16[512,2,1024]{2,0,1:T(8,128)(2,1)} copy(bf16[512,2,1024]{0,2,1:T(8,128)(2,1)} %bitcast.126) | data formatting | bytes 4194304 | tf_op jit(solution)/shard_map/btv,btq->vq/dot_general | solution.py:278
  98.7 34.9 %collective-permute-done.2 = bf16[2,1024,512]{1,2,0:T(8,128)(2,1)} collective-permute-done((bf16[2,1024,512]{1,2,0:T(8,128)(2,1)}, bf16[2,1024,512]{1,2,0:T(8,128)(2,1)}, u32[]{:S(2)}, u32[]{:S(2)}) %collective-permute-start.2) | collective-permute-done | bytes 2097184 | tf_op jit(solution)/shard_map/ppermute | solution.py:20
  133.6 3.8 %fusion.12 = bf16[2,1024,512]{1,2,0:T(8,128)(2,1)S(1)} fusion(f32[2,512,1024]{2,1,0:T(8,128)} %get-tuple-element.8, bf16[2,1024,512]{1,2,0:T(8,128)(2,1)} %collective-permute-done.2), kind=kLoop, calls=%fused_computation.20 | loop fusion | flops 4194304 | bytes 8388608 | tf_op jit(solution)/shard_map/convert_element_type | solution.py:257
  137.4 0.0 copy-start.8
  137.4 41.1 %collective-permute-done.3 = bf16[2,1024,512]{2,1,0:T(8,128)(2,1)} collective-permute-done((bf16[2,1024,512]{2,1,0:T(8,128)(2,1)}, bf16[2,1024,512]{2,1,0:T(8,128)(2,1)}, u32[]{:S(2)}, u32[]{:S(2)}) %collective-permute-start.3) | collective-permute-done | bytes 2097184 | tf_op jit(solution)/shard_map/ppermute | solution.py:20
  178.6 0.0 copy-done.13
  178.6 0.0 copy-done.17
  178.6 6.8 %fusion.9 = (bf16[2,1024,512]{2,1,0:T(8,128)(2,1)}, f32[2,1024,512]{2,1,0:T(8,128)}) fusion(f32[1024,2,512]{2,0,1:T(8,128)S(1)} %copy-done.17, bf16[2,1024,512]{2,1,0:T(8,128)(2,1)} %collective-permute-done.3, bf16[2,1024,512]{1,2,0:T(8,128)(2,1)S(1)} %fusion.12, bf16[512,512]{1,0:T(8,128)(2,1)S(1)} %copy-done.13), kind=kOutput, calls=%fused_computation.14 | convolution fusion | flops 1085276160 | bytes 15204352 | tf_op jit(solution)/shard_map/skd,de->ske/dot_general | solution.py:258
  185.3 0.0 copy-done.8
  185.3 8.1 %fusion.7 = bf16[2,1024,512]{2,1,0:T(8,128)(2,1)} fusion(f32[2,1024,512]{2,1,0:T(8,128)} %copy-done.5, bf16[2,1024,512]{2,1,0:T(8,128)(2,1)} %param.18, s32[1024]{0:T(1024)S(1)} %copy-done.14, bf16[2,1024,512]{2,1,0:T(8,128)(2,1)} %get-tuple-element.11, bf16[512,512]{1,0:T(8,128)(2,1)S(1)} %copy-done.13), kind=kOutput, calls=%fused_computation.10 | convolution fusion | flops 3235905536 | bytes 11014144 | tf_op jit(solution)/shard_map/cn,scd->snd/dot_general | solution.py:37
  193.4 2.4 fusion.46
  195.8 0.0 copy-done.16
  195.8 0.0 copy-start.7
  195.8 1.3 fusion.75
  197.1 0.3 copy-done.7
  197.4 1.2 fusion.38
  198.6 0.1 copy.58.g1
  198.8 40.0 %shard_map.138 = bf16[3,2,4,4,16,512]{5,4,3,2,1,0:T(8,128)(2,1)S(1)} custom-call(f32[2,4,4,16,512]{4,3,2,1,0:T(8,128)S(1)} %bitcast.121, f32[2,4,4,16,512]{4,3,2,1,0:T(8,128)S(1)} %copy.58.g1, f32[2,4,4,16,512]{4,3,2,1,0:T(8,128)S(1)} %bitcast.120), custom_call_target="tpu_custom_call" | custom-call | tf_op jit(solution)/shard_map/pallas_call | solution.py:183
  238.8 0.0 copy-start.18
  238.8 0.4 convert_element_type.97
  239.2 0.0 copy-start.6
  239.2 1.8 slice_multiply_fusion
  241.1 1.0 copy-done.18
  242.1 1.4 copy-done.6
  243.5 4.3 %fusion.10 = bf16[2,1024,512]{2,1,0:T(8,128)(2,1)} fusion(s32[1024]{0:T(1024)S(1)} %copy-done.14, f32[2,1024,512]{2,1,0:T(8,128)S(1)} %copy-done.18, f32[2,1024,512]{2,1,0:T(8,128)S(1)} %copy-done.6), kind=kOutput, calls=%fused_computation.16 | convolution fusion | flops 2162163712 | bytes 10489856 | tf_op jit(solution)/shard_map/cn,scd->snd/dot_general | solution.py:37
  247.8 0.0 copy-done.1
  (6 shorter events, 0.0 us)
Async XLA Ops:
  0.6 30.1 %copy-start = (bf16[32,128,128]{2,1,0:T(8,128)(2,1)S(1)}, bf16[32,128,128]{2,1,0:T(8,128)(2,1)}, u32[]{:S(2)}) copy-start(bf16[32,128,128]{2,1,0:T(8,128)(2,1)} %param.12) | copy-start | bytes 3145732
  0.6 11.7 %copy-start.2 = (bf16[2,1024,512]{2,1,0:T(8,128)(2,1)S(1)}, bf16[2,1024,512]{2,1,0:T(8,128)(2,1)}, u32[]{:S(2)}) copy-start(bf16[2,1024,512]{2,1,0:T(8,128)(2,1)} %param.11) | copy-start | bytes 6291460
  0.7 12.8 %copy-start.9 = (bf16[512,512]{1,0:T(8,128)(2,1)S(1)}, bf16[512,512]{1,0:T(8,128)(2,1)}, u32[]{:S(2)}) copy-start(bf16[512,512]{1,0:T(8,128)(2,1)} %param.19) | copy-start | bytes 1572868
  3.9 14.6 %collective-permute-start = (bf16[2,2,128,512]{3,1,2,0:T(2,128)(2,1)S(1)}, bf16[2,2,128,512]{3,1,2,0:T(2,128)(2,1)S(1)}, u32[]{:S(2)}, u32[]{:S(2)}) collective-permute-start(bf16[2,2,128,512]{3,1,2,0:T(2,128)(2,1)S(1)} %fusion.43), channel_id=1, source_target_pairs={{0,2},{2,4},{4,6},{6,8},{8,10},{10,12},{12,14},{14,16},{16,18},{18... | collective-permute-start | bytes 1572872 | tf_op jit(solution)/shard_map/ppermute | solution.py:14
  11.0 14.4 %collective-permute-start.1 = (bf16[2,2,128,512]{3,1,2,0:T(2,128)(2,1)S(1)}, bf16[2,2,128,512]{3,1,2,0:T(2,128)(2,1)S(1)}, u32[]{:S(2)}, u32[]{:S(2)}) collective-permute-start(bf16[2,2,128,512]{3,1,2,0:T(2,128)(2,1)S(1)} %fusion.44), channel_id=1, source_target_pairs={{2,0},{4,2},{6,4},{8,6},{10,8},{12,10},{14,12},{16,14},{18,16},{20... | collective-permute-start | bytes 1572872 | tf_op jit(solution)/shard_map/ppermute | solution.py:14
  13.5 11.9 %copy-start.15 = (s32[32]{0:T(128)S(1)}, s32[32]{0:T(128)}, u32[]{:S(2)}) copy-start(s32[32]{0:T(128)} %param.14) | copy-start | bytes 388
  49.2 20.0 %copy-start.11 = (s32[32]{0:T(128)S(1)}, s32[32]{0:T(128)}, u32[]{:S(2)}) copy-start(s32[32]{0:T(128)} %param.13) | copy-start | bytes 388
  69.2 11.3 %copy-start.10 = (bf16[512,512]{1,0:T(8,128)(2,1)S(1)}, bf16[512,512]{1,0:T(8,128)(2,1)}, u32[]{:S(2)}) copy-start(bf16[512,512]{1,0:T(8,128)(2,1)} %param.20) | copy-start | bytes 1572868
  78.5 2.9 %copy-start.4 = (f32[2,1024,512]{2,1,0:T(8,128)S(1)}, f32[2,1024,512]{2,1,0:T(8,128)}, u32[]{:S(2)}) copy-start(f32[2,1024,512]{2,1,0:T(8,128)} %fusion.54) | copy-start | bytes 12582916
  79.2 1.3 copy-start.3
  81.4 1.3 copy-start.14
  82.7 5.4 %copy-start.5 = (f32[2,1024,512]{2,1,0:T(8,128)}, f32[2,1024,512]{2,1,0:T(8,128)S(1)}, u32[]{:S(2)}) copy-start(f32[2,1024,512]{2,1,0:T(8,128)S(1)} %convolution_add_fusion) | copy-start | bytes 12582916
  82.7 6.6 %copy-start.12 = (bf16[2,1024,512]{2,1,0:T(8,128)(2,1)S(1)}, bf16[2,1024,512]{2,1,0:T(8,128)(2,1)}, u32[]{:S(2)}) copy-start(bf16[2,1024,512]{2,1,0:T(8,128)(2,1)} %param.18) | copy-start | bytes 6291460
  88.1 45.6 %collective-permute-start.2 = (bf16[2,1024,512]{1,2,0:T(8,128)(2,1)}, bf16[2,1024,512]{1,2,0:T(8,128)(2,1)}, u32[]{:S(2)}, u32[]{:S(2)}) collective-permute-start(bf16[2,1024,512]{1,2,0:T(8,128)(2,1)} %get-tuple-element.7), channel_id=1, source_target_pairs={{0,2},{2,0},{4,6},{6,4},{8,10},{10,8},{12,14},{14,12},{16,18},{18,... | collective-permute-start | bytes 6291464 | tf_op jit(solution)/shard_map/ppermute | solution.py:20
  94.4 84.2 %collective-permute-start.3 = (bf16[2,1024,512]{2,1,0:T(8,128)(2,1)}, bf16[2,1024,512]{2,1,0:T(8,128)(2,1)}, u32[]{:S(2)}, u32[]{:S(2)}) collective-permute-start(bf16[2,1024,512]{2,1,0:T(8,128)(2,1)} %get-tuple-element.9), channel_id=1, source_target_pairs={{0,2},{2,0},{4,6},{6,4},{8,10},{10,8},{12,14},{14,12},{16,18},{18,... | collective-permute-start | bytes 6291464 | tf_op jit(solution)/shard_map/ppermute | solution.py:20
  133.6 44.9 %copy-start.13 = (bf16[512,512]{1,0:T(8,128)(2,1)S(1)}, bf16[512,512]{1,0:T(8,128)(2,1)}, u32[]{:S(2)}) copy-start(bf16[512,512]{1,0:T(8,128)(2,1)} %param.21) | copy-start | bytes 1572868
  133.6 44.9 %copy-start.17 = (f32[1024,2,512]{2,0,1:T(8,128)S(1)}, f32[1024,2,512]{2,0,1:T(8,128)}, u32[]{:S(2)}) copy-start(f32[1024,2,512]{2,0,1:T(8,128)} %get-tuple-element.10) | copy-start | bytes 12582916
  137.4 47.9 %copy-start.8 = (bf16[2,1024,512]{1,2,0:T(8,128)(2,1)}, bf16[2,1024,512]{1,2,0:T(8,128)(2,1)S(1)}, u32[]{:S(2)}) copy-start(bf16[2,1024,512]{1,2,0:T(8,128)(2,1)S(1)} %fusion.12) | copy-start | bytes 6291460
  193.4 2.4 copy-start.16
  195.8 1.6 copy-start.7
  238.8 3.3 %copy-start.18 = (f32[2,1024,512]{2,1,0:T(8,128)S(1)}, f32[2,1024,512]{2,1,0:T(8,128)}, u32[]{:S(2)}) copy-start(f32[2,1024,512]{2,1,0:T(8,128)} %get-tuple-element.12) | copy-start | bytes 12582916
  239.2 4.3 %copy-start.6 = (f32[2,1024,512]{2,1,0:T(8,128)S(1)}, f32[2,1024,512]{2,1,0:T(8,128)}, u32[]{:S(2)}) copy-start(f32[2,1024,512]{2,1,0:T(8,128)} %copy-done.5) | copy-start | bytes 12582916
  243.5 4.3 %copy-start.1 = (bf16[32,128,128]{2,1,0:T(8,128)(2,1)S(1)}, bf16[32,128,128]{2,1,0:T(8,128)(2,1)}, u32[]{:S(2)}) copy-start(bf16[32,128,128]{2,1,0:T(8,128)(2,1)} %param.12) | copy-start | bytes 3145732

commit v2 on v1

--- a/solution.py
+++ b/solution.py
@@ -1,3 +1,4 @@
+import functools
 import math
 
 import jax
@@ -7,6 +8,17 @@
 from jax.experimental.pallas import tpu as pltpu
 from jax.sharding import PartitionSpec as P
 
+N = 1024
+D = 512
+BLK = 128
+NB = 8
+SIDE = 2
+LOW = 576
+F32 = jnp.float32
+BF16 = jnp.bfloat16
+VM = pl.BlockSpec(memory_space=pltpu.VMEM)
+SM = pl.BlockSpec(memory_space=pltpu.SMEM)
+
 
 def shifted(x, axis, by):
     length = lax.axis_size(axis)
@@ -14,34 +26,244 @@
     return lax.ppermute(x, axis, pairs)
 
 
-def partner(value, axis, distance):
-    mask = 2**distance
-    pairs = [(source, source ^ mask) for source in range(lax.axis_size(axis))]
-    return lax.ppermute(value, axis, pairs)
-
-
-def dsilu(value):
+def partner(value):
+    pairs = [(source, source ^ 1) for source in range(lax.axis_size("dom"))]
+    return lax.ppermute(value, "dom", pairs)
+
+
+def silu_pair(value):
     sig = jax.nn.sigmoid(value)
-    return sig * (1.0 + value * (1.0 - sig))
-
-
-def member_table(labels, count):
-    return (labels[None, :] == jnp.arange(count, dtype=jnp.int32)[:, None]).astype(jnp.bfloat16)
-
-
-def pooling(rows, table):
-    return jnp.einsum("cn,snd->scd", table, rows, preferred_element_type=jnp.float32)
-
-
-def lookup(coarse_rows, table):
-    return jnp.einsum("cn,scd->snd", table, coarse_rows, preferred_element_type=jnp.float32)
-
-
-def pick_blocks(labels, count, tiled):
-    table = (labels[:, None] == jnp.arange(count, dtype=jnp.int32)[None, :]).astype(jnp.bfloat16)
-    return jnp.einsum("tb,sbjd->stjd", table, tiled, preferred_element_type=jnp.float32).astype(
-        jnp.bfloat16
-    )
+    return value * sig, sig * (1.0 + value * (1.0 - sig))
+
+
+def dot(left, right):
+    return jnp.dot(left, right, preferred_element_type=F32)
+
+
+def dot_tn(left, right):
+    return lax.dot_general(left, right, (((0,), (0,)), ((), ())), preferred_element_type=F32)
+
+
+def dot_nt(left, right):
+    return lax.dot_general(left, right, (((1,), (1,)), ((), ())), preferred_element_type=F32)
+
+
+def shape(*dims, dtype=BF16):
+    return jax.ShapeDtypeStruct(dims, dtype)
+
+
+def cost(flops, size):
+    return pl.CostEstimate(flops=flops, bytes_accessed=size, transcendentals=0)
+
+
+def pick_kernel(nexts, prevs, a_ref, b_ref, a_out, b_out):
+    a_out[...] = a_ref[...]
+    b_out[...] = b_ref[...]
+
+
+def pick(nexts, prevs, tiled):
+    block = (1, 1, BLK, D)
+    return pl.pallas_call(
+        pick_kernel,
+        out_shape=(shape(SIDE, 2, BLK, D), shape(SIDE, 2, BLK, D)),
+        grid_spec=pltpu.PrefetchScalarGridSpec(
+            num_scalar_prefetch=2,
+            grid=(SIDE, 2),
+            in_specs=[
+                pl.BlockSpec(block, lambda s, j, n, p: (s, n[j], 0, 0)),
+                pl.BlockSpec(block, lambda s, j, n, p: (s, p[j], 0, 0)),
+            ],
+            out_specs=[pl.BlockSpec(block, lambda s, j, n, p: (s, j, 0, 0))] * 2,
+        ),
+        cost_estimate=cost(0, 2**21),
+    )(nexts, prevs, tiled, tiled)
+
+
+def store_split(value, low, high):
+    low[...] = value[:LOW].astype(BF16)
+    high[...] = value[LOW:].astype(BF16)
+
+
+def label_kernel(row_ref, col_ref, ct_ref, lab_row, lab_col, count, low0, low1, high, table, flip):
+    row, col = row_ref[...], col_ref[...]
+    step = 256
+
+    def tables(i, carry):
+        at = pl.ds(pl.multiple_of(i * step, step), step)
+        down = lax.broadcasted_iota(jnp.int32, (step, N), 0) + i * step
+        across = lax.broadcasted_iota(jnp.int32, (step, N), 1)
+        table[at, :] = (row == down).astype(F32).astype(BF16)
+        flip[at, :] = (col_ref[at, :] == across).astype(F32).astype(BF16)
+        return carry
+
+    lax.fori_loop(0, N // step, tables, 0)
+    held_row = dot(jnp.ones((16, N), BF16), flip[...])
+    held_col = dot(table[...], jnp.ones((N, 128), BF16))
+
+    def ones_of(held, value):
+        return (held == value).astype(F32)
+
+    total = jnp.sum(ones_of(held_row[:1], 1.0), axis=1, keepdims=True)
+    row_in = jnp.concatenate([ones_of(held_row, 1.0), ones_of(held_row, 2.0)], axis=0).astype(BF16)
+    col_in = jnp.concatenate([ones_of(held_col, 1.0), ones_of(held_col, 2.0)], axis=1).astype(BF16)
+
+    def before(i, carry):
+        at = pl.ds(pl.multiple_of(i * step, step), step)
+        down = lax.broadcasted_iota(jnp.int32, (step, N), 0) + i * step
+        across = lax.broadcasted_iota(jnp.int32, (step, N), 1)
+        table[at, :] = (across < down).astype(F32).astype(BF16)
+        flip[at, :] = (down < across).astype(F32).astype(BF16)
+        return carry
+
+    lax.fori_loop(0, N // step, before, 0)
+    row_rank = dot(row_in, flip[...])
+    col_rank = dot(table[...], col_in)
+    new_row = jnp.where(held_row[:1] == 1.0, row_rank[:1], total + row_rank[16:17])
+    new_col = jnp.where(held_col[:, :1] == 1.0, col_rank[:, :1], total + col_rank[:, 128:129])
+    across = lax.broadcasted_iota(jnp.int32, (N, N), 1)
+    down = lax.broadcasted_iota(jnp.int32, (N, N), 0)
+    col_lab = jnp.sum(jnp.where(col == across, new_row, 0.0), axis=1, keepdims=True)
+    row_lab = jnp.sum(jnp.where(row == down, new_col, 0.0), axis=0, keepdims=True)
+    lab_col[...] = col_lab.astype(jnp.int32)
+    lab_row[...] = row_lab.astype(jnp.int32)
+    count[...] = jnp.broadcast_to(total, (8, 128)).astype(jnp.int32)
+    table[...] = (row_lab.astype(jnp.int32) == down).astype(F32).astype(BF16)
+    for s, low in ((0, low0), (1, low1)):
+        store_split(dot(table[...], ct_ref[s]), low, high.at[s])
+
+
+def label(cluster, cotangent):
+    return pl.pallas_call(
+        label_kernel,
+        out_shape=(
+            shape(1, N, dtype=jnp.int32),
+            shape(N, 1, dtype=jnp.int32),
+            shape(8, 128, dtype=jnp.int32),
+            shape(LOW, D),
+            shape(LOW, D),
+            shape(SIDE, N - LOW, D),
+        ),
+        in_specs=[VM] * 3,
+        out_specs=(VM,) * 6,
+        scratch_shapes=[pltpu.VMEM((N, N), BF16), pltpu.VMEM((N, N), BF16)],
+        compiler_params=pltpu.CompilerParams(vmem_limit_bytes=32 * 2**20),
+        cost_estimate=cost(4 * 2**30, 2**22),
+    )(cluster.reshape(1, N), cluster.reshape(N, 1), cotangent)
+
+
+def node_kernel(
+    rows, cols, lab_row, x_ref, prev_ref, next_ref, tiles, w_self, w_neigh,
+    agg, hidden, slope, low0, low1, high, ext, acc, table,
+):
+    for s in range(SIDE):
+        span = slice(s * D, (s + 1) * D)
+        ext[0:NB, :, span] = x_ref[s].reshape(NB, BLK, D)
+        ext[NB : NB + 2, :, span] = prev_ref[s]
+        ext[NB + 2 : NB + 4, :, span] = next_ref[s]
+    acc[...] = jnp.zeros_like(acc)
+
+    def tile(t, carry):
+        r = rows[t]
+        acc[r] = acc[r] + dot(tiles[t], ext[cols[t]])
+        return carry
+
+    lax.fori_loop(0, tiles.shape[0], tile, 0)
+    step = 256
+
+    def block(i, carry):
+        at = pl.ds(pl.multiple_of(i * step, step), step)
+        down = lax.broadcasted_iota(jnp.int32, (step, N), 0) + i * step
+        table[at, :] = (lab_row[...] == down).astype(F32).astype(BF16)
+        for s in range(SIDE):
+            span = slice(s * D, (s + 1) * D)
+            got = acc[pl.ds(i * 2, 2), :, span].reshape(step, D).astype(BF16)
+            agg[s, at, :] = got
+            pre = dot(x_ref[s, at, :], w_self[...]) + dot(got, w_neigh[...])
+            value, grad = silu_pair(pre)
+            hidden[s, at, :] = value.astype(BF16)
+            slope[s, at, :] = grad.astype(BF16)
+        return carry
+
+    lax.fori_loop(0, N // step, block, 0)
+    for s, low in ((0, low0), (1, low1)):
+        store_split(dot(table[...], hidden[s]), low, high.at[s])
+
+
+def node_step(tile_row, tile_col, lab_row, features, got_prev, got_next, tiles, w_self, w_neigh):
+    full = shape(SIDE, N, D)
+    return pl.pallas_call(
+        node_kernel,
+        out_shape=(full, full, full, shape(LOW, D), shape(LOW, D), shape(SIDE, N - LOW, D)),
+        in_specs=[SM, SM] + [VM] * 7,
+        out_specs=(VM,) * 6,
+        scratch_shapes=[
+            pltpu.VMEM((NB + 4, BLK, SIDE * D), BF16),
+            pltpu.VMEM((NB, BLK, SIDE * D), F32),
+            pltpu.VMEM((N, N), BF16),
+        ],
+        compiler_params=pltpu.CompilerParams(vmem_limit_bytes=32 * 2**20),
+        cost_estimate=cost(10 * 2**30, 2**23),
+    )(tile_row, tile_col, lab_row, features, got_prev, got_next, tiles, w_self, w_neigh)
+
+
+def tail_kernel(
+    s, more, count, lab_col, rec_h, rec_c, far_h, far_c, low_h, high_h, low_c, high_c,
+    hidden, slope, agg, x_ref, ct_ref, w_coarse, *rest,
+):
+    if more:
+        old0, old1, old2, _, g0, g1, g2, out, flip, both = rest
+    else:
+        g0, g1, g2, out, flip, both = rest
+    shared = lax.broadcasted_iota(jnp.int32, (N, 1), 0) < count[0:1, 0:1]
+
+    def joined(low, high, rec, far):
+        own = jnp.concatenate([low[...], high[s]], axis=0).astype(F32)
+        got = jnp.concatenate([rec[...], far[s]], axis=0).astype(F32)
+        return own + jnp.where(shared, got, 0.0)
+
+    coarse = (0.5 * joined(low_h, high_h, rec_h, far_h)).astype(BF16)
+    act = dot(coarse, w_coarse[...])
+    value, grad = silu_pair(act)
+    both[:, :D] = value.astype(BF16)
+    grad_act = (joined(low_c, high_c, rec_c, far_c) * grad).astype(BF16)
+    both[:, D:] = dot_nt(grad_act, w_coarse[...]).astype(BF16)
+    weighed = (grad_act.astype(F32) * jnp.where(shared, 0.5, 1.0)).astype(BF16)
+    third = dot_tn(coarse, weighed)
+    across = lax.broadcasted_iota(jnp.int32, (N, N), 1)
+    flip[...] = (lab_col[...] == across).astype(F32).astype(BF16)
+    back = dot(flip[...], both[:, D:])
+    grad_pre = ((ct_ref[s].astype(F32) + 0.5 * back) * slope[s].astype(F32)).astype(BF16)
+    first = dot_tn(x_ref[s], grad_pre)
+    second = dot_tn(agg[s], grad_pre)
+    if more:
+        g0[...] = old0[...] + first
+        g1[...] = old1[...] + second
+        g2[...] = old2[...] + third
+    else:
+        g0[...] = first
+        g1[...] = second
+        g2[...] = third
+    out[0] = (hidden[s].astype(F32) + dot(flip[...], both[:, :D])).astype(BF16)
+
+
+def tail(s, args, old):
+    grads = (shape(D, D, dtype=F32),) * 3
+    more = old is not None
+    extra = list(old) if more else []
+    return pl.pallas_call(
+        functools.partial(tail_kernel, s, more),
+        out_shape=grads + (shape(SIDE, N, D),),
+        grid_spec=pl.GridSpec(
+            grid=(1,),
+            in_specs=[VM] * (len(args) + (3 if more else 0))
+            + ([pl.BlockSpec(memory_space=pl.ANY)] if more else []),
+            out_specs=(VM, VM, VM, pl.BlockSpec((1, N, D), lambda i: (s, 0, 0))),
+            scratch_shapes=[pltpu.VMEM((N, N), BF16), pltpu.VMEM((N, 2 * D), BF16)],
+        ),
+        input_output_aliases={len(args) + 3: 3} if more else {},
+        compiler_params=pltpu.CompilerParams(vmem_limit_bytes=40 * 2**20),
+        cost_estimate=cost(8 * 2**30, 2**23),
+    )(*args, *extra)
 
 
 MESH = pl.DeviceIdType.MESH
@@ -222,71 +444,36 @@
     neighbour_weight,
     w_coarse,
 ):
-    scen, nodes, width = features.shape
-    side = tile_vals.shape[1]
-    blocks = nodes // side
-    tiled = features.reshape(scen, blocks, side, width)
-    to_next = pick_blocks(send_next, blocks, tiled)
-    to_prev = pick_blocks(send_prev, blocks, tiled)
+    to_next, to_prev = pick(send_next, send_prev, features.reshape(SIDE, NB, BLK, D))
     got_prev = shifted(to_next, "dom", 1)
     got_next = shifted(to_prev, "dom", -1)
-    extended = jnp.concatenate([tiled, got_prev, got_next], axis=1)
-    picked = pick_blocks(tile_col, extended.shape[1], extended)
-    terms = jnp.einsum("tij,stjd->stid", tile_vals, picked, preferred_element_type=jnp.float32)
-    rowhot = (tile_row[None, :] == jnp.arange(blocks, dtype=jnp.int32)[:, None]).astype(jnp.float32)
-    summed = jnp.einsum("rt,stid->srid", rowhot, terms, precision=lax.Precision.HIGHEST)
-    neighbour_total = summed.reshape(scen, nodes, width).astype(jnp.bfloat16)
-    preactivation = jnp.einsum(
-        "jkb,bt->jkt", features, self_weight, preferred_element_type=jnp.float32
+    lab_row, lab_col, count, low_c0, low_c1, high_c = label(cluster, cotangent)
+    most = lax.pmax(count[0, 0], ("dom", "batch"))
+    rec_c0 = partner(low_c0)
+    rec_c1 = partner(low_c1)
+    agg, hidden, slope, low_h0, low_h1, high_h = node_step(
+        tile_row, tile_col, lab_row, features, got_prev, got_next, tile_vals,
+        self_weight, neighbour_weight,
     )
-    preactivation = preactivation + jnp.einsum(
-        "jkb,bt->jkt", neighbour_total, neighbour_weight, preferred_element_type=jnp.float32
+    rec_h0 = partner(low_h0)
+    rec_h1 = partner(low_h1)
+    far_h, far_c = lax.cond(
+        most > LOW,
+        lambda h, c: (partner(h), partner(c)),
+        lambda h, c: (jnp.zeros_like(h), jnp.zeros_like(c)),
+        high_h,
+        high_c,
     )
-    hidden = jax.nn.silu(preactivation).astype(jnp.bfloat16)
-    table = member_table(cluster, nodes)
-    parity = lax.axis_index("dom") % 2
-    half = nodes // 2
-    own_start = parity * half
-
-    def owned(array):
-        return lax.dynamic_slice_in_dim(array, own_start, half, 1)
-
-    partial_value = pooling(hidden, table)
-    grad_partial = pooling(cotangent, table)
-    partner_sums = partner(partial_value.astype(jnp.bfloat16), "dom", 0).astype(partial_value.dtype)
-    coarse = (0.5 * (partial_value + partner_sums)).astype(jnp.bfloat16)
-    act = jnp.einsum("skd,de->ske", coarse, w_coarse, preferred_element_type=jnp.float32)
-    lifted = jax.nn.silu(act).astype(jnp.bfloat16)
-    grad_lift = grad_partial + partner(grad_partial.astype(jnp.bfloat16), "dom", 0).astype(
-        grad_partial.dtype
+    rest = (hidden, slope, agg, features, cotangent, w_coarse)
+    old = tail(
+        0, (count, lab_col, rec_h0, rec_c0, far_h, far_c, low_h0, high_h, low_c0, high_c) + rest, None
     )
-    grad_act = (grad_lift * dsilu(act)).astype(jnp.bfloat16)
-    term_coarse = jnp.einsum(
-        "skd,ske->de", owned(coarse), owned(grad_act), preferred_element_type=jnp.float32
+    *grads, output = tail(
+        1, (count, lab_col, rec_h1, rec_c1, far_h, far_c, low_h1, high_h, low_c1, high_c) + rest, old
     )
-    grad_down = jnp.einsum(
-        "ske,de->skd", grad_act, w_coarse, preferred_element_type=jnp.float32
-    ).astype(jnp.bfloat16)
-    spread = lookup(lifted, table)
-    output = (hidden.astype(jnp.float32) + spread).astype(jnp.bfloat16)
-    back = lookup(grad_down, table)
-    grad_hidden = cotangent.astype(jnp.float32) + 0.5 * back
-    preactivation_gradient = (grad_hidden * dsilu(preactivation)).astype(jnp.bfloat16)
-    self_contribution = jnp.einsum(
-        "btv,btq->vq", features, preactivation_gradient, preferred_element_type=jnp.float32
-    )
-    neighbour_contribution = jnp.einsum(
-        "btv,btq->vq", neighbour_total, preactivation_gradient, preferred_element_type=jnp.float32
-    )
-    totals = reduce_all((self_contribution, neighbour_contribution, term_coarse))
-    totals = totals.astype(jnp.float32)
-    gradient_scale = 1.0 / math.sqrt(scen * lax.axis_size("batch") * nodes * lax.axis_size("dom"))
-    return (
-        output,
-        totals[0] * gradient_scale,
-        totals[1] * gradient_scale,
-        totals[2] * gradient_scale,
-    )
+    totals = reduce_all(grads).astype(F32)
+    scale = 1.0 / math.sqrt(SIDE * lax.axis_size("batch") * N * lax.axis_size("dom"))
+    return output, totals[0] * scale, totals[1] * scale, totals[2] * scale
 
 
 def solution(mesh):

time: 253 us -> 198 us (0.78); the launches traced: 248 us -> 198 us
  blocking collectives: 0 us -> 86 us
  waiting for transfers between devices: 84.6 us -> 0.02 us
  matrix products: 78.3 us -> 0 us
  Pallas kernels: 40 us -> 82.7 us
  local copies, waits for them, and re-layouts: 31.1 us -> 15.9 us
  other arithmetic: 6.06 us -> 2.21 us
  starting transfers between devices: 6.82 us -> 9.76 us
    pmax x0 -> x1, blocking collectives: none -> 86 us  [local(): most = lax.pmax(count[0, 0], ('dom', 'batch'))]
    dot_general x15 -> x0, matrix products: 78.3 us -> none  [the longest x1 18.5 us: local(): jnp.einsum('tij,stjd->stid', tile_vals, picked, preferred_element_type=jn...]
    ppermute x2 -> x4, waiting for transfers between devices: 76.1 us -> 0.01 us  [partner(): return lax.ppermute(value, 'dom', pairs)]
    pallas_call x0 -> x5, Pallas kernels: none -> 50.4 us  [the longest x2 20.9 us: tail(): pl.pallas_call(functools.partial(tail_kernel, s, more), out_shape=grads +...]
    transpose x1 -> x0, local copies, waits for them, and re-layouts: 20 us -> none  [local(): jnp.einsum('tij,stjd->stid', tile_vals, picked, preferred_element_type=jn...]
    ppermute x2, waiting for transfers between devices: 8.54 us -> 0.01 us  [shifted(): return lax.ppermute(x, axis, pairs)]
    unnamed x38 -> x44, local copies, waits for them, and re-layouts: 5.01 us -> 13.1 us
    pallas_call x1, Pallas kernels: 40 us -> 32.3 us  [reduce_all(): pl.pallas_call(reduce_kernel, out_shape=jax.ShapeDtypeStruct((3, 2, 4, 4,...]
  transfers between devices with their start and end apart: 4 -> 6, of which waited for: 4 -> 0; matrix products, arithmetic and copies ran while one was open for 8% -> 1% of each run, Pallas kernels for 0% -> 18%
where the time goes in v2:
time: 198 us
  blocking collectives  86 us (43%)
  Pallas kernels  82.7 us (42%)
  local copies, waits for them, and re-layouts  15.9 us (8%)
  starting transfers between devices  9.76 us (5%)
  other arithmetic  2.21 us (1%)
    pmax x1, blocking collectives, local(): most = lax.pmax(count[0, 0], ('dom', 'batch'))  86 us
    pallas_call x1, Pallas kernels, reduce_all(): pl.pallas_call(reduce_kernel, out_shape=jax.ShapeDtypeStruct((3, 2, 4, 4,...  32.3 us
    pallas_call x2, Pallas kernels, tail(): pl.pallas_call(functools.partial(tail_kernel, s, more), out_shape=grads +...  20.9 us
    pallas_call x1, Pallas kernels, node_step(): pl.pallas_call(node_kernel, out_shape=(full, full, full, shape(LOW, D), s...  16.2 us
    unnamed x44, local copies, waits for them, and re-layouts  13.1 us
    pallas_call x1, Pallas kernels, label(): pl.pallas_call(label_kernel, out_shape=(shape(1, N, dtype=jnp.int32), sha...  9.04 us
    ppermute x2, starting transfers between devices, shifted(): return lax.ppermute(x, axis, pairs)  6.09 us
    pallas_call x1, Pallas kernels, pick(): pl.pallas_call(pick_kernel, out_shape=(shape(SIDE, 2, BLK, D), shape(SIDE...  4.22 us
  transfers between devices with their start and end apart: 6, of which 0 were waited for; matrix products, arithmetic and copies ran while one was open for 1% of the time, Pallas kernels for 18%

profile of v2, /device:TPU:1, one launch (start us, length us, event | category | flops | bytes accessed | tf_op | source)
XLA Modules:
  0.0 198.0 jit_solution(15418840797929782001)
XLA Ops:
  0.6 0.0 copy-start.1
  0.6 4.2 %shard_map.139 = (bf16[2,2,128,512]{3,2,1,0:T(8,128)(2,1)}, bf16[2,2,128,512]{3,2,1,0:T(8,128)(2,1)}) custom-call(s32[2]{0:T(128)} %nexts.1, s32[2]{0:T(128)} %prevs.1, bf16[2,8,128,512]{3,2,1,0:T(8,128)(2,1)} %bitcast.10, bf16[2,8,128,512]{3,2,1,0:T(8,128)(2,1)} %bitcast.11), custom_call_target="tpu_custom_call" | custom-call | bytes 2097152 | tf_op jit(solution)/shard_map/pallas_call | solution.py:66
  4.9 4.8 %collective-permute-start.2 = (bf16[2,2,128,512]{3,2,1,0:T(8,128)(2,1)}, bf16[2,2,128,512]{3,2,1,0:T(8,128)(2,1)}, u32[]{:S(2)}, u32[]{:S(2)}) collective-permute-start(bf16[2,2,128,512]{3,2,1,0:T(8,128)(2,1)} %get-tuple-element.37), channel_id=1, source_target_pairs={{0,2},{2,4},{4,6},{6,8},{8,10},{10,12},{12,14},{14,16},{16,18},{18... | collective-permute-start | bytes 1572872 | tf_op jit(solution)/shard_map/ppermute | solution.py:26
  9.7 1.3 collective-permute-start.3
  11.0 0.0 copy-done.1
  11.0 0.2 copy.16.col_ref
  11.2 0.0 copy-start.2
  11.2 1.6 copy-done.2
  12.8 0.0 copy-start
  12.8 0.0 copy-start.3
  12.8 0.0 copy-start.6
  12.8 0.0 copy-start.7
  12.8 0.0 copy-start.9
  12.8 0.0 copy-start.10
  12.8 9.0 %shard_map.138 = (s32[1,1024]{1,0:T(1,128)S(1)}, s32[1024,1]{1,0:T(8,128)S(1)}, s32[8,128]{1,0:T(8,128)S(1)}, bf16[576,512]{1,0:T(8,128)(2,1)}, bf16[576,512]{1,...) custom-call(s32[1,1024]{1,0:T(1,128)S(1)} %bitcast.16, s32[1024,1]{1,0:T(8,128)S(1)} %copy.16.col_ref, ...), custom_call_target="tpu_custom_call" | custom-call | flops 4294967296 | bytes 4194304 | tf_op jit(solution)/shard_map/pallas_call | solution.py:136
  21.9 0.0 copy-start.19
  21.9 0.8 copy-done.19
  22.7 2.1 %collective-permute-start.7 = (bf16[576,512]{1,0:T(8,128)(2,1)}, bf16[576,512]{1,0:T(8,128)(2,1)}, u32[]{:S(2)}, u32[]{:S(2)}) collective-permute-start(bf16[576,512]{1,0:T(8,128)(2,1)} %get-tuple-element.49.low_c), channel_id=1, source_target_pairs={{0,2},{2,0},{4,6},{6,4},{8,10},{10,8},{12,14},{14,12},{16,18},{18,... | collective-permute-start | bytes 1769480 | tf_op jit(solution)/shard_map/ppermute | solution.py:31
  24.8 0.0 collective-permute-done.2.prev_ref
  24.8 0.0 collective-permute-done.3.next_ref
  24.8 0.0 copy-done
  24.8 0.0 copy-done.3
  24.8 0.0 copy-done.6
  24.8 0.0 copy-done.7
  24.8 0.0 copy-done.9
  24.8 0.0 copy-done.10
  24.8 0.0 copy-start.8
  24.8 16.2 %shard_map.140 = (bf16[2,1024,512]{2,1,0:T(8,128)(2,1)S(1)}, bf16[2,1024,512]{2,1,0:T(8,128)(2,1)S(1)}, bf16[2,1024,512]{2,1,0:T(8,128)(2,1)S(1)}, bf16[576,512]...) custom-call(s32[32]{0:T(128)S(1)} %copy-done.9, s32[32]{0:T(128)S(1)} %copy-done.10, ...), custom_call_target="tpu_custom_call" | custom-call | flops 10737418240 | bytes 8388608 | tf_op jit(solution)/shard_map/pallas_call | solution.py:194
  41.0 0.0 copy-start.4
  41.0 0.8 copy-done.4
  41.8 0.0 copy-start.11
  41.8 1.3 copy-done.11
  43.2 0.0 copy-start.13
  43.2 1.3 copy-done.13
  44.5 0.0 copy-start.16
  44.5 1.4 copy-done.16
  45.9 0.0 collective-permute-start.6
  45.9 1.4 collective-permute-start.5
  47.3 0.5 slice.15
  47.8 86.0 %pmax.7 = s32[]{:T(128)} all-reduce(s32[]{:T(128)} %bitcast.3), channel_id=1, replica_groups=mesh['dom'=64,'batch'=2] {'dom','batch'}, use_global_device_ids=true, to_apply=%region_0.0 | all-reduce | flops 1 | bytes 8 | tf_op jit(solution)/shard_map/pmax | solution.py:451
  134.4 2.1 %conditional.1 = (bf16[2,448,512]{2,1,0:T(8,128)(2,1)}, bf16[2,448,512]{2,1,0:T(8,128)(2,1)}) conditional(s32[]{:T(128)} %convert_element_type.7, () %tuple.16, (bf16[2,448,512]{2,1,0:T(8,128)(2,1)}, bf16[2,448,512]{2,1,0:T(8,128)(2,1)S(1)}) %tuple.17), branch_computations={%region_1.0_spmd, %region_2.0_spmd} | conditional | bytes 7340128 | solution.py:460
  134.4 1.1 broadcast.14.clone
  135.5 1.0 broadcast.14
  136.5 0.1 collective-permute-start.4
  136.6 0.0 collective-permute-done.7.rec_c
  136.6 0.0 collective-permute-done.6.rec_h
  136.6 0.0 copy-done.8
  136.6 0.0 copy-start.12
  136.6 1.6 copy-done.12
  138.2 0.0 copy-start.14
  138.2 1.6 copy-done.14
  139.8 1.6 copy-done.17
  141.4 1.0 copy-done.20
  142.5 10.6 %shard_map.141 = (f32[512,512]{1,0:T(8,128)S(1)}, f32[512,512]{1,0:T(8,128)S(1)}, f32[512,512]{1,0:T(8,128)S(1)}, bf16[2,1024,512]{2,1,0:T(8,128)(2,1)}) custom-call(s32[8,128]{1,0:T(8,128)S(1)} %get-tuple-element.34.count, s32[1024,1]{1,0:T(8,128)S(1)} %copy-done.20, bf16[576,512]{1,0:T(8,128)(2,1)S(1)} %collective-permute-done.6.rec_h, ...), custom_call_target="tpu_custom_call" | custom-call | flops 8589934592 | bytes 8388608 | tf_op jit(solution)/shard_map/pallas_call | solution.py:253
  153.1 0.0 collective-permute-done.5.rec_c
  153.1 0.0 collective-permute-done.4.rec_h
  153.1 0.0 copy-done.5
  153.1 0.0 copy-done.15
  153.1 0.0 copy-done.18
  153.1 0.0 copy-done.21
  153.1 10.3 %shard_map.142 = (f32[512,512]{1,0:T(8,128)S(1)}, f32[512,512]{1,0:T(8,128)S(1)}, f32[512,512]{1,0:T(8,128)S(1)}, bf16[2,1024,512]{2,1,0:T(8,128)(2,1)}) custom-call(s32[8,128]{1,0:T(8,128)S(1)} %get-tuple-element.34.count, s32[1024,1]{1,0:T(8,128)S(1)} %copy-done.20, ...), custom_call_target="tpu_custom_call", output_to_operand_aliasing={{3}: (19, {})} | custom-call | flops 8589934592 | bytes 8388608 | tf_op jit(solution)/shard_map/pallas_call | solution.py:253
  163.4 32.3 %shard_map.143 = bf16[3,2,4,4,16,512]{5,4,3,2,1,0:T(8,128)(2,1)S(1)} custom-call(f32[2,4,4,16,512]{4,3,2,1,0:T(8,128)S(1)} %bitcast.12, f32[2,4,4,16,512]{4,3,2,1,0:T(8,128)S(1)} %bitcast.13, f32[2,4,4,16,512]{4,3,2,1,0:T(8,128)S(1)} %bitcast.14), custom_call_target="tpu_custom_call" | custom-call | tf_op jit(solution)/shard_map/pallas_call | solution.py:405
  195.8 0.5 convert_element_type.8
  196.2 1.8 slice_multiply_fusion
  (6 shorter events, 0.0 us)
Async XLA Ops:
  0.6 10.3 %copy-start.1 = (s32[1024]{0:T(1024)S(1)}, s32[1024]{0:T(1024)}, u32[]{:S(2)}) copy-start(s32[1024]{0:T(1024)} %param.19) | copy-start | bytes 12292
  4.9 19.9 %collective-permute-start.2 = (bf16[2,2,128,512]{3,2,1,0:T(8,128)(2,1)}, bf16[2,2,128,512]{3,2,1,0:T(8,128)(2,1)}, u32[]{:S(2)}, u32[]{:S(2)}) collective-permute-start(bf16[2,2,128,512]{3,2,1,0:T(8,128)(2,1)} %get-tuple-element.37), channel_id=1, source_target_pairs={{0,2},{2,4},{4,6},{6,8},{8,10},{10,12},{12,14},{14,16},{16,18},{18... | collective-permute-start | bytes 1572872 | tf_op jit(solution)/shard_map/ppermute | solution.py:26
  9.7 15.1 %collective-permute-start.3 = (bf16[2,2,128,512]{3,2,1,0:T(8,128)(2,1)}, bf16[2,2,128,512]{3,2,1,0:T(8,128)(2,1)}, u32[]{:S(2)}, u32[]{:S(2)}) collective-permute-start(bf16[2,2,128,512]{3,2,1,0:T(8,128)(2,1)} %get-tuple-element.38), channel_id=1, source_target_pairs={{2,0},{4,2},{6,4},{8,6},{10,8},{12,10},{14,12},{16,14},{18,16},{20... | collective-permute-start | bytes 1572872 | tf_op jit(solution)/shard_map/ppermute | solution.py:26
  11.2 1.6 copy-start.2
  12.8 12.0 %copy-start = (bf16[2,1024,512]{2,1,0:T(8,128)(2,1)S(1)}, bf16[2,1024,512]{2,1,0:T(8,128)(2,1)}, u32[]{:S(2)}) copy-start(bf16[2,1024,512]{2,1,0:T(8,128)(2,1)} %x_ref.5) | copy-start | bytes 6291460
  12.8 12.0 %copy-start.3 = (bf16[32,128,128]{2,1,0:T(8,128)(2,1)S(1)}, bf16[32,128,128]{2,1,0:T(8,128)(2,1)}, u32[]{:S(2)}) copy-start(bf16[32,128,128]{2,1,0:T(8,128)(2,1)} %tiles.1) | copy-start | bytes 3145732
  12.8 12.0 %copy-start.6 = (bf16[512,512]{1,0:T(8,128)(2,1)S(1)}, bf16[512,512]{1,0:T(8,128)(2,1)}, u32[]{:S(2)}) copy-start(bf16[512,512]{1,0:T(8,128)(2,1)} %w_self.1) | copy-start | bytes 1572868
  12.8 12.0 %copy-start.7 = (bf16[512,512]{1,0:T(8,128)(2,1)S(1)}, bf16[512,512]{1,0:T(8,128)(2,1)}, u32[]{:S(2)}) copy-start(bf16[512,512]{1,0:T(8,128)(2,1)} %w_neigh.1) | copy-start | bytes 1572868
  12.8 12.0 %copy-start.9 = (s32[32]{0:T(128)S(1)}, s32[32]{0:T(128)}, u32[]{:S(2)}) copy-start(s32[32]{0:T(128)} %rows.1) | copy-start | bytes 388
  12.8 12.0 %copy-start.10 = (s32[32]{0:T(128)S(1)}, s32[32]{0:T(128)}, u32[]{:S(2)}) copy-start(s32[32]{0:T(128)} %cols.1) | copy-start | bytes 388
  21.9 0.8 copy-start.19
  22.7 113.9 %collective-permute-start.7 = (bf16[576,512]{1,0:T(8,128)(2,1)}, bf16[576,512]{1,0:T(8,128)(2,1)}, u32[]{:S(2)}, u32[]{:S(2)}) collective-permute-start(bf16[576,512]{1,0:T(8,128)(2,1)} %get-tuple-element.49.low_c), channel_id=1, source_target_pairs={{0,2},{2,0},{4,6},{6,4},{8,10},{10,8},{12,14},{14,12},{16,18},{18,... | collective-permute-start | bytes 1769480 | tf_op jit(solution)/shard_map/ppermute | solution.py:31
  24.8 111.8 %copy-start.8 = (bf16[512,512]{1,0:T(8,128)(2,1)S(1)}, bf16[512,512]{1,0:T(8,128)(2,1)}, u32[]{:S(2)}) copy-start(bf16[512,512]{1,0:T(8,128)(2,1)} %w_coarse.3) | copy-start | bytes 1572868
  41.0 0.8 copy-start.4
  41.8 1.3 copy-start.11
  43.2 1.3 copy-start.13
  44.5 1.4 copy-start.16
  45.9 90.8 %collective-permute-start.6 = (bf16[576,512]{1,0:T(8,128)(2,1)}, bf16[576,512]{1,0:T(8,128)(2,1)S(1)}, u32[]{:S(2)}, u32[]{:S(2)}) collective-permute-start(bf16[576,512]{1,0:T(8,128)(2,1)} %get-tuple-element.48.low_h), channel_id=1, source_target_pairs={{0,2},{2,0},{4,6},{6,4},{8,10},{10,8},{12,14},{14,12},{16,18},{18,... | collective-permute-start | bytes 1769480 | tf_op jit(solution)/shard_map/ppermute | solution.py:31
  45.9 107.2 %collective-permute-start.5 = (bf16[576,512]{1,0:T(8,128)(2,1)S(1)}, bf16[576,512]{1,0:T(8,128)(2,1)S(1)}, u32[]{:S(2)}, u32[]{:S(2)}) collective-permute-start(bf16[576,512]{1,0:T(8,128)(2,1)S(1)} %get-tuple-element.40.low_c), channel_id=1, source_target_pairs={{0,2},{2,0},{4,6},{6,4},{8,10},{10,8},{12,14},{14,12},{16,18},{18,... | collective-permute-start | bytes 1769480 | tf_op jit(solution)/shard_map/ppermute | solution.py:31
  136.5 16.6 %collective-permute-start.4 = (bf16[576,512]{1,0:T(8,128)(2,1)}, bf16[576,512]{1,0:T(8,128)(2,1)S(1)}, u32[]{:S(2)}, u32[]{:S(2)}) collective-permute-start(bf16[576,512]{1,0:T(8,128)(2,1)} %copy-done.4), channel_id=1, source_target_pairs={{0,2},{2,0},{4,6},{6,4},{8,10},{10,8},{12,14},{14,12},{16,18},{18,... | collective-permute-start | bytes 1769480 | tf_op jit(solution)/shard_map/ppermute | solution.py:31
  136.6 1.6 copy-start.12
  138.2 1.6 copy-start.14
  139.8 1.6 copy-start.17
  141.4 1.0 copy-start.20
  142.4 10.6 %copy-start.5 = (bf16[576,512]{1,0:T(8,128)(2,1)S(1)}, bf16[576,512]{1,0:T(8,128)(2,1)}, u32[]{:S(2)}) copy-start(bf16[576,512]{1,0:T(8,128)(2,1)} %copy-done.4) | copy-start | bytes 1769476
  142.5 10.6 %copy-start.15 = (bf16[2,1024,512]{2,1,0:T(8,128)(2,1)S(1)}, bf16[2,1024,512]{2,1,0:T(8,128)(2,1)}, u32[]{:S(2)}) copy-start(bf16[2,1024,512]{2,1,0:T(8,128)(2,1)} %copy-done.13) | copy-start | bytes 6291460
  142.5 10.6 %copy-start.18 = (bf16[2,1024,512]{2,1,0:T(8,128)(2,1)S(1)}, bf16[2,1024,512]{2,1,0:T(8,128)(2,1)}, u32[]{:S(2)}) copy-start(bf16[2,1024,512]{2,1,0:T(8,128)(2,1)} %copy-done.16) | copy-start | bytes 6291460
  142.5 10.7 %copy-start.21 = (bf16[2,448,512]{2,1,0:T(8,128)(2,1)S(1)}, bf16[2,448,512]{2,1,0:T(8,128)(2,1)}, u32[]{:S(2)}) copy-start(bf16[2,448,512]{2,1,0:T(8,128)(2,1)} %get-tuple-element.41.high_h) | copy-start | bytes 2752516

commit v3 on v0

v3 whole, which is shorter than its diff:
```python
import math

import jax
import jax.numpy as jnp
from jax import lax
from jax.experimental import pallas as pl
from jax.experimental.pallas import tpu as pltpu
from jax.sharding import PartitionSpec as P

N = 1024
D = 512
BLK = 128
NB = 8
SIDE = 2
LOW = 576
F32 = jnp.float32
BF16 = jnp.bfloat16
VM = pl.BlockSpec(memory_space=pltpu.VMEM)
MESH = pl.DeviceIdType.MESH
SM = pl.BlockSpec(memory_space=pltpu.SMEM)


def partner(value):
    pairs = [(source, source ^ 1) for source in range(lax.axis_size("dom"))]
    return lax.ppermute(value, "dom", pairs)


def silu_pair(value):
    sig = jax.nn.sigmoid(value)
    return value * sig, sig * (1.0 + value * (1.0 - sig))


def dot(left, right):
    return jnp.dot(left, right, preferred_element_type=F32)


def dot_tn(left, right):
    return lax.dot_general(left, right, (((0,), (0,)), ((), ())), preferred_element_type=F32)


def dot_nt(left, right):
    return lax.dot_general(left, right, (((1,), (1,)), ((), ())), preferred_element_type=F32)


def shape(*dims, dtype=BF16):
    return jax.ShapeDtypeStruct(dims, dtype)


def cost(flops, size):
    return pl.CostEstimate(flops=flops, bytes_accessed=size, transcendentals=0)


class Place:
    def __init__(self):
        self.dom = lax.axis_index("dom")
        self.core = lax.axis_index("batch")
        self.at = (self.dom // 16, (self.dom // 4) % 4, self.dom % 4)

    def peer(self, axis, k):
        spot = (self.at[axis] + k) % 4
        return (self.dom + (spot - self.at[axis]) * (16, 4, 1)[axis], self.core), spot


def remote(src, dst, send, recv, device):
    copy = pltpu.make_async_remote_copy(
        src_ref=src, dst_ref=dst, send_sem=send, recv_sem=recv, device_id=device, device_id_type=MESH
    )
    copy.start()
    return copy


def greet(devices):
    barrier = pltpu.get_barrier_semaphore()
    for device in devices:
        pl.semaphore_signal(barrier, inc=1, device_id=device, device_id_type=MESH)
    return lambda: pl.semaphore_wait(barrier, len(devices))


def front_kernel(
    nexts, prevs, row_ref, col_ref, x_ref, ct_ref,
    lab_row, lab_col, count, most, sums, low, got_prev, got_next,
    to_next, to_prev, table, flip, peak, peaks,
    halo_send, halo_recv, peak_send, peak_recv,
):
    here = Place()
    nxt = ((here.dom + 1) % 64, here.core)
    prv = ((here.dom + 63) % 64, here.core)
    wait = greet([nxt, prv] + [here.peer(a, k)[0] for a in range(3) for k in (1, 2, 3)])
    for s in range(SIDE):
        for j in range(2):
            to_next[s, j] = x_ref[s, nexts[j]]
            to_prev[s, j] = x_ref[s, prevs[j]]
    wait()
    halo = []
    for s in range(SIDE):
        halo.append(remote(to_next.at[s], got_prev.at[s], halo_send.at[0, s], halo_recv.at[0, s], nxt))
        halo.append(remote(to_prev.at[s], got_next.at[s], halo_send.at[1, s], halo_recv.at[1, s], prv))

    row, col = row_ref[...], col_ref[...]
    step = 256

    def tables(i, carry):
        at = pl.ds(pl.multiple_of(i * step, step), step)
        down = lax.broadcasted_iota(jnp.int32, (step, N), 0) + i * step
        across = lax.broadcasted_iota(jnp.int32, (step, N), 1)
        table[at, :] = (row == down).astype(F32).astype(BF16)
        flip[at, :] = (col_ref[at, :] == across).astype(F32).astype(BF16)
        return carry

    lax.fori_loop(0, N // step, tables, 0)
    held_row = dot(jnp.ones((16, N), BF16), flip[...])
    held_col = dot(table[...], jnp.ones((N, 128), BF16))

    def ones_of(held, value):
        return (held == value).astype(F32)

    total = jnp.sum(ones_of(held_row[:1], 1.0), axis=1, keepdims=True)
    count[...] = jnp.broadcast_to(total, (8, 128)).astype(jnp.int32)
    peak[0] = jnp.broadcast_to(total, (8, 128))

    def spread(a):
        return [
            remote(peak.at[a], peaks.at[a, k - 1], peak_send.at[a, k - 1], peak_recv.at[a, k - 1], here.peer(a, k)[0])
            for k in (1, 2, 3)
        ]

    def settle(a, copies):
        for copy in copies:
            copy.wait()
        top = peak[a]
        for k in range(3):
            top = jnp.maximum(top, peaks[a, k])
        return top

    first = spread(0)
    row_in = jnp.concatenate([ones_of(held_row, 1.0), ones_of(held_row, 2.0)], axis=0).astype(BF16)
    col_in = jnp.concatenate([ones_of(held_col, 1.0), ones_of(held_col, 2.0)], axis=1).astype(BF16)

    def before(i, carry):
        at = pl.ds(pl.multiple_of(i * step, step), step)
        down = lax.broadcasted_iota(jnp.int32, (step, N), 0) + i * step
        across = lax.broadcasted_iota(jnp.int32, (step, N), 1)
        table[at, :] = (across < down).astype(F32).astype(BF16)
        flip[at, :] = (down < across).astype(F32).astype(BF16)
        return carry

    lax.fori_loop(0, N // step, before, 0)
    row_rank = dot(row_in, flip[...])
    col_rank = dot(table[...], col_in)
    new_row = jnp.where(held_row[:1] == 1.0, row_rank[:1], total + row_rank[16:17])
    new_col = jnp.where(held_col[:, :1] == 1.0, col_rank[:, :1], total + col_rank[:, 128:129])
    across = lax.broadcasted_iota(jnp.int32, (N, N), 1)
    down = lax.broadcasted_iota(jnp.int32, (N, N), 0)
    col_lab = jnp.sum(jnp.where(col == across, new_row, 0.0), axis=1, keepdims=True)
    row_lab = jnp.sum(jnp.where(row == down, new_col, 0.0), axis=0, keepdims=True)
    lab_col[...] = col_lab.astype(jnp.int32)
    lab_row[...] = row_lab.astype(jnp.int32)
    peak[1] = settle(0, first)
    second = spread(1)
    table[...] = (row_lab.astype(jnp.int32) == down).astype(F32).astype(BF16)

    def pool(s):
        got = dot(table[...], ct_ref[s]).astype(BF16)
        sums[s] = got
        low[s] = got[:LOW]

    pool(0)
    peak[2] = settle(1, second)
    third = spread(2)
    pool(1)
    most[...] = settle(2, third).astype(jnp.int32)
    for copy in halo:
        copy.wait()

    @pl.when(here.dom == 0)
    def _():
        got_prev[...] = jnp.zeros_like(got_prev)

    @pl.when(here.dom == 63)
    def _():
        got_next[...] = jnp.zeros_like(got_next)


def front(send_next, send_prev, cluster, features, cotangent):
    halo = (SIDE, 2, BLK, D)
    return pl.pallas_call(
        front_kernel,
        out_shape=(
            shape(1, N, dtype=jnp.int32),
            shape(N, 1, dtype=jnp.int32),
            shape(8, 128, dtype=jnp.int32),
            shape(8, 128, dtype=jnp.int32),
            shape(SIDE, N, D),
            shape(SIDE, LOW, D),
            shape(*halo),
            shape(*halo),
        ),
        in_specs=[SM, SM] + [VM] * 4,
        out_specs=(VM,) * 8,
        scratch_shapes=[
            pltpu.VMEM(halo, BF16),
            pltpu.VMEM(halo, BF16),
            pltpu.VMEM((N, N), BF16),
            pltpu.VMEM((N, N), BF16),
            pltpu.VMEM((3, 8, 128), F32),
            pltpu.VMEM((3, 3, 8, 128), F32),
            pltpu.SemaphoreType.DMA((2, SIDE)),
            pltpu.SemaphoreType.DMA((2, SIDE)),
            pltpu.SemaphoreType.DMA((3, 3)),
            pltpu.SemaphoreType.DMA((3, 3)),
        ],
        compiler_params=pltpu.CompilerParams(
            collective_id=0, has_side_effects=True, vmem_limit_bytes=28 * 2**20
        ),
        cost_estimate=cost(4 * 2**30, 2**22),
    )(
        send_next, send_prev, cluster.reshape(1, N), cluster.reshape(N, 1),
        features.reshape(SIDE, NB, BLK, D), cotangent,
    )


def node_kernel(
    rows, cols, lab_row, x_ref, prev_ref, next_ref, tiles, w_self, w_neigh,
    agg, hidden, slope, sums, ext, acc, table,
):
    for s in range(SIDE):
        span = slice(s * D, (s + 1) * D)
        ext[0:NB, :, span] = x_ref[s].reshape(NB, BLK, D)
        ext[NB : NB + 2, :, span] = prev_ref[s]
        ext[NB + 2 : NB + 4, :, span] = next_ref[s]
    acc[...] = jnp.zeros_like(acc)

    def tile(t, carry):
        r = rows[t]
        acc[r] = acc[r] + dot(tiles[t], ext[cols[t]])
        return carry

    lax.fori_loop(0, tiles.shape[0], tile, 0)
    step = 256

    def block(i, carry):
        at = pl.ds(pl.multiple_of(i * step, step), step)
        down = lax.broadcasted_iota(jnp.int32, (step, N), 0) + i * step
        table[at, :] = (lab_row[...] == down).astype(F32).astype(BF16)
        for s in range(SIDE):
            span = slice(s * D, (s + 1) * D)
            got = acc[pl.ds(i * 2, 2), :, span].reshape(step, D).astype(BF16)
            agg[s, at, :] = got
            pre = dot(x_ref[s, at, :], w_self[...]) + dot(got, w_neigh[...])
            value, grad = silu_pair(pre)
            hidden[s, at, :] = value.astype(BF16)
            slope[s, at, :] = grad.astype(BF16)
        return carry

    lax.fori_loop(0, N // step, block, 0)
    for s in range(SIDE):
        sums[s] = dot(table[...], hidden[s]).astype(BF16)


def node_step(tile_row, tile_col, lab_row, features, got_prev, got_next, tiles, w_self, w_neigh):
    full = shape(SIDE, N, D)
    return pl.pallas_call(
        node_kernel,
        out_shape=(full,) * 4,
        in_specs=[SM, SM] + [VM] * 7,
        out_specs=(VM,) * 4,
        scratch_shapes=[
            pltpu.VMEM((NB + 4, BLK, SIDE * D), BF16),
            pltpu.VMEM((NB, BLK, SIDE * D), F32),
            pltpu.VMEM((N, N), BF16),
        ],
        compiler_params=pltpu.CompilerParams(vmem_limit_bytes=24 * 2**20),
        cost_estimate=cost(10 * 2**30, 2**23),
    )(tile_row, tile_col, lab_row, features, got_prev, got_next, tiles, w_self, w_neigh)


EARLY, MID, LAST = (640, 1024), (0, 384), (384, 640)
ORDERS = ((0, 1, 2), (1, 2, 0), (2, 0, 1))
ENTRY = (2, 0, 1)


def back_kernel(
    count, lab_col, sums_h, sums_c, rec_c, far_h, far_c, hidden, slope, agg, x_ref, ct_ref, w_coarse,
    total, out,
    rec_h, flip, lifted, down, coarse, weighed, x_turn, a_turn, w_turn, grad_pre, part, grads,
    send0, recv0, acc, buf1, recv1, sum2, buf2, recv2, sum3, buf3, recv3,
    swap_send, swap_recv, send_sem, recv_sem, side_send, side_recv,
):
    here = Place()
    core = here.core
    other = (here.dom, 1 - core)
    pair = (here.dom + 1 - 2 * (here.dom % 2), core)
    wait = greet([other, pair] + [here.peer(a, k)[0] for a in range(3) for k in (1, 2, 3)])
    wait()
    swaps = []
    for s in range(SIDE):
        for i, (lo, hi) in enumerate((MID, (LAST[0], LOW))):
            rows = pl.ds(lo, hi - lo)
            swaps.append(
                remote(sums_h.at[s, rows], rec_h.at[s, rows], swap_send.at[s, i], swap_recv.at[s, i], pair)
            )

    step = 256

    def one_hot(i, carry):
        at = pl.ds(pl.multiple_of(i * step, step), step)
        across = lax.broadcasted_iota(jnp.int32, (step, N), 1)
        flip[at, :] = (lab_col[at, :] == across).astype(F32).astype(BF16)
        return carry

    lax.fori_loop(0, N // step, one_hot, 0)
    w_turn[...] = w_coarse[...].T

    def level(s, span):
        lo, hi = span
        shared = lax.broadcasted_iota(jnp.int32, (hi - lo, 1), 0) + lo < count[0:1, 0:1]

        def joined(own, rec, far):
            if lo >= LOW:
                got = far[s, lo - LOW : hi - LOW]
            elif hi <= LOW:
                got = rec[s, lo:hi]
            else:
                got = jnp.concatenate([rec[s, lo:LOW], far[s, : hi - LOW]], axis=0)
            return own[s, lo:hi].astype(F32) + jnp.where(shared, got.astype(F32), 0.0)

        rows = (0.5 * joined(sums_h, rec_h, far_h)).astype(BF16)
        coarse[s, lo:hi] = rows
        value, grad = silu_pair(dot(rows, w_coarse[...]))
        lifted[s, lo:hi] = value.astype(BF16)
        grad_act = (joined(sums_c, rec_c, far_c) * grad).astype(BF16)
        down[s, lo:hi] = dot(grad_act, w_turn[...]).astype(BF16)
        weighed[s, lo:hi] = (grad_act.astype(F32) * jnp.where(shared, 0.5, 1.0)).astype(BF16)

    def looked(s, span):
        lo, hi = span
        return dot(flip[:, lo:hi], down[s, lo:hi])

    def product(s, span):
        lo, hi = span
        return dot_tn(coarse[s, lo:hi], weighed[s, lo:hi])

    def emit(s, lo, hi):
        out[s, lo:hi] = (hidden[s, lo:hi].astype(F32) + dot(flip[lo:hi, :], lifted[s])).astype(BF16)

    def store(p, value):
        grads[p] = value.reshape(2, 4, 4, 16, D)

    def load(p):
        return grads[p].reshape(D, D)

    for s in range(SIDE):
        level(s, EARLY)
        x_turn[s] = x_ref[s].T
        a_turn[s] = agg[s].T

    swaps[0].wait_recv()
    level(0, MID)
    swaps[1].wait_recv()
    level(0, LAST)
    back = dot(flip[...], down[0])
    grad_pre[...] = ((ct_ref[0].astype(F32) + 0.5 * back) * slope[0].astype(F32)).astype(BF16)
    store(0, dot(x_turn[0], grad_pre[...]))
    store(1, dot(a_turn[0], grad_pre[...]))
    store(2, product(0, (0, N)) + product(1, EARLY))
    part[...] = looked(1, EARLY)
    emit(0, 0, N)

    swaps[2].wait_recv()
    level(1, MID)
    part[...] += looked(1, MID)
    store(2, load(2) + product(1, MID))
    swaps[3].wait_recv()
    level(1, LAST)
    first = [None] * 3

    def hand(p):
        send0[p] = grads[p, 1 - core].astype(BF16)
        first[p] = remote(send0.at[p], recv0.at[p], side_send.at[0, p], side_recv.at[0, p], other)

    store(2, load(2) + product(1, LAST))
    hand(2)
    back = part[...] + looked(1, LAST)
    grad_pre[...] = ((ct_ref[1].astype(F32) + 0.5 * back) * slope[1].astype(F32)).astype(BF16)
    store(0, load(0) + dot(x_turn[1], grad_pre[...]))
    hand(0)
    store(1, load(1) + dot(a_turn[1], grad_pre[...]))
    hand(1)

    def scatter(p, phase, pick, landing):
        copies = []
        for k in (1, 2, 3):
            device, spot = here.peer(ORDERS[p][phase], k)
            copies.append(
                remote(
                    pick(spot), landing.at[p, k - 1], send_sem.at[phase, p, k - 1],
                    recv_sem.at[phase, p, k - 1], device,
                )
            )
        return copies

    def gather(p, phase, piece):
        return [
            remote(
                piece, piece, send_sem.at[5 - phase, p, k - 1], recv_sem.at[5 - phase, p, k - 1],
                here.peer(ORDERS[p][phase], k)[0],
            )
            for k in (1, 2, 3)
        ]

    def mine(p, phase):
        return here.at[ORDERS[p][phase]]

    def cols(spot):
        return pl.ds(pl.multiple_of(spot * 128, 128), 128)

    stages = [[None] * 3 for _ in range(6)]

    def arrived(stage, p):
        for copy in stages[stage][p]:
            copy.wait_recv()

    for p in ENTRY:
        first[p].wait_recv()
        value = grads[p, core] + recv0[p].astype(F32)
        acc[p] = value
        buf1[p] = value.astype(BF16)
        stages[0][p] = scatter(p, 0, lambda spot: buf1.at[p, spot], recv1)
    emit(1, 0, 512)
    for p in ENTRY:
        arrived(0, p)
        value = acc[p, mine(p, 0)]
        for k in range(3):
            value = value + recv1[p, k].astype(F32)
        sum2[p] = value
        buf2[p] = value.astype(BF16)
        stages[1][p] = scatter(p, 1, lambda spot: buf2.at[p, spot], recv2)
    emit(1, 512, 768)
    for p in ENTRY:
        arrived(1, p)
        value = sum2[p, mine(p, 1)]
        for k in range(3):
            value = value + recv2[p, k].astype(F32)
        sum3[p] = value
        buf3[p] = value.astype(BF16)
        stages[2][p] = scatter(p, 2, lambda spot: buf3.at[p, :, cols(spot)], recv3)
    emit(1, 768, 1024)
    for p in ENTRY:
        arrived(2, p)
        value = sum3[p, :, cols(mine(p, 2))]
        for k in range(3):
            value = value + recv3[p, k].astype(F32)
        piece = total.at[p, core, mine(p, 0), mine(p, 1), :, cols(mine(p, 2))]
        piece[...] = value.astype(BF16)
        stages[3][p] = gather(p, 2, piece)
    for p in ENTRY:
        arrived(3, p)
        stages[4][p] = gather(p, 1, total.at[p, core, mine(p, 0), mine(p, 1)])
    for p in ENTRY:
        arrived(4, p)
        stages[5][p] = gather(p, 0, total.at[p, core, mine(p, 0)])
    last = []
    for p in ENTRY:
        arrived(5, p)
        last.append(remote(total.at[p, core], total.at[p, core], side_send.at[1, p], side_recv.at[1, p], other))
    for copy in last:
        copy.wait_recv()
    for group in stages:
        for copies in group:
            for copy in copies:
                copy.wait_send()
    for copy in swaps + first + last:
        copy.wait_send()


def back_step(*args):
    half = (3, 4, 4, 16, D)
    return pl.pallas_call(
        back_kernel,
        out_shape=(shape(3, 2, 4, 4, 16, D), shape(SIDE, N, D)),
        in_specs=[VM] * len(args),
        out_specs=(VM, VM),
        scratch_shapes=[
            pltpu.VMEM((SIDE, LOW, D), BF16),
            pltpu.VMEM((N, N), BF16),
            pltpu.VMEM((SIDE, N, D), BF16),
            pltpu.VMEM((SIDE, N, D), BF16),
            pltpu.VMEM((SIDE, N, D), BF16),
            pltpu.VMEM((SIDE, N, D), BF16),
            pltpu.VMEM((SIDE, D, N), BF16),
            pltpu.VMEM((SIDE, D, N), BF16),
            pltpu.VMEM((D, D), BF16),
            pltpu.VMEM((N, D), BF16),
            pltpu.VMEM((N, D), F32),
            pltpu.VMEM((3, 2, 4, 4, 16, D), F32),
            pltpu.VMEM(half, BF16),
            pltpu.VMEM(half, BF16),
            pltpu.VMEM(half, F32),
            pltpu.VMEM(half, BF16),
            pltpu.VMEM((3, 3, 4, 16, D), BF16),
            pltpu.VMEM((3, 4, 16, D), F32),
            pltpu.VMEM((3, 4, 16, D), BF16),
            pltpu.VMEM((3, 3, 16, D), BF16),
            pltpu.VMEM((3, 16, D), F32),
            pltpu.VMEM((3, 16, D), BF16),
            pltpu.VMEM((3, 3, 16, 128), BF16),
            pltpu.SemaphoreType.DMA((SIDE, 2)),
            pltpu.SemaphoreType.DMA((SIDE, 2)),
            pltpu.SemaphoreType.DMA((6, 3, 3)),
            pltpu.SemaphoreType.DMA((6, 3, 3)),
            pltpu.SemaphoreType.DMA((2, 3)),
            pltpu.SemaphoreType.DMA((2, 3)),
        ],
        compiler_params=pltpu.CompilerParams(
            collective_id=1, has_side_effects=True, vmem_limit_bytes=38 * 2**20
        ),
        cost_estimate=cost(12 * 2**30, 2**24),
    )(*args)


def local(
    features,
    tile_vals,
    tile_row,
    tile_col,
    send_next,
    send_prev,
    cluster,
    cotangent,
    self_weight,
    neighbour_weight,
    w_coarse,
):
    lab_row, lab_col, count, most, sums_c, low_c, got_prev, got_next = front(
        send_next, send_prev, cluster, features, cotangent
    )
    rec_c = partner(low_c)
    agg, hidden, slope, sums_h = node_step(
        tile_row, tile_col, lab_row, features, got_prev, got_next, tile_vals,
        self_weight, neighbour_weight,
    )
    far_h, far_c = lax.cond(
        most[0, 0] > LOW,
        lambda h, c: (partner(h[:, LOW:]), partner(c[:, LOW:])),
        lambda h, c: (jnp.zeros((SIDE, N - LOW, D), BF16),) * 2,
        sums_h,
        sums_c,
    )
    total, output = back_step(
        count, lab_col, sums_h, sums_c, rec_c, far_h, far_c, hidden, slope, agg, features, cotangent,
        w_coarse,
    )
    scale = 1.0 / math.sqrt(SIDE * lax.axis_size("batch") * N * lax.axis_size("dom"))
    totals = total.reshape(3, D, D).astype(F32)
    return output, totals[0] * scale, totals[1] * scale, totals[2] * scale


def solution(mesh):
    in_specs = (
        P("batch", "dom", None),
        P("dom", None, None),
        P("dom"),
        P("dom"),
        P("dom"),
        P("dom"),
        P("dom"),
        P("batch", "dom", None),
        P(),
        P(),
        P(),
    )
    out_specs = (P("batch", "dom", None), P(), P(), P())
    return jax.shard_map(local, mesh=mesh, in_specs=in_specs, out_specs=out_specs, check_vma=False)
```

time: 389 us -> 135 us (0.35); the launches traced: 384 us -> 135 us
  waiting for transfers between devices: 242 us -> 1.59 us
  Pallas kernels: 0 us -> 110 us
  matrix products: 85.5 us -> 0 us
  between operations: 14.7 us -> 1.42 us
  local copies, waits for them, and re-layouts: 28.1 us -> 19.7 us
  starting transfers between devices: 7.09 us -> 0.62 us
  other arithmetic: 6.86 us -> 2.19 us
    psum x1 -> x0, waiting for transfers between devices: 153 us -> none  [local(): lax.psum((self_contribution, neighbour_contribution, term_coarse), ('dom'...]
    pallas_call x0 -> x3, Pallas kernels: none -> 110 us  [the longest x1 67.1 us: back_step(): pl.pallas_call(back_kernel, out_shape=(shape(3, 2, 4, 4, 16, D), shape(SI...]
    ppermute x4 -> x1, waiting for transfers between devices: 88.5 us -> 1.59 us  [partner(): return lax.ppermute(value, 'dom', pairs)]
    dot_general x15 -> x0, matrix products: 85.5 us -> none  [the longest x1 18.5 us: local(): jnp.einsum('tij,stjd->stid', tile_vals, picked, preferred_element_type=jn...]
    transpose x1 -> x0, local copies, waits for them, and re-layouts: 20.1 us -> none  [local(): jnp.einsum('tij,stjd->stid', tile_vals, picked, preferred_element_type=jn...]
    unnamed x39 -> x41, local copies, waits for them, and re-layouts: 6.24 us -> 16.2 us
    ppermute x4 -> x1, starting transfers between devices: 7.05 us -> 0.62 us  [partner(): return lax.ppermute(value, 'dom', pairs)]
  transfers between devices with their start and end apart: 5 -> 1, of which waited for: 5 -> 1; matrix products, arithmetic and copies ran while one was open for 6% -> 2% of each run, Pallas kernels for 0% -> 12%
where the time goes in v3:
time: 135 us
  Pallas kernels  110 us (81%)
  local copies, waits for them, and re-layouts  19.7 us (15%)
  other arithmetic  2.19 us (2%)
  waiting for transfers between devices  1.59 us (1%)
  between operations  1.42 us (1%)
    pallas_call x1, Pallas kernels, back_step(): pl.pallas_call(back_kernel, out_shape=(shape(3, 2, 4, 4, 16, D), shape(SI...  67.1 us
    pallas_call x1, Pallas kernels, front(): pl.pallas_call(front_kernel, out_shape=(shape(1, N, dtype=jnp.int32), sha...  26.6 us
    unnamed x41, local copies, waits for them, and re-layouts  16.2 us
    pallas_call x1, Pallas kernels, node_step(): pl.pallas_call(node_kernel, out_shape=(full,) * 4, in_specs=[SM, SM] + [V...  15.8 us
  transfers between devices with their start and end apart: 1, of which 1 were waited for; matrix products, arithmetic and copies ran while one was open for 2% of the time, Pallas kernels for 12%

profile of v3, /device:TPU:1, one launch (start us, length us, event | category | flops | bytes accessed | tf_op | source)
XLA Modules:
  0.0 135.0 jit_solution(656972858029354181)
XLA Ops:
  0.6 0.9 copy.15.col_ref
  1.5 0.0 copy-start
  1.6 0.7 copy-done
  2.2 0.0 copy-start.1
  2.2 1.6 %copy-done.1 = bf16[2,1024,512]{2,1,0:T(8,128)(2,1)S(1)} copy-done((bf16[2,1024,512]{2,1,0:T(8,128)(2,1)S(1)}, bf16[2,1024,512]{2,1,0:T(8,128)(2,1)}, u32[]{:S(2)}) %copy-start.1) | copy-done | bytes 2097176
  3.8 0.0 copy-start.3
  3.8 1.6 %copy-done.3 = bf16[2,1024,512]{2,1,0:T(8,128)(2,1)S(1)} copy-done((bf16[2,1024,512]{2,1,0:T(8,128)(2,1)S(1)}, bf16[2,1024,512]{2,1,0:T(8,128)(2,1)}, u32[]{:S(2)}) %copy-start.3) | copy-done | bytes 2097176
  5.4 0.0 copy-start.9
  5.4 0.7 copy-done.9
  6.1 0.0 copy-start.10
  6.1 0.7 copy-done.10
  6.7 0.0 copy-start.2
  6.7 0.0 copy-start.5
  6.7 0.0 copy-start.6
  6.7 0.0 copy-start.7
  6.7 0.0 copy-start.11
  6.8 0.0 copy-start.12
  6.8 26.6 %shard_map.138 = (s32[1,1024]{1,0:T(1,128)S(1)}, s32[1024,1]{1,0:T(8,128)S(1)}, s32[8,128]{1,0:T(8,128)S(1)}, s32[8,128]{1,0:T(8,128)S(1)}, bf16[2,1024,512]{2,1...) custom-call(s32[2]{0:T(128)S(1)} %copy-done.9, ...), custom_call_target="tpu_custom_call" | custom-call | flops 4294967296 | bytes 4194304 | tf_op jit(solution)/shard_map/pallas_call | solution.py:186
  33.4 0.0 copy-start.19
  33.4 0.6 collective-permute-start.2
  34.0 0.6 slice.21
  35.2 0.0 copy-done.2
  35.2 0.0 copy-done.5
  35.3 0.0 copy-done.6
  35.3 0.0 copy-done.7
  35.3 0.0 copy-done.11
  35.3 0.0 copy-done.12
  35.3 15.8 %shard_map.139 = (bf16[2,1024,512]{2,1,0:T(8,128)(2,1)S(1)}, bf16[2,1024,512]{2,1,0:T(8,128)(2,1)S(1)}, bf16[2,1024,512]{2,1,0:T(8,128)(2,1)S(1)}, bf16[2,1024,512]{2,1,0:T(8,128)(2,1)}) custom-call(s32[32]{0:T(128)S(1)} %copy-done.11, s32[32]{0:T(128)S(1)} %copy-done.12, s32[1,1024]{1,0:T(1,128)S(1)} %get-tuple-element.28.lab_row, ...), custom_call_target="tpu_custom_call" | custom-call | flops 10737418240 | bytes 8388608 | tf_op jit(solution)/shard_map/pallas_call | solution.py:262
  51.1 0.0 copy-start.17
  51.1 1.3 copy-done.17
  52.4 0.0 copy-start.13
  52.4 0.0 copy-start.15
  52.4 0.0 copy-start.8
  52.4 0.0 copy-done.19
  52.4 1.4 %copy-done.13 = bf16[2,1024,512]{2,1,0:T(8,128)(2,1)} copy-done((bf16[2,1024,512]{2,1,0:T(8,128)(2,1)}, bf16[2,1024,512]{2,1,0:T(8,128)(2,1)S(1)}, u32[]{:S(2)}) %copy-start.13) | copy-done | bytes 2097176
  53.8 0.6 copy-done.15
  54.4 2.0 %conditional.1 = (bf16[2,448,512]{2,1,0:T(8,128)(2,1)}, bf16[2,448,512]{2,1,0:T(8,128)(2,1)}) conditional(s32[]{:T(128)} %bitcast.3, () %tuple.16, (bf16[2,1024,512]{2,1,0:T(8,128)(2,1)}, bf16[2,1024,512]{2,1,0:T(8,128)(2,1)S(1)}) %tuple.17), branch_computations={%region_0.0_spmd, %region_1.0_spmd} | conditional | bytes 11010144 | solution.py:542
  54.4 1.0 broadcast.14.clone
  55.4 1.0 broadcast.14
  56.4 1.6 %collective-permute-done.2.rec_c = bf16[2,576,512]{2,1,0:T(8,128)(2,1)} collective-permute-done((bf16[2,576,512]{2,1,0:T(8,128)(2,1)}, bf16[2,576,512]{2,1,0:T(8,128)(2,1)}, u32[]{:S(2)}, u32[]{:S(2)}) %collective-permute-start.2) | collective-permute-done | bytes 1179680 | tf_op jit(solution)/shard_map/ppermute | solution.py:25
  58.0 0.0 copy-done.8
  58.0 0.0 copy-start.4
  58.0 1.6 %copy-done.4 = bf16[2,1024,512]{2,1,0:T(8,128)(2,1)S(1)} copy-done((bf16[2,1024,512]{2,1,0:T(8,128)(2,1)S(1)}, bf16[2,1024,512]{2,1,0:T(8,128)(2,1)}, u32[]{:S(2)}) %copy-start.4) | copy-done | bytes 2097176
  59.6 0.0 copy-start.14
  59.6 1.6 %copy-done.14 = bf16[2,1024,512]{2,1,0:T(8,128)(2,1)S(1)} copy-done((bf16[2,1024,512]{2,1,0:T(8,128)(2,1)S(1)}, bf16[2,1024,512]{2,1,0:T(8,128)(2,1)}, u32[]{:S(2)}) %copy-start.14) | copy-done | bytes 2097176
  61.1 0.0 copy-start.16
  61.1 1.6 %copy-done.16 = bf16[2,1024,512]{2,1,0:T(8,128)(2,1)S(1)} copy-done((bf16[2,1024,512]{2,1,0:T(8,128)(2,1)S(1)}, bf16[2,1024,512]{2,1,0:T(8,128)(2,1)}, u32[]{:S(2)}) %copy-start.16) | copy-done | bytes 2097176
  62.7 0.0 copy-start.18
  62.7 1.6 %copy-done.18 = bf16[2,1024,512]{2,1,0:T(8,128)(2,1)S(1)} copy-done((bf16[2,1024,512]{2,1,0:T(8,128)(2,1)S(1)}, bf16[2,1024,512]{2,1,0:T(8,128)(2,1)}, u32[]{:S(2)}) %copy-start.18) | copy-done | bytes 2097176
  64.3 67.1 %shard_map.140 = (bf16[3,2,4,4,16,512]{5,4,3,2,1,0:T(8,128)(2,1)S(1)}, bf16[2,1024,512]{2,1,0:T(8,128)(2,1)S(1)}) custom-call(s32[8,128]{1,0:T(8,128)S(1)} %get-tuple-element.26.count, s32[1024,1]{1,0:T(8,128)S(1)} %get-tuple-element.27.lab_col, bf16[2,1024,512]{2,1,0:T(8,128)(2,1)} %get-tuple-element.31.sums_h, bf16[2,1024,512]{2,1,0:T(8,128)(2,1)} %copy-done.19, ...), custom_call_target="tpu_custom_call" | custom-call | flops 12884901888 | bytes 16777216 | tf_op jit(solution)/shard_map/pallas_call | solution.py:478
  131.5 0.4 convert_element_type.12
  131.9 1.8 %slice_multiply_fusion = (f32[1,2,4,4,16,512]{5,4,3,2,1,0:T(8,128)}, f32[1,2,4,4,16,512]{5,4,3,2,1,0:T(8,128)}, f32[1,2,4,4,16,512]{5,4,3,2,1,0:T(8,128)}) fusion(f32[3,2,4,4,16,512]{5,4,3,2,1,0:T(8,128)S(1)} %convert_element_type.12), kind=kLoop, calls=%fused_computation | loop fusion | flops 786432 | bytes 6291456 | tf_op jit(solution)/shard_map/mul | solution.py:555
  133.7 1.3 copy.21
Async XLA Ops:
  1.5 0.7 copy-start
  2.2 1.6 %copy-start.1 = (bf16[2,1024,512]{2,1,0:T(8,128)(2,1)S(1)}, bf16[2,1024,512]{2,1,0:T(8,128)(2,1)}, u32[]{:S(2)}) copy-start(bf16[2,1024,512]{2,1,0:T(8,128)(2,1)} %x_ref.3) | copy-start | bytes 6291460
  3.8 1.6 %copy-start.3 = (bf16[2,1024,512]{2,1,0:T(8,128)(2,1)S(1)}, bf16[2,1024,512]{2,1,0:T(8,128)(2,1)}, u32[]{:S(2)}) copy-start(bf16[2,1024,512]{2,1,0:T(8,128)(2,1)} %ct_ref.3) | copy-start | bytes 6291460
  5.4 0.7 copy-start.9
  6.1 0.7 copy-start.10
  6.7 28.5 %copy-start.2 = (bf16[2,1024,512]{2,1,0:T(8,128)(2,1)S(1)}, bf16[2,1024,512]{2,1,0:T(8,128)(2,1)}, u32[]{:S(2)}) copy-start(bf16[2,1024,512]{2,1,0:T(8,128)(2,1)} %x_ref.3) | copy-start | bytes 6291460
  6.7 28.5 %copy-start.5 = (bf16[32,128,128]{2,1,0:T(8,128)(2,1)S(1)}, bf16[32,128,128]{2,1,0:T(8,128)(2,1)}, u32[]{:S(2)}) copy-start(bf16[32,128,128]{2,1,0:T(8,128)(2,1)} %tiles.1) | copy-start | bytes 3145732
  6.7 28.5 %copy-start.6 = (bf16[512,512]{1,0:T(8,128)(2,1)S(1)}, bf16[512,512]{1,0:T(8,128)(2,1)}, u32[]{:S(2)}) copy-start(bf16[512,512]{1,0:T(8,128)(2,1)} %w_self.1) | copy-start | bytes 1572868
  6.7 28.5 %copy-start.7 = (bf16[512,512]{1,0:T(8,128)(2,1)S(1)}, bf16[512,512]{1,0:T(8,128)(2,1)}, u32[]{:S(2)}) copy-start(bf16[512,512]{1,0:T(8,128)(2,1)} %w_neigh.1) | copy-start | bytes 1572868
  6.7 28.5 %copy-start.11 = (s32[32]{0:T(128)S(1)}, s32[32]{0:T(128)}, u32[]{:S(2)}) copy-start(s32[32]{0:T(128)} %rows.1) | copy-start | bytes 388
  6.8 28.5 %copy-start.12 = (s32[32]{0:T(128)S(1)}, s32[32]{0:T(128)}, u32[]{:S(2)}) copy-start(s32[32]{0:T(128)} %cols.1) | copy-start | bytes 388
  33.4 19.0 %copy-start.19 = (bf16[2,1024,512]{2,1,0:T(8,128)(2,1)}, bf16[2,1024,512]{2,1,0:T(8,128)(2,1)S(1)}, u32[]{:S(2)}) copy-start(bf16[2,1024,512]{2,1,0:T(8,128)(2,1)S(1)} %get-tuple-element.32.sums_c) | copy-start | bytes 6291460
  33.4 24.6 %collective-permute-start.2 = (bf16[2,576,512]{2,1,0:T(8,128)(2,1)}, bf16[2,576,512]{2,1,0:T(8,128)(2,1)}, u32[]{:S(2)}, u32[]{:S(2)}) collective-permute-start(bf16[2,576,512]{2,1,0:T(8,128)(2,1)} %get-tuple-element.33), channel_id=1, source_target_pairs={{0,2},{2,0},{4,6},{6,4},{8,10},{10,8},{12,14},{14,12},{16,18},{18,... | collective-permute-start | bytes 3538952 | tf_op jit(solution)/shard_map/ppermute | solution.py:25
  51.1 1.3 copy-start.17
  52.4 1.4 %copy-start.13 = (bf16[2,1024,512]{2,1,0:T(8,128)(2,1)}, bf16[2,1024,512]{2,1,0:T(8,128)(2,1)S(1)}, u32[]{:S(2)}) copy-start(bf16[2,1024,512]{2,1,0:T(8,128)(2,1)S(1)} %get-tuple-element.39.agg) | copy-start | bytes 6291460
  52.4 2.0 %copy-start.15 = (bf16[2,1024,512]{2,1,0:T(8,128)(2,1)}, bf16[2,1024,512]{2,1,0:T(8,128)(2,1)S(1)}, u32[]{:S(2)}) copy-start(bf16[2,1024,512]{2,1,0:T(8,128)(2,1)S(1)} %get-tuple-element.37.hidden) | copy-start | bytes 6291460
  52.4 5.6 %copy-start.8 = (bf16[512,512]{1,0:T(8,128)(2,1)S(1)}, bf16[512,512]{1,0:T(8,128)(2,1)}, u32[]{:S(2)}) copy-start(bf16[512,512]{1,0:T(8,128)(2,1)} %w_coarse.1) | copy-start | bytes 1572868
  58.0 1.6 %copy-start.4 = (bf16[2,1024,512]{2,1,0:T(8,128)(2,1)S(1)}, bf16[2,1024,512]{2,1,0:T(8,128)(2,1)}, u32[]{:S(2)}) copy-start(bf16[2,1024,512]{2,1,0:T(8,128)(2,1)} %ct_ref.3) | copy-start | bytes 6291460
  59.6 1.6 %copy-start.14 = (bf16[2,1024,512]{2,1,0:T(8,128)(2,1)S(1)}, bf16[2,1024,512]{2,1,0:T(8,128)(2,1)}, u32[]{:S(2)}) copy-start(bf16[2,1024,512]{2,1,0:T(8,128)(2,1)} %copy-done.13) | copy-start | bytes 6291460
  61.1 1.6 %copy-start.16 = (bf16[2,1024,512]{2,1,0:T(8,128)(2,1)S(1)}, bf16[2,1024,512]{2,1,0:T(8,128)(2,1)}, u32[]{:S(2)}) copy-start(bf16[2,1024,512]{2,1,0:T(8,128)(2,1)} %copy-done.15) | copy-start | bytes 6291460
  62.7 1.6 %copy-start.18 = (bf16[2,1024,512]{2,1,0:T(8,128)(2,1)S(1)}, bf16[2,1024,512]{2,1,0:T(8,128)(2,1)}, u32[]{:S(2)}) copy-start(bf16[2,1024,512]{2,1,0:T(8,128)(2,1)} %copy-done.17) | copy-start | bytes 6291460

commit v4 on v3

--- a/solution.py
+++ b/solution.py
@@ -18,6 +18,7 @@
 VM = pl.BlockSpec(memory_space=pltpu.VMEM)
 MESH = pl.DeviceIdType.MESH
 SM = pl.BlockSpec(memory_space=pltpu.SMEM)
+HB = pl.BlockSpec(memory_space=pltpu.HBM)
 
 
 def partner(value):
@@ -59,6 +60,11 @@
     def peer(self, axis, k):
         spot = (self.at[axis] + k) % 4
         return (self.dom + (spot - self.at[axis]) * (16, 4, 1)[axis], self.core), spot
+
+    def across(self, first, second, k):
+        spot, spot2 = (self.at[first] + k // 4) % 4, (self.at[second] + k % 4) % 4
+        step = (spot - self.at[first]) * (16, 4, 1)[first] + (spot2 - self.at[second]) * (16, 4, 1)[second]
+        return (self.dom + step, self.core), spot, spot2
 
 
 def remote(src, dst, send, recv, device):
@@ -76,45 +82,71 @@
     return lambda: pl.semaphore_wait(barrier, len(devices))
 
 
+def local_copy(src, dst, sem):
+    copy = pltpu.make_async_copy(src, dst, sem)
+    copy.start()
+    return copy
+
+
+def upright(row):
+    return jnp.broadcast_to(row, (128, N)).T[:, :1]
+
+
 def front_kernel(
-    nexts, prevs, row_ref, col_ref, x_ref, ct_ref,
-    lab_row, lab_col, count, most, sums, low, got_prev, got_next,
-    to_next, to_prev, table, flip, peak, peaks,
-    halo_send, halo_recv, peak_send, peak_recv,
+    nexts_in, prevs_in, row_in, x_in, ct_in,
+    lab_row, count, most, sums, low, got_prev, got_next,
+    nexts, prevs, row_ref, x_ref, ct_ref, to_next, to_prev, table, held, rank, peak, peaks,
+    load_sem, halo_send, halo_recv, peak_send, peak_recv,
 ):
     here = Place()
     nxt = ((here.dom + 1) % 64, here.core)
     prv = ((here.dom + 63) % 64, here.core)
+    loads = [
+        local_copy(src, dst, load_sem.at[i])
+        for i, (src, dst) in enumerate(
+            ((nexts_in, nexts), (prevs_in, prevs), (x_in, x_ref), (row_in, row_ref), (ct_in, ct_ref))
+        )
+    ]
     wait = greet([nxt, prv] + [here.peer(a, k)[0] for a in range(3) for k in (1, 2, 3)])
-    for s in range(SIDE):
+    for copy in loads[:3]:
+        copy.wait()
+    halo = []
+
+    def take(s):
         for j in range(2):
             to_next[s, j] = x_ref[s, nexts[j]]
             to_prev[s, j] = x_ref[s, prevs[j]]
-    wait()
-    halo = []
-    for s in range(SIDE):
+
+    def ship(s):
         halo.append(remote(to_next.at[s], got_prev.at[s], halo_send.at[0, s], halo_recv.at[0, s], nxt))
         halo.append(remote(to_prev.at[s], got_next.at[s], halo_send.at[1, s], halo_recv.at[1, s], prv))
 
-    row, col = row_ref[...], col_ref[...]
-    step = 256
-
-    def tables(i, carry):
-        at = pl.ds(pl.multiple_of(i * step, step), step)
-        down = lax.broadcasted_iota(jnp.int32, (step, N), 0) + i * step
-        across = lax.broadcasted_iota(jnp.int32, (step, N), 1)
-        table[at, :] = (row == down).astype(F32).astype(BF16)
-        flip[at, :] = (col_ref[at, :] == across).astype(F32).astype(BF16)
+    take(0)
+    wait()
+    ship(0)
+    take(1)
+    ship(1)
+    loads[3].wait()
+    row = row_ref[...]
+    step = 128
+    blocks = N // step
+
+    def span(i):
+        return pl.ds(pl.multiple_of(i * step, step), step)
+
+    def downs(i):
+        return lax.broadcasted_iota(jnp.int32, (step, N), 0) + i * step
+
+    def wide(value):
+        return jnp.broadcast_to(jnp.sum(value, axis=1, keepdims=True), (step, 128))
+
+    def holding(i, carry):
+        held[span(i), :] = wide(jnp.where(row == downs(i), 1.0, 0.0))
         return carry
 
-    lax.fori_loop(0, N // step, tables, 0)
-    held_row = dot(jnp.ones((16, N), BF16), flip[...])
-    held_col = dot(table[...], jnp.ones((N, 128), BF16))
-
-    def ones_of(held, value):
-        return (held == value).astype(F32)
-
-    total = jnp.sum(ones_of(held_row[:1], 1.0), axis=1, keepdims=True)
+    lax.fori_loop(0, blocks, holding, 0)
+    held_row = held[...].T[:1]
+    total = jnp.sum(jnp.where(held_row == 1.0, 1.0, 0.0), axis=1, keepdims=True)
     count[...] = jnp.broadcast_to(total, (8, 128)).astype(jnp.int32)
     peak[0] = jnp.broadcast_to(total, (8, 128))
 
@@ -133,31 +165,33 @@
         return top
 
     first = spread(0)
-    row_in = jnp.concatenate([ones_of(held_row, 1.0), ones_of(held_row, 2.0)], axis=0).astype(BF16)
-    col_in = jnp.concatenate([ones_of(held_col, 1.0), ones_of(held_col, 2.0)], axis=1).astype(BF16)
-
-    def before(i, carry):
-        at = pl.ds(pl.multiple_of(i * step, step), step)
-        down = lax.broadcasted_iota(jnp.int32, (step, N), 0) + i * step
+    both = jnp.where(held_row == 1.0, 1.0, jnp.where(held_row == 2.0, 2048.0, 0.0))
+
+    def ranking(i, carry):
         across = lax.broadcasted_iota(jnp.int32, (step, N), 1)
-        table[at, :] = (across < down).astype(F32).astype(BF16)
-        flip[at, :] = (down < across).astype(F32).astype(BF16)
+        rank[span(i), :] = wide(jnp.where(across < downs(i), both, 0.0))
         return carry
 
-    lax.fori_loop(0, N // step, before, 0)
-    row_rank = dot(row_in, flip[...])
-    col_rank = dot(table[...], col_in)
-    new_row = jnp.where(held_row[:1] == 1.0, row_rank[:1], total + row_rank[16:17])
-    new_col = jnp.where(held_col[:, :1] == 1.0, col_rank[:, :1], total + col_rank[:, 128:129])
-    across = lax.broadcasted_iota(jnp.int32, (N, N), 1)
-    down = lax.broadcasted_iota(jnp.int32, (N, N), 0)
-    col_lab = jnp.sum(jnp.where(col == across, new_row, 0.0), axis=1, keepdims=True)
-    row_lab = jnp.sum(jnp.where(row == down, new_col, 0.0), axis=0, keepdims=True)
-    lab_col[...] = col_lab.astype(jnp.int32)
-    lab_row[...] = row_lab.astype(jnp.int32)
+    lax.fori_loop(0, blocks, ranking, 0)
+    ranks = rank[:, :1].astype(jnp.int32)
+    whole = total.astype(jnp.int32) + (ranks >> 11)
+    rank[...] = jnp.broadcast_to(jnp.where(held[:, :1] == 1.0, ranks & 2047, whole), (N, 128)).astype(F32)
+
+    def naming(i, carry):
+        mine = jnp.where(row == downs(i), rank[span(i), :1], 0.0)
+        return carry + jnp.sum(mine, axis=0, keepdims=True)
+
+    label = lax.fori_loop(0, blocks, naming, jnp.zeros((1, N), F32)).astype(jnp.int32)
+    lab_row[...] = label
+
+    def one_hot(i, carry):
+        table[span(i), :] = (label == downs(i)).astype(F32).astype(BF16)
+        return carry
+
+    lax.fori_loop(0, blocks, one_hot, 0)
     peak[1] = settle(0, first)
     second = spread(1)
-    table[...] = (row_lab.astype(jnp.int32) == down).astype(F32).astype(BF16)
+    loads[4].wait()
 
     def pool(s):
         got = dot(table[...], ct_ref[s]).astype(BF16)
@@ -187,7 +221,6 @@
         front_kernel,
         out_shape=(
             shape(1, N, dtype=jnp.int32),
-            shape(N, 1, dtype=jnp.int32),
             shape(8, 128, dtype=jnp.int32),
             shape(8, 128, dtype=jnp.int32),
             shape(SIDE, N, D),
@@ -195,15 +228,22 @@
             shape(*halo),
             shape(*halo),
         ),
-        in_specs=[SM, SM] + [VM] * 4,
-        out_specs=(VM,) * 8,
+        in_specs=[HB] * 5,
+        out_specs=(VM,) * 7,
         scratch_shapes=[
+            pltpu.SMEM((2,), jnp.int32),
+            pltpu.SMEM((2,), jnp.int32),
+            pltpu.VMEM((1, N), jnp.int32),
+            pltpu.VMEM((SIDE, NB, BLK, D), BF16),
+            pltpu.VMEM((SIDE, N, D), BF16),
             pltpu.VMEM(halo, BF16),
             pltpu.VMEM(halo, BF16),
             pltpu.VMEM((N, N), BF16),
-            pltpu.VMEM((N, N), BF16),
+            pltpu.VMEM((N, 128), F32),
+            pltpu.VMEM((N, 128), F32),
             pltpu.VMEM((3, 8, 128), F32),
             pltpu.VMEM((3, 3, 8, 128), F32),
+            pltpu.SemaphoreType.DMA((5,)),
             pltpu.SemaphoreType.DMA((2, SIDE)),
             pltpu.SemaphoreType.DMA((2, SIDE)),
             pltpu.SemaphoreType.DMA((3, 3)),
@@ -213,10 +253,7 @@
             collective_id=0, has_side_effects=True, vmem_limit_bytes=28 * 2**20
         ),
         cost_estimate=cost(4 * 2**30, 2**22),
-    )(
-        send_next, send_prev, cluster.reshape(1, N), cluster.reshape(N, 1),
-        features.reshape(SIDE, NB, BLK, D), cotangent,
-    )
+    )(send_next, send_prev, cluster.reshape(1, N), features.reshape(SIDE, NB, BLK, D), cotangent)
 
 
 def node_kernel(
@@ -280,11 +317,13 @@
 
 
 def back_kernel(
-    count, lab_col, sums_h, sums_c, rec_c, far_h, far_c, hidden, slope, agg, x_ref, ct_ref, w_coarse,
+    count, lab_row, w_coarse, sums_h_in, sums_c_in, rec_c_in, far_h_in, far_c_in, x_in, agg_in,
+    ct_in, slope_in, hidden_in,
     total, out,
+    sums_h, sums_c, rec_c, far_h, far_c, x_ref, agg, ct_ref, slope, hidden, load_sem,
     rec_h, flip, lifted, down, coarse, weighed, x_turn, a_turn, w_turn, grad_pre, part, grads,
-    send0, recv0, acc, buf1, recv1, sum2, buf2, recv2, sum3, buf3, recv3,
-    swap_send, swap_recv, send_sem, recv_sem, side_send, side_recv,
+    send0, recv0, acc, buf1, recv1, sum2, buf2, recv2,
+    swap_send, swap_recv, send_sem, recv_sem, plane_send, plane_recv, side_send, side_recv,
 ):
     here = Place()
     core = here.core
@@ -292,24 +331,28 @@
     pair = (here.dom + 1 - 2 * (here.dom % 2), core)
     wait = greet([other, pair] + [here.peer(a, k)[0] for a in range(3) for k in (1, 2, 3)])
     wait()
-    swaps = []
+    swaps, loads = [], []
     for s in range(SIDE):
         for i, (lo, hi) in enumerate((MID, (LAST[0], LOW))):
             rows = pl.ds(lo, hi - lo)
             swaps.append(
-                remote(sums_h.at[s, rows], rec_h.at[s, rows], swap_send.at[s, i], swap_recv.at[s, i], pair)
+                remote(sums_h_in.at[s, rows], rec_h.at[s, rows], swap_send.at[s, i], swap_recv.at[s, i], pair)
             )
 
-    step = 256
-
-    def one_hot(i, carry):
-        at = pl.ds(pl.multiple_of(i * step, step), step)
-        across = lax.broadcasted_iota(jnp.int32, (step, N), 1)
-        flip[at, :] = (lab_col[at, :] == across).astype(F32).astype(BF16)
-        return carry
-
-    lax.fori_loop(0, N // step, one_hot, 0)
+    for i, (src, dst) in enumerate(
+        (
+            (sums_h_in, sums_h), (sums_c_in, sums_c), (far_h_in, far_h), (far_c_in, far_c), (rec_c_in, rec_c),
+            (x_in, x_ref), (agg_in, agg), (ct_in, ct_ref), (slope_in, slope), (hidden_in, hidden),
+        )
+    ):
+        loads.append(local_copy(src, dst, load_sem.at[i]))
+    label = upright(lab_row[...].astype(F32)).astype(jnp.int32)
+    across = lax.broadcasted_iota(jnp.int32, (128, N), 1)
+    for i in range(0, N, 128):
+        flip[i : i + 128, :] = (label[i : i + 128] == across).astype(F32).astype(BF16)
     w_turn[...] = w_coarse[...].T
+    for copy in loads[:5]:
+        copy.wait()
 
     def level(s, span):
         lo, hi = span
@@ -351,6 +394,9 @@
 
     for s in range(SIDE):
         level(s, EARLY)
+    for copy in loads[5:]:
+        copy.wait()
+    for s in range(SIDE):
         x_turn[s] = x_ref[s].T
         a_turn[s] = agg[s].T
 
@@ -387,34 +433,13 @@
     store(1, load(1) + dot(a_turn[1], grad_pre[...]))
     hand(1)
 
-    def scatter(p, phase, pick, landing):
-        copies = []
-        for k in (1, 2, 3):
-            device, spot = here.peer(ORDERS[p][phase], k)
-            copies.append(
-                remote(
-                    pick(spot), landing.at[p, k - 1], send_sem.at[phase, p, k - 1],
-                    recv_sem.at[phase, p, k - 1], device,
-                )
-            )
-        return copies
-
-    def gather(p, phase, piece):
-        return [
-            remote(
-                piece, piece, send_sem.at[5 - phase, p, k - 1], recv_sem.at[5 - phase, p, k - 1],
-                here.peer(ORDERS[p][phase], k)[0],
-            )
-            for k in (1, 2, 3)
-        ]
-
-    def mine(p, phase):
-        return here.at[ORDERS[p][phase]]
+    def mine(p):
+        return [here.at[axis] for axis in ORDERS[p]]
 
     def cols(spot):
         return pl.ds(pl.multiple_of(spot * 128, 128), 128)
 
-    stages = [[None] * 3 for _ in range(6)]
+    stages = [[None] * 3 for _ in range(4)]
 
     def arrived(stage, p):
         for copy in stages[stage][p]:
@@ -425,43 +450,57 @@
         value = grads[p, core] + recv0[p].astype(F32)
         acc[p] = value
         buf1[p] = value.astype(BF16)
-        stages[0][p] = scatter(p, 0, lambda spot: buf1.at[p, spot], recv1)
+        stages[0][p] = []
+        for k in (1, 2, 3):
+            device, spot = here.peer(ORDERS[p][0], k)
+            stages[0][p].append(
+                remote(buf1.at[p, spot], recv1.at[p, k - 1], send_sem.at[0, p, k - 1], recv_sem.at[0, p, k - 1], device)
+            )
     emit(1, 0, 512)
     for p in ENTRY:
         arrived(0, p)
-        value = acc[p, mine(p, 0)]
+        value = acc[p, mine(p)[0]]
         for k in range(3):
             value = value + recv1[p, k].astype(F32)
         sum2[p] = value
         buf2[p] = value.astype(BF16)
-        stages[1][p] = scatter(p, 1, lambda spot: buf2.at[p, spot], recv2)
-    emit(1, 512, 768)
+    for p in ENTRY:
+        stages[1][p] = []
+        for k in range(1, 16):
+            device, spot, spot2 = here.across(ORDERS[p][1], ORDERS[p][2], k)
+            stages[1][p].append(
+                remote(
+                    buf2.at[p, spot, :, cols(spot2)], recv2.at[p, k - 1],
+                    plane_send.at[0, p, k - 1], plane_recv.at[0, p, k - 1], device,
+                )
+            )
+    emit(1, 512, 1024)
     for p in ENTRY:
         arrived(1, p)
-        value = sum2[p, mine(p, 1)]
-        for k in range(3):
+        one, two, three = mine(p)
+        value = sum2[p, two, :, cols(three)]
+        for k in range(15):
             value = value + recv2[p, k].astype(F32)
-        sum3[p] = value
-        buf3[p] = value.astype(BF16)
-        stages[2][p] = scatter(p, 2, lambda spot: buf3.at[p, :, cols(spot)], recv3)
-    emit(1, 768, 1024)
+        piece = total.at[p, core, one, two, :, cols(three)]
+        piece[...] = value.astype(BF16)
+        stages[2][p] = []
+        for k in range(1, 16):
+            device, _, _ = here.across(ORDERS[p][1], ORDERS[p][2], k)
+            stages[2][p].append(
+                remote(piece, piece, plane_send.at[1, p, k - 1], plane_recv.at[1, p, k - 1], device)
+            )
     for p in ENTRY:
         arrived(2, p)
-        value = sum3[p, :, cols(mine(p, 2))]
-        for k in range(3):
-            value = value + recv3[p, k].astype(F32)
-        piece = total.at[p, core, mine(p, 0), mine(p, 1), :, cols(mine(p, 2))]
-        piece[...] = value.astype(BF16)
-        stages[3][p] = gather(p, 2, piece)
+        piece = total.at[p, core, mine(p)[0]]
+        stages[3][p] = []
+        for k in (1, 2, 3):
+            device, _ = here.peer(ORDERS[p][0], k)
+            stages[3][p].append(
+                remote(piece, piece, send_sem.at[1, p, k - 1], recv_sem.at[1, p, k - 1], device)
+            )
+    last = []
     for p in ENTRY:
         arrived(3, p)
-        stages[4][p] = gather(p, 1, total.at[p, core, mine(p, 0), mine(p, 1)])
-    for p in ENTRY:
-        arrived(4, p)
-        stages[5][p] = gather(p, 0, total.at[p, core, mine(p, 0)])
-    last = []
-    for p in ENTRY:
-        arrived(5, p)
         last.append(remote(total.at[p, core], total.at[p, core], side_send.at[1, p], side_recv.at[1, p], other))
     for copy in last:
         copy.wait_recv()
@@ -478,9 +517,20 @@
     return pl.pallas_call(
         back_kernel,
         out_shape=(shape(3, 2, 4, 4, 16, D), shape(SIDE, N, D)),
-        in_specs=[VM] * len(args),
+        in_specs=[VM] * 3 + [HB] * (len(args) - 3),
         out_specs=(VM, VM),
         scratch_shapes=[
+            pltpu.VMEM((SIDE, N, D), BF16),
+            pltpu.VMEM((SIDE, N, D), BF16),
+            pltpu.VMEM((SIDE, LOW, D), BF16),
+            pltpu.VMEM((SIDE, N - LOW, D), BF16),
+            pltpu.VMEM((SIDE, N - LOW, D), BF16),
+            pltpu.VMEM((SIDE, N, D), BF16),
+            pltpu.VMEM((SIDE, N, D), BF16),
+            pltpu.VMEM((SIDE, N, D), BF16),
+            pltpu.VMEM((SIDE, N, D), BF16),
+            pltpu.VMEM((SIDE, N, D), BF16),
+            pltpu.SemaphoreType.DMA((10,)),
             pltpu.VMEM((SIDE, LOW, D), BF16),
             pltpu.VMEM((N, N), BF16),
             pltpu.VMEM((SIDE, N, D), BF16),
@@ -500,19 +550,18 @@
             pltpu.VMEM((3, 3, 4, 16, D), BF16),
             pltpu.VMEM((3, 4, 16, D), F32),
             pltpu.VMEM((3, 4, 16, D), BF16),
-            pltpu.VMEM((3, 3, 16, D), BF16),
-            pltpu.VMEM((3, 16, D), F32),
-            pltpu.VMEM((3, 16, D), BF16),
-            pltpu.VMEM((3, 3, 16, 128), BF16),
+            pltpu.VMEM((3, 15, 16, 128), BF16),
             pltpu.SemaphoreType.DMA((SIDE, 2)),
             pltpu.SemaphoreType.DMA((SIDE, 2)),
-            pltpu.SemaphoreType.DMA((6, 3, 3)),
-            pltpu.SemaphoreType.DMA((6, 3, 3)),
+            pltpu.SemaphoreType.DMA((2, 3, 3)),
+            pltpu.SemaphoreType.DMA((2, 3, 3)),
+            pltpu.SemaphoreType.DMA((2, 3, 15)),
+            pltpu.SemaphoreType.DMA((2, 3, 15)),
             pltpu.SemaphoreType.DMA((2, 3)),
             pltpu.SemaphoreType.DMA((2, 3)),
         ],
         compiler_params=pltpu.CompilerParams(
-            collective_id=1, has_side_effects=True, vmem_limit_bytes=38 * 2**20
+            collective_id=1, has_side_effects=True, vmem_limit_bytes=56 * 2**20
         ),
         cost_estimate=cost(12 * 2**30, 2**24),
     )(*args)
@@ -531,7 +580,7 @@
     neighbour_weight,
     w_coarse,
 ):
-    lab_row, lab_col, count, most, sums_c, low_c, got_prev, got_next = front(
+    lab_row, count, most, sums_c, low_c, got_prev, got_next = front(
         send_next, send_prev, cluster, features, cotangent
     )
     rec_c = partner(low_c)
@@ -547,12 +596,11 @@
         sums_c,
     )
     total, output = back_step(
-        count, lab_col, sums_h, sums_c, rec_c, far_h, far_c, hidden, slope, agg, features, cotangent,
-        w_coarse,
+        count, lab_row, w_coarse, sums_h, sums_c, rec_c, far_h, far_c, features, agg, cotangent, slope,
+        hidden,
     )
     scale = 1.0 / math.sqrt(SIDE * lax.axis_size("batch") * N * lax.axis_size("dom"))
-    totals = total.reshape(3, D, D).astype(F32)
-    return output, totals[0] * scale, totals[1] * scale, totals[2] * scale
+    return (output,) + tuple(total[p].reshape(D, D).astype(F32) * scale for p in range(3))
 
 
 def solution(mesh):

time: 135 us -> 125 us (0.926)
  local copies, waits for them, and re-layouts: 19.7 us -> 12.3 us
  Pallas kernels: 110 us -> 106 us
    unnamed x41 -> x35, local copies, waits for them, and re-layouts: 16.2 us -> 9.81 us
    pallas_call x1, Pallas kernels: 67.1 us -> 64.6 us  [back_step(): pl.pallas_call(back_kernel, out_shape=(shape(3, 2, 4, 4, 16, D), shape(SI...]
    mul x1, other arithmetic: 1.76 us -> 3.31 us  [local(): total[p].reshape(D, D).astype(F32) * scale]
  transfers between devices with their start and end apart: 1 -> 1, of which waited for: 1 -> 1; matrix products, arithmetic and copies ran while one was open for 2% -> 2% of each run, Pallas kernels for 12% -> 13%
where the time goes in v4:
time: 125 us
  Pallas kernels  106 us (85%)
  local copies, waits for them, and re-layouts  12.3 us (10%)
  other arithmetic  3.31 us (3%)
  waiting for transfers between devices  1.55 us (1%)
  between operations  1.42 us (1%)
    pallas_call x1, Pallas kernels, back_step(): pl.pallas_call(back_kernel, out_shape=(shape(3, 2, 4, 4, 16, D), shape(SI...  64.6 us
    pallas_call x1, Pallas kernels, front(): pl.pallas_call(front_kernel, out_shape=(shape(1, N, dtype=jnp.int32), sha...  25.4 us
    pallas_call x1, Pallas kernels, node_step(): pl.pallas_call(node_kernel, out_shape=(full,) * 4, in_specs=[SM, SM] + [V...  15.7 us
    unnamed x35, local copies, waits for them, and re-layouts  9.81 us
    mul x1, other arithmetic, local(): total[p].reshape(D, D).astype(F32) * scale  3.31 us
  transfers between devices with their start and end apart: 1, of which 1 were waited for; matrix products, arithmetic and copies ran while one was open for 2% of the time, Pallas kernels for 13%

profile of v4, /device:TPU:1, one launch (start us, length us, event | category | flops | bytes accessed | tf_op | source)
XLA Modules:
  0.0 124.9 jit_solution(3354010242803065668)
XLA Ops:
  0.6 0.0 copy-start
  0.6 1.6 %copy-done = bf16[2,1024,512]{2,1,0:T(8,128)(2,1)S(1)} copy-done((bf16[2,1024,512]{2,1,0:T(8,128)(2,1)S(1)}, bf16[2,1024,512]{2,1,0:T(8,128)(2,1)}, u32[]{:S(2)}) %copy-start) | copy-done | bytes 2097176
  2.2 0.0 copy-start.2
  2.2 1.6 %copy-done.2 = bf16[2,1024,512]{2,1,0:T(8,128)(2,1)S(1)} copy-done((bf16[2,1024,512]{2,1,0:T(8,128)(2,1)S(1)}, bf16[2,1024,512]{2,1,0:T(8,128)(2,1)}, u32[]{:S(2)}) %copy-start.2) | copy-done | bytes 2097176
  3.8 0.0 copy-start.6
  3.8 0.7 copy-done.6
  4.5 0.0 copy-start.7
  4.5 0.7 copy-done.7
  5.2 0.0 copy-start.8
  5.2 0.7 copy-done.8
  5.8 0.0 copy-start.1
  5.8 0.0 copy-start.3
  5.8 0.0 copy-start.4
  5.8 0.0 copy-start.5
  5.8 0.0 copy-start.9
  5.8 0.0 copy-start.10
  5.8 25.4 %shard_map.138 = (s32[1,1024]{1,0:T(1,128)S(1)}, s32[8,128]{1,0:T(8,128)S(1)}, s32[8,128]{1,0:T(8,128)S(1)}, bf16[2,1024,512]{2,1,0:T(8,128)(2,1)S(1)}, bf16[2,5...) custom-call(s32[2]{0:T(128)S(1)} %copy-done.7, ...), custom_call_target="tpu_custom_call" | custom-call | flops 4294967296 | bytes 4194304 | tf_op jit(solution)/shard_map/pallas_call | solution.py:220
  31.2 0.0 copy-start.14
  31.2 0.0 copy-start.15
  31.2 0.6 collective-permute-start.2
  31.9 0.5 slice.18
  33.0 0.0 copy-done.1
  33.0 0.0 copy-done.3
  33.0 0.0 copy-done.4
  33.1 0.0 copy-done.5
  33.1 0.0 copy-done.9
  33.1 0.0 copy-done.10
  33.1 15.7 %shard_map.139 = (bf16[2,1024,512]{2,1,0:T(8,128)(2,1)S(1)}, bf16[2,1024,512]{2,1,0:T(8,128)(2,1)S(1)}, bf16[2,1024,512]{2,1,0:T(8,128)(2,1)S(1)}, bf16[2,1024,512]{2,1,0:T(8,128)(2,1)}) custom-call(s32[32]{0:T(128)S(1)} %copy-done.9, s32[32]{0:T(128)S(1)} %copy-done.10, s32[1,1024]{1,0:T(1,128)S(1)} %get-tuple-element.26.lab_row, ...), custom_call_target="tpu_custom_call" | custom-call | flops 10737418240 | bytes 8388608 | tf_op jit(solution)/shard_map/pallas_call | solution.py:299
  48.7 0.0 copy-done.14
  48.7 0.0 copy-done.15
  48.7 0.0 copy-start.13
  48.8 1.3 %copy-done.13 = bf16[2,1024,512]{2,1,0:T(8,128)(2,1)} copy-done((bf16[2,1024,512]{2,1,0:T(8,128)(2,1)}, bf16[2,1024,512]{2,1,0:T(8,128)(2,1)S(1)}, u32[]{:S(2)}) %copy-start.13) | copy-done | bytes 2097176
  50.1 0.0 copy-start.11
  50.1 0.0 copy-start.12
  50.1 1.3 %copy-done.11 = bf16[2,1024,512]{2,1,0:T(8,128)(2,1)} copy-done((bf16[2,1024,512]{2,1,0:T(8,128)(2,1)}, bf16[2,1024,512]{2,1,0:T(8,128)(2,1)S(1)}, u32[]{:S(2)}) %copy-start.11) | copy-done | bytes 2097176
  51.4 0.6 copy-done.12
  52.0 2.0 %conditional.1 = (bf16[2,448,512]{2,1,0:T(8,128)(2,1)}, bf16[2,448,512]{2,1,0:T(8,128)(2,1)}) conditional(s32[]{:T(128)} %bitcast.2, () %tuple.16, (bf16[2,1024,512]{2,1,0:T(8,128)(2,1)}, bf16[2,1024,512]{2,1,0:T(8,128)(2,1)S(1)}) %tuple.17), branch_computations={%region_0.0_spmd, %region_1.0_spmd} | conditional | bytes 11010144 | solution.py:591
  52.0 1.0 broadcast.8.clone
  53.1 1.0 broadcast.8
  54.1 1.5 %collective-permute-done.2.rec_c_in = bf16[2,576,512]{2,1,0:T(8,128)(2,1)} collective-permute-done((bf16[2,576,512]{2,1,0:T(8,128)(2,1)S(1)}, bf16[2,576,512]{2,1,0:T(8,128)(2,1)}, u32[]{:S(2)}, u32[]{:S(2)}) %collective-permute-start.2) | collective-permute-done | bytes 1179680 | tf_op jit(solution)/shard_map/ppermute | solution.py:26
  55.6 64.6 %shard_map.140 = (bf16[3,2,4,4,16,512]{5,4,3,2,1,0:T(8,128)(2,1)}, bf16[2,1024,512]{2,1,0:T(8,128)(2,1)}) custom-call(s32[8,128]{1,0:T(8,128)} %copy-done.15, s32[1,1024]{1,0:T(1,128)} %copy-done.14, bf16[512,512]{1,0:T(8,128)(2,1)} %w_coarse.1, bf16[2,1024,512]{2,1,0:T(8,128)(2,1)} %get-tuple-element.29.sums_h_in, ...), custom_call_target="tpu_custom_call" | custom-call | flops 12884901888 | bytes 16777216 | tf_op jit(solution)/shard_map/pallas_call | solution.py:517
  120.2 0.0 copy-start.16
  120.2 3.3 %convert_multiply_fusion = (f32[1,2,4,4,16,512]{5,4,3,2,1,0:T(8,128)}, f32[1,2,4,4,16,512]{5,4,3,2,1,0:T(8,128)}, f32[1,2,4,4,16,512]{5,4,3,2,1,0:T(8,128)}) fusion(bf16[3,2,4,4,16,512]{5,4,3,2,1,0:T(8,128)(2,1)} %get-tuple-element.39), kind=kLoop, calls=%fused_computation | loop fusion | flops 1572864 | bytes 4718592 | tf_op jit(solution)/shard_map/mul | solution.py:603
  123.5 0.0 copy-done.16
  123.5 1.3 %copy.20 = bf16[2,1024,512]{2,1,0:T(8,128)(2,1)} copy(bf16[2,1024,512]{2,1,0:T(8,128)(2,1)S(1)} %copy-done.16) | data formatting | bytes 4194304
Async XLA Ops:
  0.6 1.6 %copy-start = (bf16[2,1024,512]{2,1,0:T(8,128)(2,1)S(1)}, bf16[2,1024,512]{2,1,0:T(8,128)(2,1)}, u32[]{:S(2)}) copy-start(bf16[2,1024,512]{2,1,0:T(8,128)(2,1)} %x_in.1) | copy-start | bytes 6291460
  2.2 1.6 %copy-start.2 = (bf16[2,1024,512]{2,1,0:T(8,128)(2,1)S(1)}, bf16[2,1024,512]{2,1,0:T(8,128)(2,1)}, u32[]{:S(2)}) copy-start(bf16[2,1024,512]{2,1,0:T(8,128)(2,1)} %ct_in.3) | copy-start | bytes 6291460
  3.8 0.7 copy-start.6
  4.5 0.7 copy-start.7
  5.2 0.7 copy-start.8
  5.8 27.2 %copy-start.1 = (bf16[2,1024,512]{2,1,0:T(8,128)(2,1)S(1)}, bf16[2,1024,512]{2,1,0:T(8,128)(2,1)}, u32[]{:S(2)}) copy-start(bf16[2,1024,512]{2,1,0:T(8,128)(2,1)} %x_in.1) | copy-start | bytes 6291460
  5.8 27.2 %copy-start.3 = (bf16[32,128,128]{2,1,0:T(8,128)(2,1)S(1)}, bf16[32,128,128]{2,1,0:T(8,128)(2,1)}, u32[]{:S(2)}) copy-start(bf16[32,128,128]{2,1,0:T(8,128)(2,1)} %tiles.1) | copy-start | bytes 3145732
  5.8 27.2 %copy-start.4 = (bf16[512,512]{1,0:T(8,128)(2,1)S(1)}, bf16[512,512]{1,0:T(8,128)(2,1)}, u32[]{:S(2)}) copy-start(bf16[512,512]{1,0:T(8,128)(2,1)} %w_self.1) | copy-start | bytes 1572868
  5.8 27.2 %copy-start.5 = (bf16[512,512]{1,0:T(8,128)(2,1)S(1)}, bf16[512,512]{1,0:T(8,128)(2,1)}, u32[]{:S(2)}) copy-start(bf16[512,512]{1,0:T(8,128)(2,1)} %w_neigh.1) | copy-start | bytes 1572868
  5.8 27.2 %copy-start.9 = (s32[32]{0:T(128)S(1)}, s32[32]{0:T(128)}, u32[]{:S(2)}) copy-start(s32[32]{0:T(128)} %rows.1) | copy-start | bytes 388
  5.8 27.2 %copy-start.10 = (s32[32]{0:T(128)S(1)}, s32[32]{0:T(128)}, u32[]{:S(2)}) copy-start(s32[32]{0:T(128)} %cols.1) | copy-start | bytes 388
  31.2 17.5 %copy-start.14 = (s32[1,1024]{1,0:T(1,128)}, s32[1,1024]{1,0:T(1,128)S(1)}, u32[]{:S(2)}) copy-start(s32[1,1024]{1,0:T(1,128)S(1)} %get-tuple-element.26.lab_row) | copy-start | bytes 12292
  31.2 17.5 %copy-start.15 = (s32[8,128]{1,0:T(8,128)}, s32[8,128]{1,0:T(8,128)S(1)}, u32[]{:S(2)}) copy-start(s32[8,128]{1,0:T(8,128)S(1)} %get-tuple-element.25.count) | copy-start | bytes 12292
  31.2 24.4 %collective-permute-start.2 = (bf16[2,576,512]{2,1,0:T(8,128)(2,1)S(1)}, bf16[2,576,512]{2,1,0:T(8,128)(2,1)}, u32[]{:S(2)}, u32[]{:S(2)}) collective-permute-start(bf16[2,576,512]{2,1,0:T(8,128)(2,1)S(1)} %get-tuple-element.31), channel_id=1, source_target_pairs={{0,2},{2,0},{4,6},{6,4},{8,10},{10,8},{12,14},{14,12},{16,18},{18,... | collective-permute-start | bytes 3538952 | tf_op jit(solution)/shard_map/ppermute | solution.py:26
  48.7 1.3 %copy-start.13 = (bf16[2,1024,512]{2,1,0:T(8,128)(2,1)}, bf16[2,1024,512]{2,1,0:T(8,128)(2,1)S(1)}, u32[]{:S(2)}) copy-start(bf16[2,1024,512]{2,1,0:T(8,128)(2,1)S(1)} %get-tuple-element.36.slope_in) | copy-start | bytes 6291460
  50.1 1.3 %copy-start.11 = (bf16[2,1024,512]{2,1,0:T(8,128)(2,1)}, bf16[2,1024,512]{2,1,0:T(8,128)(2,1)S(1)}, u32[]{:S(2)}) copy-start(bf16[2,1024,512]{2,1,0:T(8,128)(2,1)S(1)} %get-tuple-element.35.agg_in) | copy-start | bytes 6291460
  50.1 2.0 %copy-start.12 = (bf16[2,1024,512]{2,1,0:T(8,128)(2,1)}, bf16[2,1024,512]{2,1,0:T(8,128)(2,1)S(1)}, u32[]{:S(2)}) copy-start(bf16[2,1024,512]{2,1,0:T(8,128)(2,1)S(1)} %get-tuple-element.37.hidden_in) | copy-start | bytes 6291460
  120.2 3.3 %copy-start.16 = (bf16[2,1024,512]{2,1,0:T(8,128)(2,1)S(1)}, bf16[2,1024,512]{2,1,0:T(8,128)(2,1)}, u32[]{:S(2)}) copy-start(bf16[2,1024,512]{2,1,0:T(8,128)(2,1)} %get-tuple-element.51) | copy-start | bytes 6291460

commit v5 on v4

--- a/solution.py
+++ b/solution.py
@@ -1,3 +1,4 @@
+import functools
 import math
 
 import jax
@@ -13,12 +14,13 @@
 NB = 8
 SIDE = 2
 LOW = 576
+HEAD = 160
 F32 = jnp.float32
 BF16 = jnp.bfloat16
 VM = pl.BlockSpec(memory_space=pltpu.VMEM)
 MESH = pl.DeviceIdType.MESH
 SM = pl.BlockSpec(memory_space=pltpu.SMEM)
-HB = pl.BlockSpec(memory_space=pltpu.HBM)
+HB = pl.BlockSpec(memory_space=pl.ANY)
 
 
 def partner(value):
@@ -45,6 +47,10 @@
 
 def shape(*dims, dtype=BF16):
     return jax.ShapeDtypeStruct(dims, dtype)
+
+
+def in_hbm(value):
+    return pltpu.with_memory_space_constraint(value, pltpu.HBM)
 
 
 def cost(flops, size):
@@ -94,11 +100,12 @@
 
 def front_kernel(
     nexts_in, prevs_in, row_in, x_in, ct_in,
-    lab_row, count, most, sums, low, got_prev, got_next,
+    lab_row, count, most, sums, low, head, got_prev, got_next,
     nexts, prevs, row_ref, x_ref, ct_ref, to_next, to_prev, table, held, rank, peak, peaks,
-    load_sem, halo_send, halo_recv, peak_send, peak_recv,
+    load_sem, halo_send, halo_recv, peak_send, peak_recv, head_send, head_recv,
 ):
     here = Place()
+    pair = (here.dom + 1 - 2 * (here.dom % 2), here.core)
     nxt = ((here.dom + 1) % 64, here.core)
     prv = ((here.dom + 63) % 64, here.core)
     loads = [
@@ -196,7 +203,8 @@
     def pool(s):
         got = dot(table[...], ct_ref[s]).astype(BF16)
         sums[s] = got
-        low[s] = got[:LOW]
+        low[s] = got[HEAD:LOW]
+        halo.append(remote(sums.at[s, pl.ds(0, HEAD)], head.at[s], head_send.at[s], head_recv.at[s], pair))
 
     pool(0)
     peak[2] = settle(1, second)
@@ -224,12 +232,13 @@
             shape(8, 128, dtype=jnp.int32),
             shape(8, 128, dtype=jnp.int32),
             shape(SIDE, N, D),
-            shape(SIDE, LOW, D),
+            shape(SIDE, LOW - HEAD, D),
+            shape(SIDE, HEAD, D),
             shape(*halo),
             shape(*halo),
         ),
         in_specs=[HB] * 5,
-        out_specs=(VM,) * 7,
+        out_specs=(VM,) * 8,
         scratch_shapes=[
             pltpu.SMEM((2,), jnp.int32),
             pltpu.SMEM((2,), jnp.int32),
@@ -248,17 +257,22 @@
             pltpu.SemaphoreType.DMA((2, SIDE)),
             pltpu.SemaphoreType.DMA((3, 3)),
             pltpu.SemaphoreType.DMA((3, 3)),
+            pltpu.SemaphoreType.DMA((SIDE,)),
+            pltpu.SemaphoreType.DMA((SIDE,)),
         ],
         compiler_params=pltpu.CompilerParams(
-            collective_id=0, has_side_effects=True, vmem_limit_bytes=28 * 2**20
+            collective_id=0, has_side_effects=True, vmem_limit_bytes=24 * 2**20
         ),
         cost_estimate=cost(4 * 2**30, 2**22),
-    )(send_next, send_prev, cluster.reshape(1, N), features.reshape(SIDE, NB, BLK, D), cotangent)
+    )(
+        in_hbm(send_next), in_hbm(send_prev), in_hbm(cluster.reshape(1, N)),
+        in_hbm(features.reshape(SIDE, NB, BLK, D)), in_hbm(cotangent),
+    )
 
 
 def node_kernel(
     rows, cols, lab_row, x_ref, prev_ref, next_ref, tiles, w_self, w_neigh,
-    agg, hidden, slope, sums, ext, acc, table,
+    agg_out, hidden_out, slope_out, sums_out, agg, hidden, slope, sums, ext, acc, table, sem,
 ):
     for s in range(SIDE):
         span = slice(s * D, (s + 1) * D)
@@ -290,34 +304,47 @@
         return carry
 
     lax.fori_loop(0, N // step, block, 0)
+    copies = [
+        local_copy(src, dst, sem.at[i])
+        for i, (src, dst) in enumerate(((agg, agg_out), (hidden, hidden_out), (slope, slope_out)))
+    ]
     for s in range(SIDE):
         sums[s] = dot(table[...], hidden[s]).astype(BF16)
+        copies.append(local_copy(sums.at[s], sums_out.at[s], sem.at[3 + s]))
+    for copy in copies:
+        copy.wait()
 
 
 def node_step(tile_row, tile_col, lab_row, features, got_prev, got_next, tiles, w_self, w_neigh):
-    full = shape(SIDE, N, D)
+    full = pltpu.HBM((SIDE, N, D), BF16)
     return pl.pallas_call(
         node_kernel,
         out_shape=(full,) * 4,
         in_specs=[SM, SM] + [VM] * 7,
-        out_specs=(VM,) * 4,
+        out_specs=(HB,) * 4,
         scratch_shapes=[
+            pltpu.VMEM((SIDE, N, D), BF16),
+            pltpu.VMEM((SIDE, N, D), BF16),
+            pltpu.VMEM((SIDE, N, D), BF16),
+            pltpu.VMEM((SIDE, N, D), BF16),
             pltpu.VMEM((NB + 4, BLK, SIDE * D), BF16),
             pltpu.VMEM((NB, BLK, SIDE * D), F32),
             pltpu.VMEM((N, N), BF16),
+            pltpu.SemaphoreType.DMA((5,)),
         ],
-        compiler_params=pltpu.CompilerParams(vmem_limit_bytes=24 * 2**20),
+        compiler_params=pltpu.CompilerParams(vmem_limit_bytes=34 * 2**20),
         cost_estimate=cost(10 * 2**30, 2**23),
     )(tile_row, tile_col, lab_row, features, got_prev, got_next, tiles, w_self, w_neigh)
 
 
-EARLY, MID, LAST = (640, 1024), (0, 384), (384, 640)
+EARLY = (640, 1024)
+CHUNKS = (((0, 384), (384, 640)), ((0, 256), (256, 512), (512, 640)))
 ORDERS = ((0, 1, 2), (1, 2, 0), (2, 0, 1))
 ENTRY = (2, 0, 1)
 
 
 def back_kernel(
-    count, lab_row, w_coarse, sums_h_in, sums_c_in, rec_c_in, far_h_in, far_c_in, x_in, agg_in,
+    count, lab_row, w_coarse, sums_h_in, sums_c_in, head_in, rec_c_in, far_h_in, far_c_in, x_in, agg_in,
     ct_in, slope_in, hidden_in,
     total, out,
     sums_h, sums_c, rec_c, far_h, far_c, x_ref, agg, ct_ref, slope, hidden, load_sem,
@@ -333,15 +360,16 @@
     wait()
     swaps, loads = [], []
     for s in range(SIDE):
-        for i, (lo, hi) in enumerate((MID, (LAST[0], LOW))):
-            rows = pl.ds(lo, hi - lo)
+        for i, (lo, hi) in enumerate(CHUNKS[s]):
+            rows = pl.ds(lo, min(hi, LOW) - lo)
             swaps.append(
                 remote(sums_h_in.at[s, rows], rec_h.at[s, rows], swap_send.at[s, i], swap_recv.at[s, i], pair)
             )
 
     for i, (src, dst) in enumerate(
         (
-            (sums_h_in, sums_h), (sums_c_in, sums_c), (far_h_in, far_h), (far_c_in, far_c), (rec_c_in, rec_c),
+            (sums_h_in, sums_h), (sums_c_in, sums_c), (far_h_in, far_h), (far_c_in, far_c),
+            (head_in, rec_c.at[:, pl.ds(0, HEAD)]), (rec_c_in, rec_c.at[:, pl.ds(HEAD, LOW - HEAD)]),
             (x_in, x_ref), (agg_in, agg), (ct_in, ct_ref), (slope_in, slope), (hidden_in, hidden),
         )
     ):
@@ -351,7 +379,7 @@
     for i in range(0, N, 128):
         flip[i : i + 128, :] = (label[i : i + 128] == across).astype(F32).astype(BF16)
     w_turn[...] = w_coarse[...].T
-    for copy in loads[:5]:
+    for copy in loads[:6]:
         copy.wait()
 
     def level(s, span):
@@ -394,16 +422,15 @@
 
     for s in range(SIDE):
         level(s, EARLY)
-    for copy in loads[5:]:
+    for copy in loads[6:]:
         copy.wait()
     for s in range(SIDE):
         x_turn[s] = x_ref[s].T
         a_turn[s] = agg[s].T
 
-    swaps[0].wait_recv()
-    level(0, MID)
-    swaps[1].wait_recv()
-    level(0, LAST)
+    for i, span in enumerate(CHUNKS[0]):
+        swaps[i].wait_recv()
+        level(0, span)
     back = dot(flip[...], down[0])
     grad_pre[...] = ((ct_ref[0].astype(F32) + 0.5 * back) * slope[0].astype(F32)).astype(BF16)
     store(0, dot(x_turn[0], grad_pre[...]))
@@ -411,12 +438,13 @@
     store(2, product(0, (0, N)) + product(1, EARLY))
     part[...] = looked(1, EARLY)
     emit(0, 0, N)
-
-    swaps[2].wait_recv()
-    level(1, MID)
-    part[...] += looked(1, MID)
-    store(2, load(2) + product(1, MID))
-    swaps[3].wait_recv()
+    for i, span in enumerate(CHUNKS[1][:-1]):
+        swaps[2 + i].wait_recv()
+        level(1, span)
+        part[...] += looked(1, span)
+        store(2, load(2) + product(1, span))
+    LAST = CHUNKS[1][-1]
+    swaps[4].wait_recv()
     level(1, LAST)
     first = [None] * 3
 
@@ -530,7 +558,7 @@
             pltpu.VMEM((SIDE, N, D), BF16),
             pltpu.VMEM((SIDE, N, D), BF16),
             pltpu.VMEM((SIDE, N, D), BF16),
-            pltpu.SemaphoreType.DMA((10,)),
+            pltpu.SemaphoreType.DMA((11,)),
             pltpu.VMEM((SIDE, LOW, D), BF16),
             pltpu.VMEM((N, N), BF16),
             pltpu.VMEM((SIDE, N, D), BF16),
@@ -551,8 +579,8 @@
             pltpu.VMEM((3, 4, 16, D), F32),
             pltpu.VMEM((3, 4, 16, D), BF16),
             pltpu.VMEM((3, 15, 16, 128), BF16),
-            pltpu.SemaphoreType.DMA((SIDE, 2)),
-            pltpu.SemaphoreType.DMA((SIDE, 2)),
+            pltpu.SemaphoreType.DMA((SIDE, 3)),
+            pltpu.SemaphoreType.DMA((SIDE, 3)),
             pltpu.SemaphoreType.DMA((2, 3, 3)),
             pltpu.SemaphoreType.DMA((2, 3, 3)),
             pltpu.SemaphoreType.DMA((2, 3, 15)),
@@ -561,10 +589,30 @@
             pltpu.SemaphoreType.DMA((2, 3)),
         ],
         compiler_params=pltpu.CompilerParams(
-            collective_id=1, has_side_effects=True, vmem_limit_bytes=56 * 2**20
+            collective_id=1, has_side_effects=True, vmem_limit_bytes=46 * 2**20
         ),
         cost_estimate=cost(12 * 2**30, 2**24),
-    )(*args)
+    )(*args[:3], *(in_hbm(arg) for arg in args[3:]))
+
+
+def close_kernel(scale, total, out_in, out, g0, g1, g2, wide, sem):
+    copies = [local_copy(out_in.at[s], out.at[s], sem.at[3 + s]) for s in range(SIDE)]
+    for p, g in enumerate((g0, g1, g2)):
+        wide[p] = total[p].astype(F32) * scale
+        copies.append(local_copy(wide.at[p], g, sem.at[p]))
+    for copy in copies:
+        copy.wait()
+
+
+def close(scale, total, out):
+    return pl.pallas_call(
+        functools.partial(close_kernel, scale),
+        out_shape=(shape(SIDE, N, D),) + (shape(D, D, dtype=F32),) * 3,
+        in_specs=[VM, VM],
+        out_specs=(HB,) * 4,
+        scratch_shapes=[pltpu.VMEM((3, D, D), F32), pltpu.SemaphoreType.DMA((5,))],
+        compiler_params=pltpu.CompilerParams(vmem_limit_bytes=8 * 2**20),
+    )(total, out)
 
 
 def local(
@@ -580,7 +628,7 @@
     neighbour_weight,
     w_coarse,
 ):
-    lab_row, count, most, sums_c, low_c, got_prev, got_next = front(
+    lab_row, count, most, sums_c, low_c, head_c, got_prev, got_next = front(
         send_next, send_prev, cluster, features, cotangent
     )
     rec_c = partner(low_c)
@@ -596,11 +644,11 @@
         sums_c,
     )
     total, output = back_step(
-        count, lab_row, w_coarse, sums_h, sums_c, rec_c, far_h, far_c, features, agg, cotangent, slope,
+        count, lab_row, w_coarse, sums_h, sums_c, head_c, rec_c, far_h, far_c, features, agg, cotangent, slope,
         hidden,
     )
     scale = 1.0 / math.sqrt(SIDE * lax.axis_size("batch") * N * lax.axis_size("dom"))
-    return (output,) + tuple(total[p].reshape(D, D).astype(F32) * scale for p in range(3))
+    return close(scale, total.reshape(3, D, D), output)
 
 
 def solution(mesh):

time: 125 us -> 112 us (0.90)
  local copies, waits for them, and re-layouts: 12.3 us -> 2.63 us
  other arithmetic: 3.31 us -> 0 us
  starting transfers between devices: 0.62 us -> 2.24 us
  waiting for transfers between devices: 1.55 us -> 0.01 us
    unnamed x35 -> x18, local copies, waits for them, and re-layouts: 9.81 us -> 0.04 us
    pallas_call x1, Pallas kernels: 64.6 us -> 59.9 us  [back_step(): pl.pallas_call(back_kernel, out_shape=(shape(3, 2, 4, 4, 16, D), shape(SI...]
    mul x1 -> x0, other arithmetic: 3.31 us -> none  [local(): total[p].reshape(D, D).astype(F32) * scale]
    pallas_call x0 -> x1, Pallas kernels: none -> 2.4 us  [close(): pl.pallas_call(functools.partial(close_kernel, scale), out_shape=(shape(S...]
    pallas_call x1, Pallas kernels: 25.4 us -> 27.2 us  [front(): pl.pallas_call(front_kernel, out_shape=(shape(1, N, dtype=jnp.int32), sha...]
    ppermute x1, starting transfers between devices: 0.62 us -> 2.24 us  [partner(): return lax.ppermute(value, 'dom', pairs)]
    ppermute x1, waiting for transfers between devices: 1.55 us -> 0.01 us  [partner(): return lax.ppermute(value, 'dom', pairs)]
  transfers between devices with their start and end apart: 1 -> 1, of which waited for: 1 -> 0; matrix products, arithmetic and copies ran while one was open for 2% -> 2% of each run, Pallas kernels for 13% -> 14%
where the time goes in v5:
time: 112 us; the launch traced here: 111 us
  Pallas kernels  105 us (94%)
  local copies, waits for them, and re-layouts  2.63 us (2%)
  starting transfers between devices  2.24 us (2%)
  between operations  1.61 us (1%)
    pallas_call x1, Pallas kernels, back_step(): pl.pallas_call(back_kernel, out_shape=(shape(3, 2, 4, 4, 16, D), shape(SI...  59.9 us
    pallas_call x1, Pallas kernels, front(): pl.pallas_call(front_kernel, out_shape=(shape(1, N, dtype=jnp.int32), sha...  27.2 us
    pallas_call x1, Pallas kernels, node_step(): pl.pallas_call(node_kernel, out_shape=(full,) * 4, in_specs=[SM, SM] + [V...  15.4 us
    pallas_call x1, Pallas kernels, close(): pl.pallas_call(functools.partial(close_kernel, scale), out_shape=(shape(S...  2.4 us
  transfers between devices with their start and end apart: 1, of which 0 were waited for; matrix products, arithmetic and copies ran while one was open for 2% of the time, Pallas kernels for 14%

profile of v5, /device:TPU:1, one launch (start us, length us, event | category | flops | bytes accessed | tf_op | source)
XLA Modules:
  0.0 111.5 jit_solution(17916429304589818725)
XLA Ops:
  0.6 0.0 copy-start
  0.6 0.0 copy-start.1
  0.7 0.0 copy-start.2
  0.7 0.0 copy-start.3
  0.7 0.0 copy-start.5
  0.7 0.0 copy-start.6
  0.7 27.2 %shard_map.138 = (s32[1,1024]{1,0:T(1,128)S(1)}, s32[8,128]{1,0:T(8,128)S(1)}, s32[8,128]{1,0:T(8,128)S(1)}, bf16[2,1024,512]{2,1,0:T(8,128)(2,1)S(1)}, bf16[2,4...) custom-call(s32[2]{0:T(128)} %nexts_in.1, ...), custom_call_target="tpu_custom_call" | custom-call | flops 4294967296 | bytes 4194304 | tf_op jit(solution)/shard_map/pallas_call | solution.py:228
  27.9 0.0 copy-start.7
  28.0 0.0 copy-start.8
  28.0 2.2 %collective-permute-start.2 = (bf16[2,416,512]{2,1,0:T(8,128)(2,1)S(1)}, bf16[2,416,512]{2,1,0:T(8,128)(2,1)}, u32[]{:S(2)}, u32[]{:S(2)}) collective-permute-start(bf16[2,416,512]{2,1,0:T(8,128)(2,1)S(1)} %get-tuple-element.33), channel_id=1, source_target_pairs={{0,2},{2,0},{4,6},{6,4},{8,10},{10,8},{12,14},{14,12},{16,18},{18,... | collective-permute-start | bytes 2555912 | tf_op jit(solution)/shard_map/ppermute | solution.py:28
  30.2 0.5 slice.9
  31.4 0.0 copy-done
  31.4 0.0 copy-done.1
  31.4 0.0 copy-done.2
  31.4 0.0 copy-done.3
  31.4 0.0 copy-done.5
  31.4 0.0 copy-done.6
  31.4 15.4 %shard_map.139 = (bf16[2,1024,512]{2,1,0:T(8,128)(2,1)}, bf16[2,1024,512]{2,1,0:T(8,128)(2,1)}, bf16[2,1024,512]{2,1,0:T(8,128)(2,1)}, bf16[2,1024,512]{2,1,0:T(8,128)(2,1)}) custom-call(s32[32]{0:T(128)S(1)} %copy-done.5, s32[32]{0:T(128)S(1)} %copy-done.6, s32[1,1024]{1,0:T(1,128)S(1)} %get-tuple-element.27.lab_row, bf16[2,1024,512]{2,1,0:T(8,128)(2,1)S(1)} %copy-done, ...), custom_call_target="tpu_custom_call" | custom-call | flops 10737418240 | bytes 8388608 | tf_op jit(solution)/shard_map/pallas_call | solution.py:320
  46.9 0.0 copy-done.7
  46.9 0.0 copy-start.4
  46.9 0.0 copy-done.8
  46.9 2.1 %conditional.1 = (bf16[2,448,512]{2,1,0:T(8,128)(2,1)}, bf16[2,448,512]{2,1,0:T(8,128)(2,1)}) conditional(s32[]{:T(128)} %bitcast.2, () %tuple.15, (bf16[2,1024,512]{2,1,0:T(8,128)(2,1)}, bf16[2,1024,512]{2,1,0:T(8,128)(2,1)S(1)}) %tuple.16), branch_computations={%region_0.0_spmd, %region_1.0_spmd} | conditional | bytes 11010144 | solution.py:639
  46.9 1.0 broadcast.2.clone
  47.9 1.1 broadcast.2
  49.0 0.0 collective-permute-done.2.rec_c_in
  49.0 0.0 copy-done.4
  49.0 59.9 %shard_map.140 = (bf16[3,2,4,4,16,512]{5,4,3,2,1,0:T(8,128)(2,1)S(1)}, bf16[2,1024,512]{2,1,0:T(8,128)(2,1)S(1)}) custom-call(s32[8,128]{1,0:T(8,128)S(1)} %get-tuple-element.26.count, s32[1,1024]{1,0:T(1,128)S(1)} %get-tuple-element.27.lab_row, bf16[512,512]{1,0:T(8,128)(2,1)S(1)} %copy-done.4, bf16[2,1024,512]{2,1,0:T(8,128)(2,1)} %get-tuple-element.30.sums_h_in, ...), custom_call_target="tpu_custom_call" | custom-call | flops 12884901888 | bytes 16777216 | tf_op jit(solution)/shard_map/pallas_call | solution.py:545
  108.9 2.4 %shard_map.141 = (bf16[2,1024,512]{2,1,0:T(8,128)(2,1)}, f32[512,512]{1,0:T(8,128)}, f32[512,512]{1,0:T(8,128)}, f32[512,512]{1,0:T(8,128)}) custom-call(bf16[3,512,512]{2,1,0:T(8,128)(2,1)S(1)} %bitcast.4, bf16[2,1024,512]{2,1,0:T(8,128)(2,1)S(1)} %get-tuple-element.41.out_in), custom_call_target="tpu_custom_call" | custom-call | tf_op jit(solution)/shard_map/pallas_call | solution.py:608
Async XLA Ops:
  0.6 30.7 %copy-start = (bf16[2,1024,512]{2,1,0:T(8,128)(2,1)S(1)}, bf16[2,1024,512]{2,1,0:T(8,128)(2,1)}, u32[]{:S(2)}) copy-start(bf16[2,1024,512]{2,1,0:T(8,128)(2,1)} %x_in.1) | copy-start | bytes 6291460
  0.6 30.7 %copy-start.1 = (bf16[32,128,128]{2,1,0:T(8,128)(2,1)S(1)}, bf16[32,128,128]{2,1,0:T(8,128)(2,1)}, u32[]{:S(2)}) copy-start(bf16[32,128,128]{2,1,0:T(8,128)(2,1)} %tiles.1) | copy-start | bytes 3145732
  0.7 30.7 %copy-start.2 = (bf16[512,512]{1,0:T(8,128)(2,1)S(1)}, bf16[512,512]{1,0:T(8,128)(2,1)}, u32[]{:S(2)}) copy-start(bf16[512,512]{1,0:T(8,128)(2,1)} %w_self.1) | copy-start | bytes 1572868
  0.7 30.7 %copy-start.3 = (bf16[512,512]{1,0:T(8,128)(2,1)S(1)}, bf16[512,512]{1,0:T(8,128)(2,1)}, u32[]{:S(2)}) copy-start(bf16[512,512]{1,0:T(8,128)(2,1)} %w_neigh.1) | copy-start | bytes 1572868
  0.7 30.7 %copy-start.5 = (s32[32]{0:T(128)S(1)}, s32[32]{0:T(128)}, u32[]{:S(2)}) copy-start(s32[32]{0:T(128)} %rows.1) | copy-start | bytes 388
  0.7 30.7 %copy-start.6 = (s32[32]{0:T(128)S(1)}, s32[32]{0:T(128)}, u32[]{:S(2)}) copy-start(s32[32]{0:T(128)} %cols.1) | copy-start | bytes 388
  27.9 18.9 %copy-start.7 = (bf16[2,160,512]{2,1,0:T(8,128)(2,1)}, bf16[2,160,512]{2,1,0:T(8,128)(2,1)S(1)}, u32[]{:S(2)}) copy-start(bf16[2,160,512]{2,1,0:T(8,128)(2,1)S(1)} %get-tuple-element.32.head_in) | copy-start | bytes 983044
  28.0 18.9 %copy-start.8 = (bf16[2,1024,512]{2,1,0:T(8,128)(2,1)}, bf16[2,1024,512]{2,1,0:T(8,128)(2,1)S(1)}, u32[]{:S(2)}) copy-start(bf16[2,1024,512]{2,1,0:T(8,128)(2,1)S(1)} %get-tuple-element.31.sums_c_in) | copy-start | bytes 6291460
  28.0 21.0 %collective-permute-start.2 = (bf16[2,416,512]{2,1,0:T(8,128)(2,1)S(1)}, bf16[2,416,512]{2,1,0:T(8,128)(2,1)}, u32[]{:S(2)}, u32[]{:S(2)}) collective-permute-start(bf16[2,416,512]{2,1,0:T(8,128)(2,1)S(1)} %get-tuple-element.33), channel_id=1, source_target_pairs={{0,2},{2,0},{4,6},{6,4},{8,10},{10,8},{12,14},{14,12},{16,18},{18,... | collective-permute-start | bytes 2555912 | tf_op jit(solution)/shard_map/ppermute | solution.py:28
  46.9 2.1 %copy-start.4 = (bf16[512,512]{1,0:T(8,128)(2,1)S(1)}, bf16[512,512]{1,0:T(8,128)(2,1)}, u32[]{:S(2)}) copy-start(bf16[512,512]{1,0:T(8,128)(2,1)} %w_coarse.1) | copy-start | bytes 1572868

commit v6 on v5

--- a/solution.py
+++ b/solution.py
@@ -14,7 +14,7 @@
 NB = 8
 SIDE = 2
 LOW = 576
-HEAD = 160
+HEAD = 176
 F32 = jnp.float32
 BF16 = jnp.bfloat16
 VM = pl.BlockSpec(memory_space=pltpu.VMEM)
@@ -286,7 +286,7 @@
         acc[r] = acc[r] + dot(tiles[t], ext[cols[t]])
         return carry
 
-    lax.fori_loop(0, tiles.shape[0], tile, 0)
+    lax.fori_loop(0, tiles.shape[0], tile, 0, unroll=8)
     step = 256
 
     def block(i, carry):
@@ -338,9 +338,11 @@
 
 
 EARLY = (640, 1024)
-CHUNKS = (((0, 384), (384, 640)), ((0, 256), (256, 512), (512, 640)))
+CHUNKS = (((0, 384), (384, 640)), ((0, 256), (256, 384), (384, 640)))
 ORDERS = ((0, 1, 2), (1, 2, 0), (2, 0, 1))
+LATE = CHUNKS[1][-1][1] - CHUNKS[1][-1][0]
 ENTRY = (2, 0, 1)
+FARTHEST = sorted(range(1, 16), key=lambda k: -min(k // 4, 4 - k // 4) - min(k % 4, 4 - k % 4))
 
 
 def back_kernel(
@@ -348,7 +350,7 @@
     ct_in, slope_in, hidden_in,
     total, out,
     sums_h, sums_c, rec_c, far_h, far_c, x_ref, agg, ct_ref, slope, hidden, load_sem,
-    rec_h, flip, lifted, down, coarse, weighed, x_turn, a_turn, w_turn, grad_pre, part, grads,
+    rec_h, flip, lifted, down, coarse, weighed, x_turn, a_turn, w_turn, grad_pre, part0, part, x_last, a_last, slope_last, grads,
     send0, recv0, acc, buf1, recv1, sum2, buf2, recv2,
     swap_send, swap_recv, send_sem, recv_sem, plane_send, plane_recv, side_send, side_recv,
 ):
@@ -382,11 +384,13 @@
     for copy in loads[:6]:
         copy.wait()
 
-    def level(s, span):
+    def level(s, span, came=True):
         lo, hi = span
         shared = lax.broadcasted_iota(jnp.int32, (hi - lo, 1), 0) + lo < count[0:1, 0:1]
 
         def joined(own, rec, far):
+            if not came:
+                return own[s, lo:hi].astype(F32)
             if lo >= LOW:
                 got = far[s, lo - LOW : hi - LOW]
             elif hi <= LOW:
@@ -400,7 +404,10 @@
         value, grad = silu_pair(dot(rows, w_coarse[...]))
         lifted[s, lo:hi] = value.astype(BF16)
         grad_act = (joined(sums_c, rec_c, far_c) * grad).astype(BF16)
-        down[s, lo:hi] = dot(grad_act, w_turn[...]).astype(BF16)
+        below = dot(grad_act, w_turn[...])
+        if not came:
+            below = jnp.where(shared, 0.0, below)
+        down[s, lo:hi] = below.astype(BF16)
         weighed[s, lo:hi] = (grad_act.astype(F32) * jnp.where(shared, 0.5, 1.0)).astype(BF16)
 
     def looked(s, span):
@@ -428,22 +435,33 @@
         x_turn[s] = x_ref[s].T
         a_turn[s] = agg[s].T
 
+    part0[...] = looked(0, EARLY)
+    part[...] = looked(1, EARLY)
+    store(2, product(0, EARLY) + product(1, EARLY))
+    LAST = CHUNKS[1][-1]
+    level(1, LAST, False)
+    part[...] += looked(1, LAST)
+    late = flip[:, LAST[0] : LAST[1]]
+    x_last[...] = dot(x_turn[1], late).astype(BF16)
+    a_last[...] = dot(a_turn[1], late).astype(BF16)
+    slope_last[...] = dot_tn(late, slope[1]).astype(BF16)
+
     for i, span in enumerate(CHUNKS[0]):
         swaps[i].wait_recv()
         level(0, span)
-    back = dot(flip[...], down[0])
-    grad_pre[...] = ((ct_ref[0].astype(F32) + 0.5 * back) * slope[0].astype(F32)).astype(BF16)
+        part0[...] += looked(0, span)
+        store(2, load(2) + product(0, span))
+    grad_pre[...] = ((ct_ref[0].astype(F32) + 0.5 * part0[...]) * slope[0].astype(F32)).astype(BF16)
     store(0, dot(x_turn[0], grad_pre[...]))
     store(1, dot(a_turn[0], grad_pre[...]))
-    store(2, product(0, (0, N)) + product(1, EARLY))
-    part[...] = looked(1, EARLY)
-    emit(0, 0, N)
     for i, span in enumerate(CHUNKS[1][:-1]):
         swaps[2 + i].wait_recv()
         level(1, span)
         part[...] += looked(1, span)
         store(2, load(2) + product(1, span))
-    LAST = CHUNKS[1][-1]
+    grad_pre[...] = ((ct_ref[1].astype(F32) + 0.5 * part[...]) * slope[1].astype(F32)).astype(BF16)
+    store(0, load(0) + dot(x_turn[1], grad_pre[...]))
+    store(1, load(1) + dot(a_turn[1], grad_pre[...]))
     swaps[4].wait_recv()
     level(1, LAST)
     first = [None] * 3
@@ -454,11 +472,12 @@
 
     store(2, load(2) + product(1, LAST))
     hand(2)
-    back = part[...] + looked(1, LAST)
-    grad_pre[...] = ((ct_ref[1].astype(F32) + 0.5 * back) * slope[1].astype(F32)).astype(BF16)
-    store(0, load(0) + dot(x_turn[1], grad_pre[...]))
+    split = lax.broadcasted_iota(jnp.int32, (LAST[1] - LAST[0], 1), 0) + LAST[0] < count[0:1, 0:1]
+    below = jnp.where(split, 0.5 * down[1, LAST[0] : LAST[1]].astype(F32), 0.0)
+    grad_last = (below * slope_last[...].astype(F32)).astype(BF16)
+    store(0, load(0) + dot(x_last[...], grad_last))
     hand(0)
-    store(1, load(1) + dot(a_turn[1], grad_pre[...]))
+    store(1, load(1) + dot(a_last[...], grad_last))
     hand(1)
 
     def mine(p):
@@ -479,12 +498,12 @@
         acc[p] = value
         buf1[p] = value.astype(BF16)
         stages[0][p] = []
-        for k in (1, 2, 3):
+        for k in (2, 1, 3):
             device, spot = here.peer(ORDERS[p][0], k)
             stages[0][p].append(
                 remote(buf1.at[p, spot], recv1.at[p, k - 1], send_sem.at[0, p, k - 1], recv_sem.at[0, p, k - 1], device)
             )
-    emit(1, 0, 512)
+    emit(0, 0, N)
     for p in ENTRY:
         arrived(0, p)
         value = acc[p, mine(p)[0]]
@@ -494,7 +513,7 @@
         buf2[p] = value.astype(BF16)
     for p in ENTRY:
         stages[1][p] = []
-        for k in range(1, 16):
+        for k in FARTHEST:
             device, spot, spot2 = here.across(ORDERS[p][1], ORDERS[p][2], k)
             stages[1][p].append(
                 remote(
@@ -502,7 +521,7 @@
                     plane_send.at[0, p, k - 1], plane_recv.at[0, p, k - 1], device,
                 )
             )
-    emit(1, 512, 1024)
+    emit(1, 0, 512)
     for p in ENTRY:
         arrived(1, p)
         one, two, three = mine(p)
@@ -512,16 +531,17 @@
         piece = total.at[p, core, one, two, :, cols(three)]
         piece[...] = value.astype(BF16)
         stages[2][p] = []
-        for k in range(1, 16):
+        for k in FARTHEST:
             device, _, _ = here.across(ORDERS[p][1], ORDERS[p][2], k)
             stages[2][p].append(
                 remote(piece, piece, plane_send.at[1, p, k - 1], plane_recv.at[1, p, k - 1], device)
             )
+    emit(1, 512, N)
     for p in ENTRY:
         arrived(2, p)
         piece = total.at[p, core, mine(p)[0]]
         stages[3][p] = []
-        for k in (1, 2, 3):
+        for k in (2, 1, 3):
             device, _ = here.peer(ORDERS[p][0], k)
             stages[3][p].append(
                 remote(piece, piece, send_sem.at[1, p, k - 1], recv_sem.at[1, p, k - 1], device)
@@ -570,6 +590,10 @@
             pltpu.VMEM((D, D), BF16),
             pltpu.VMEM((N, D), BF16),
             pltpu.VMEM((N, D), F32),
+            pltpu.VMEM((N, D), F32),
+            pltpu.VMEM((D, LATE), BF16),
+            pltpu.VMEM((D, LATE), BF16),
+            pltpu.VMEM((LATE, D), BF16),
             pltpu.VMEM((3, 2, 4, 4, 16, D), F32),
             pltpu.VMEM(half, BF16),
             pltpu.VMEM(half, BF16),
@@ -589,7 +613,7 @@
             pltpu.SemaphoreType.DMA((2, 3)),
         ],
         compiler_params=pltpu.CompilerParams(
-            collective_id=1, has_side_effects=True, vmem_limit_bytes=46 * 2**20
+            collective_id=1, has_side_effects=True, vmem_limit_bytes=48 * 2**20
         ),
         cost_estimate=cost(12 * 2**30, 2**24),
     )(*args[:3], *(in_hbm(arg) for arg in args[3:]))

time: 112 us -> 109 us (0.973)
  Pallas kernels: 105 us -> 101 us
  waiting for transfers between devices: 0.01 us -> 1.64 us
    pallas_call x1, Pallas kernels: 15.4 us -> 11.3 us  [node_step(): pl.pallas_call(node_kernel, out_shape=(full,) * 4, in_specs=[SM, SM] + [V...]
    ppermute x1, waiting for transfers between devices: 0.01 us -> 1.64 us  [partner(): return lax.ppermute(value, 'dom', pairs)]
  transfers between devices with their start and end apart: 1 -> 1, of which waited for: 0 -> 1; matrix products, arithmetic and copies ran while one was open for 2% -> 2% of each run, Pallas kernels for 14% -> 10%
where the time goes in v6:
time: 109 us
  Pallas kernels  101 us (93%)
  local copies, waits for them, and re-layouts  2.63 us (2%)
  starting transfers between devices  2.24 us (2%)
  waiting for transfers between devices  1.64 us (2%)
  between operations  1.63 us (1%)
    pallas_call x1, Pallas kernels, back_step(): pl.pallas_call(back_kernel, out_shape=(shape(3, 2, 4, 4, 16, D), shape(SI...  59.5 us
    pallas_call x1, Pallas kernels, front(): pl.pallas_call(front_kernel, out_shape=(shape(1, N, dtype=jnp.int32), sha...  27.9 us
    pallas_call x1, Pallas kernels, node_step(): pl.pallas_call(node_kernel, out_shape=(full,) * 4, in_specs=[SM, SM] + [V...  11.3 us
    pallas_call x1, Pallas kernels, close(): pl.pallas_call(functools.partial(close_kernel, scale), out_shape=(shape(S...  2.4 us
    ppermute x1, starting transfers between devices, partner(): return lax.ppermute(value, 'dom', pairs)  2.24 us
  transfers between devices with their start and end apart: 1, of which 1 were waited for; matrix products, arithmetic and copies ran while one was open for 2% of the time, Pallas kernels for 10%

profile of v6, /device:TPU:1, one launch (start us, length us, event | category | flops | bytes accessed | tf_op | source)
XLA Modules:
  0.0 109.2 jit_solution(3615257591524681842)
XLA Ops:
  0.6 0.0 copy-start
  0.6 0.0 copy-start.1
  0.7 0.0 copy-start.2
  0.7 0.0 copy-start.3
  0.7 0.0 copy-start.5
  0.7 0.0 copy-start.6
  0.7 27.9 %shard_map.138 = (s32[1,1024]{1,0:T(1,128)S(1)}, s32[8,128]{1,0:T(8,128)S(1)}, s32[8,128]{1,0:T(8,128)S(1)}, bf16[2,1024,512]{2,1,0:T(8,128)(2,1)S(1)}, bf16[2,4...) custom-call(s32[2]{0:T(128)} %nexts_in.1, ...), custom_call_target="tpu_custom_call" | custom-call | flops 4294967296 | bytes 4194304 | tf_op jit(solution)/shard_map/pallas_call | solution.py:228
  28.7 0.0 copy-start.7
  28.7 0.0 copy-start.8
  28.7 2.2 %collective-permute-start.2 = (bf16[2,400,512]{2,1,0:T(8,128)(2,1)S(1)}, bf16[2,400,512]{2,1,0:T(8,128)(2,1)}, u32[]{:S(2)}, u32[]{:S(2)}) collective-permute-start(bf16[2,400,512]{2,1,0:T(8,128)(2,1)S(1)} %get-tuple-element.33), channel_id=1, source_target_pairs={{0,2},{2,0},{4,6},{6,4},{8,10},{10,8},{12,14},{14,12},{16,18},{18,... | collective-permute-start | bytes 2457608 | tf_op jit(solution)/shard_map/ppermute | solution.py:28
  30.9 0.5 slice.9
  32.1 0.0 copy-done
  32.1 0.0 copy-done.1
  32.1 0.0 copy-done.2
  32.1 0.0 copy-done.3
  32.1 0.0 copy-done.5
  32.1 0.0 copy-done.6
  32.1 11.3 %shard_map.139 = (bf16[2,1024,512]{2,1,0:T(8,128)(2,1)}, bf16[2,1024,512]{2,1,0:T(8,128)(2,1)}, bf16[2,1024,512]{2,1,0:T(8,128)(2,1)}, bf16[2,1024,512]{2,1,0:T(8,128)(2,1)}) custom-call(s32[32]{0:T(128)S(1)} %copy-done.5, s32[32]{0:T(128)S(1)} %copy-done.6, s32[1,1024]{1,0:T(1,128)S(1)} %get-tuple-element.27.lab_row, bf16[2,1024,512]{2,1,0:T(8,128)(2,1)S(1)} %copy-done, ...), custom_call_target="tpu_custom_call" | custom-call | flops 10737418240 | bytes 8388608 | tf_op jit(solution)/shard_map/pallas_call | solution.py:320
  43.4 0.0 copy-done.7
  43.4 0.0 copy-start.4
  43.4 0.0 copy-done.8
  43.4 2.1 %conditional.1 = (bf16[2,448,512]{2,1,0:T(8,128)(2,1)}, bf16[2,448,512]{2,1,0:T(8,128)(2,1)}) conditional(s32[]{:T(128)} %bitcast.2, () %tuple.15, (bf16[2,1024,512]{2,1,0:T(8,128)(2,1)}, bf16[2,1024,512]{2,1,0:T(8,128)(2,1)S(1)}) %tuple.16), branch_computations={%region_0.0_spmd, %region_1.0_spmd} | conditional | bytes 11010144 | solution.py:663
  43.4 1.0 broadcast.2.clone
  44.4 1.1 broadcast.2
  45.5 1.6 %collective-permute-done.2.rec_c_in = bf16[2,400,512]{2,1,0:T(8,128)(2,1)} collective-permute-done((bf16[2,400,512]{2,1,0:T(8,128)(2,1)S(1)}, bf16[2,400,512]{2,1,0:T(8,128)(2,1)}, u32[]{:S(2)}, u32[]{:S(2)}) %collective-permute-start.2) | collective-permute-done | bytes 819232 | tf_op jit(solution)/shard_map/ppermute | solution.py:28
  47.2 0.0 copy-done.4
  47.2 59.5 %shard_map.140 = (bf16[3,2,4,4,16,512]{5,4,3,2,1,0:T(8,128)(2,1)S(1)}, bf16[2,1024,512]{2,1,0:T(8,128)(2,1)S(1)}) custom-call(s32[8,128]{1,0:T(8,128)S(1)} %get-tuple-element.26.count, s32[1,1024]{1,0:T(1,128)S(1)} %get-tuple-element.27.lab_row, bf16[512,512]{1,0:T(8,128)(2,1)S(1)} %copy-done.4, bf16[2,1024,512]{2,1,0:T(8,128)(2,1)} %get-tuple-element.30.sums_h_in, ...), custom_call_target="tpu_custom_call" | custom-call | flops 12884901888 | bytes 16777216 | tf_op jit(solution)/shard_map/pallas_call | solution.py:565
  106.6 2.4 %shard_map.141 = (bf16[2,1024,512]{2,1,0:T(8,128)(2,1)}, f32[512,512]{1,0:T(8,128)}, f32[512,512]{1,0:T(8,128)}, f32[512,512]{1,0:T(8,128)}) custom-call(bf16[3,512,512]{2,1,0:T(8,128)(2,1)S(1)} %bitcast.4, bf16[2,1024,512]{2,1,0:T(8,128)(2,1)S(1)} %get-tuple-element.41.out_in), custom_call_target="tpu_custom_call" | custom-call | tf_op jit(solution)/shard_map/pallas_call | solution.py:632
Async XLA Ops:
  0.6 31.4 %copy-start = (bf16[2,1024,512]{2,1,0:T(8,128)(2,1)S(1)}, bf16[2,1024,512]{2,1,0:T(8,128)(2,1)}, u32[]{:S(2)}) copy-start(bf16[2,1024,512]{2,1,0:T(8,128)(2,1)} %x_in.1) | copy-start | bytes 6291460
  0.6 31.4 %copy-start.1 = (bf16[32,128,128]{2,1,0:T(8,128)(2,1)S(1)}, bf16[32,128,128]{2,1,0:T(8,128)(2,1)}, u32[]{:S(2)}) copy-start(bf16[32,128,128]{2,1,0:T(8,128)(2,1)} %tiles.1) | copy-start | bytes 3145732
  0.7 31.4 %copy-start.2 = (bf16[512,512]{1,0:T(8,128)(2,1)S(1)}, bf16[512,512]{1,0:T(8,128)(2,1)}, u32[]{:S(2)}) copy-start(bf16[512,512]{1,0:T(8,128)(2,1)} %w_self.1) | copy-start | bytes 1572868
  0.7 31.4 %copy-start.3 = (bf16[512,512]{1,0:T(8,128)(2,1)S(1)}, bf16[512,512]{1,0:T(8,128)(2,1)}, u32[]{:S(2)}) copy-start(bf16[512,512]{1,0:T(8,128)(2,1)} %w_neigh.1) | copy-start | bytes 1572868
  0.7 31.4 %copy-start.5 = (s32[32]{0:T(128)S(1)}, s32[32]{0:T(128)}, u32[]{:S(2)}) copy-start(s32[32]{0:T(128)} %rows.1) | copy-start | bytes 388
  0.7 31.4 %copy-start.6 = (s32[32]{0:T(128)S(1)}, s32[32]{0:T(128)}, u32[]{:S(2)}) copy-start(s32[32]{0:T(128)} %cols.1) | copy-start | bytes 388
  28.7 14.8 %copy-start.7 = (bf16[2,176,512]{2,1,0:T(8,128)(2,1)}, bf16[2,176,512]{2,1,0:T(8,128)(2,1)S(1)}, u32[]{:S(2)}) copy-start(bf16[2,176,512]{2,1,0:T(8,128)(2,1)S(1)} %get-tuple-element.32.head_in) | copy-start | bytes 1081348
  28.7 14.8 %copy-start.8 = (bf16[2,1024,512]{2,1,0:T(8,128)(2,1)}, bf16[2,1024,512]{2,1,0:T(8,128)(2,1)S(1)}, u32[]{:S(2)}) copy-start(bf16[2,1024,512]{2,1,0:T(8,128)(2,1)S(1)} %get-tuple-element.31.sums_c_in) | copy-start | bytes 6291460
  28.7 18.5 %collective-permute-start.2 = (bf16[2,400,512]{2,1,0:T(8,128)(2,1)S(1)}, bf16[2,400,512]{2,1,0:T(8,128)(2,1)}, u32[]{:S(2)}, u32[]{:S(2)}) collective-permute-start(bf16[2,400,512]{2,1,0:T(8,128)(2,1)S(1)} %get-tuple-element.33), channel_id=1, source_target_pairs={{0,2},{2,0},{4,6},{6,4},{8,10},{10,8},{12,14},{14,12},{16,18},{18,... | collective-permute-start | bytes 2457608 | tf_op jit(solution)/shard_map/ppermute | solution.py:28
  43.4 3.8 %copy-start.4 = (bf16[512,512]{1,0:T(8,128)(2,1)S(1)}, bf16[512,512]{1,0:T(8,128)(2,1)}, u32[]{:S(2)}) copy-start(bf16[512,512]{1,0:T(8,128)(2,1)} %w_coarse.1) | copy-start | bytes 1572868
